TPU v7x, 128 devices: a whole 4x4x4 slice. The times are simulated.
128 devices in a mesh: sub: 8 (over z, core), row: 4 (over x), col: 4 (over y).
Axes of the slice: x: 4, y: 4, z: 4, core: 2. Of those that a mesh axis runs over, the one named last changes fastest.
Arguments:
- front: float32 [4, 32, 128, 32, 4, 128], P(None, ('sub', 'row'), None, None, 'col'), may hold values from -2.4 to 7.5, as said below
- child_tiles: bfloat16 [16384, 128, 128], P(('sub', 'row', 'col')), may hold values from -2.390625 to 2.390625
- tile_owner: int32 [16384, 1], P(('sub', 'row', 'col')), may hold values from 0 to 127; in each aligned block of 128 rows (0 to 127, 128 to 255, ...) at most 2 rows name the same one
- tile_slot: int32 [16384], P(('sub', 'row', 'col')), may hold values from 2 to 127
Outputs:
- updated: float32 [4, 32, 128, 32, 4, 128], P(None, ('sub', 'row'), None, None, 'col')
- panel: bfloat16 [4, 32, 128, 2, 4, 128], P(None, ('sub', 'row'), None, None, 'col')
Inputs may be any that keep to these rules, and one draw needn't show every extreme that they name: The leading 1024 x 1024 block of front, made symmetric from its lower triangle, is positive definite. `tile_owner`: at most 2 of the tiles of one device go to one owner.
All inputs are finite; a program needn't handle non-finite values.
Results may differ from a plain program's by a relative error of at most 0.0038.
Values may be sent and summed in bfloat16 or wider, within the bound.
A program may use at most 128 MiB of HBM per device.

v0:
```python
import jax
import jax.numpy as jnp
from jax import lax
from jax.sharding import PartitionSpec as P

NB = 1024


def broadcast(block, axis, source):
    block = jnp.where(lax.axis_index(axis) == source, block, jnp.zeros_like(block))
    return lax.psum(block, axis)


def local(front, child_tiles, tile_owner, tile_slot):
    row_tiles, _, tile_size, col_tiles, _, _ = front.shape
    sub_count = lax.axis_size("sub")
    row_count = lax.axis_size("row")
    col_count = lax.axis_size("col")
    dev_count = sub_count * row_count * col_count
    tile_count = child_tiles.shape[0]
    capacity = max(2, 2 * tile_count // dev_count)
    panel_tiles = NB // tile_size
    per_col = panel_tiles // col_count
    height = row_tiles * tile_size
    local_front = front.reshape(row_tiles, tile_size, col_tiles, tile_size)
    owners = tile_owner[:, 0]
    matches = (owners[:, None] == jnp.arange(dev_count, dtype=jnp.int32)[None, :]).astype(jnp.int32)
    before = jnp.cumsum(matches, 0) - matches
    placed = jnp.sum(before * matches, 1)
    outgoing = (
        jnp.zeros((dev_count, capacity, tile_size, tile_size), jnp.bfloat16)
        .at[owners, placed]
        .set(child_tiles)
    )
    targets = jnp.full((dev_count, capacity), -1, jnp.int32).at[owners, placed].set(tile_slot)
    arrived, landing = (
        lax.all_to_all(outgoing, ("sub", "row", "col"), split_axis=0, concat_axis=0, tiled=True),
        lax.all_to_all(targets, ("sub", "row", "col"), split_axis=0, concat_axis=0, tiled=True),
    )
    arrived = arrived.reshape(dev_count * capacity, tile_size, tile_size)
    landing = landing.reshape(dev_count * capacity)
    selector = (
        landing[:, None] == jnp.arange(row_tiles * col_tiles, dtype=jnp.int32)[None, :]
    ).astype(jnp.bfloat16)
    selector = selector.reshape(dev_count * capacity, row_tiles, col_tiles)
    assembled = local_front + jnp.einsum(
        "kqs,kab->qasb", selector, arrived, preferred_element_type=jnp.float32
    )
    sub_index = lax.axis_index("sub")
    row_index = lax.axis_index("row")
    col_index = lax.axis_index("col")
    group_id = sub_index * row_count + row_index
    corner = assembled[0, :, :per_col, :]
    beside_all = lax.all_gather(corner, ("row", "col"), axis=0, tiled=True)
    beside_all = beside_all.reshape(row_count, col_count, tile_size, per_col, tile_size)
    beside_all = beside_all.transpose(0, 2, 3, 1, 4).reshape(row_count * tile_size, NB)
    blocks = []
    for owner_sub in range(panel_tiles // row_count):
        blocks.append(broadcast(beside_all, "sub", owner_sub))
    pivot = jnp.concatenate(blocks, 0)
    symmetric = jnp.tril(pivot) + jnp.tril(pivot, -1).T
    factor = jnp.linalg.cholesky(symmetric)
    panel_cols = assembled[:, :, :per_col, :].reshape(height, per_col, 1, tile_size)
    widened = lax.all_gather(panel_cols, "col", axis=2, tiled=True).reshape(height, NB)
    solved = jax.scipy.linalg.solve_triangular(factor, widened.T, lower=True).T.astype(jnp.bfloat16)
    leading = lax.dynamic_slice_in_dim(
        factor, jnp.minimum(group_id, panel_tiles - 1) * tile_size, tile_size, 0
    ).astype(jnp.bfloat16)
    upper = jnp.where(group_id < panel_tiles, leading, solved[:tile_size])
    panel_rows = jnp.concatenate([upper, solved[tile_size:]], 0)
    panel_out = lax.dynamic_index_in_dim(
        panel_rows.reshape(row_tiles, tile_size, per_col, col_count, tile_size),
        col_index,
        3,
        keepdims=True,
    )
    panel_out = panel_out.reshape(row_tiles, 1, tile_size, per_col, 1, tile_size)
    across = broadcast(panel_rows, "row", col_index)
    update = jnp.einsum(
        "rk,nqbk->rqnb",
        panel_rows,
        lax.all_gather(across.reshape(1, row_tiles, tile_size, NB), "sub", axis=0, tiled=True),
        preferred_element_type=jnp.float32,
    )
    update = update.reshape(row_tiles, tile_size, col_tiles, tile_size)
    row_tile = jnp.arange(row_tiles, dtype=jnp.int32) * (row_count * sub_count) + group_id
    col_tile = jnp.arange(col_tiles, dtype=jnp.int32) * col_count + col_index
    trailing_mask = (row_tile >= panel_tiles)[:, None, None, None] & (col_tile >= panel_tiles)[
        None, None, :, None
    ]
    result = jnp.where(trailing_mask, assembled - update, assembled)
    return (result.reshape(front.shape), panel_out)


def solution(mesh):
    return jax.shard_map(
        local,
        mesh=mesh,
        in_specs=(
            P(None, ("sub", "row"), None, None, "col", None),
            P(("sub", "row", "col"), None, None),
            P(("sub", "row", "col"), None),
            P(("sub", "row", "col")),
        ),
        out_specs=(
            P(None, ("sub", "row"), None, None, "col", None),
            P(None, ("sub", "row"), None, None, "col", None),
        ),
        check_vma=False,
    )
```

profile of v0, /device:TPU:1, one launch (start us, length us, event | category | flops | bytes accessed | tf_op | source)
XLA Modules:
  0.0 870.7 jit_solution(1453275617700814061)
XLA Ops:
  9.6 11.0 %scatter_fusion.1 = s32[128,2]{0,1:T(2,128)S(1)} fusion(s32[128,2]{0,1:T(2,128)S(1)} %broadcast_in_dim.35, s32[128]{0:T(128)S(1)} %fusion.70, s32[128]{0:T(128)} %param.7), kind=kCustom, calls=%fused_computation.1 | custom fusion | bytes 2560 | tf_op jit(solution)/shard_map/scatter | solution.py:35
  21.3 11.5 %all-to-all-start.1 = ((s32[128,1,2]{2,1,0:T(1,128)}), s32[128,1,2]{2,1,0:T(1,128)S(1)}, u32[]{:S(2)}, u32[]{:S(2)}) async-start(s32[128,1,2]{2,1,0:T(1,128)} %copy.65), calls=%async_computation.1 | async-start | bytes 131072 | tf_op jit(solution)/shard_map/all_to_all | solution.py:38
  32.8 5.5 broadcast_in_dim.34
  38.3 20.7 %scatter_fusion = bf16[128,2,128,128]{3,2,1,0:T(8,128)(2,1)} fusion(bf16[128,2,128,128]{3,2,1,0:T(8,128)(2,1)} %broadcast_in_dim.34, s32[128]{0:T(128)S(1)} %fusion.70, bf16[128,128,128]{2,1,0:T(8,128)(2,1)} %param.5), kind=kCustom, calls=%fused_computation | custom fusion | bytes 12583936 | tf_op jit(solution)/shard_map/scatter | solution.py:33
  59.1 10.2 %all-to-all-start = ((bf16[128,2,128,128]{3,2,1,0:T(8,128)(2,1)}), bf16[128,2,128,128]{3,2,1,0:T(8,128)(2,1)}, u32[]{:S(2)}, u32[]{:S(2)}) async-start(bf16[128,2,128,128]{3,2,1,0:T(8,128)(2,1)} %scatter_fusion), calls=%async_computation | async-start | bytes 16777216 | tf_op jit(solution)/shard_map/all_to_all | solution.py:37
  70.8 99.1 %all-to-all-done = bf16[128,2,128,128]{3,2,1,0:T(8,128)(2,1)} async-done(((bf16[128,2,128,128]{3,2,1,0:T(8,128)(2,1)}), bf16[128,2,128,128]{3,2,1,0:T(8,128)(2,1)}, u32[]{:S(2)}, u32[]{:S(2)}) %all-to-all-start) | async-done | bytes 8388640 | tf_op jit(solution)/shard_map/all_to_all | solution.py:37
  169.9 12.2 %copy.64 = bf16[128,2,128,128]{3,1,0,2:T(2,128)(2,1)S(1)} copy(bf16[128,2,128,128]{3,2,1,0:T(8,128)(2,1)} %all-to-all-done) | data formatting | bytes 16777216 | tf_op jit(solution)/shard_map/all_to_all | solution.py:37
  182.1 5.1 bitcast_add_fusion
  187.3 3.4 copy-done
  194.4 40.8 %all-gather.9.cloned.1.call-done = f32[1,2048,2,128]{3,2,0,1:T(2,128)} async-done(((f32[1,128,2,128]{3,2,0,1:T(2,128)}), f32[1,2048,2,128]{3,2,0,1:T(2,128)}) %all-gather.9.cloned.1.call-update) | async-done | bytes 2097168 | tf_op jit(solution)/shard_map/all_gather | solution.py:54
  240.6 3.1 select_n.100
  246.4 3.2 select_n.95
  249.6 18.8 %all-gather.5.cloned.1.call-done = f32[512,2,4,128]{3,0,1,2:T(8,128)} async-done(((f32[512,2,1,128]{3,0,1,2:T(8,128)}), f32[512,2,4,128]{3,0,1,2:T(8,128)}) %all-gather.5.cloned.1.call-update) | async-done | bytes 2097168 | tf_op jit(solution)/shard_map/all_gather | solution.py:64
  270.4 71.8 %all-reduce.7.cloned.1.call-done = (f32[512,1024]{1,0:T(8,128)}, f32[512,1024]{1,0:T(8,128)}) async-done(((f32[512,1024]{1,0:T(8,128)}, f32[512,1024]{1,0:T(8,128)}), (f32[512,1024]{1,0:T(8,128)}, f32[512,1024]{1,0:T(8,128)})) %all-reduce.7.cloned.1.call-update) | async-done | bytes 4194320 | tf_op jit(solution)/shard_map/psum | solution.py:11
  349.1 5.3 copy.68
  354.4 5.9 bitcast_add_fusion.2
  360.3 5.5 copy.69
  365.9 4.4 fusion.1
  372.2 11.7 %cholesky.222 = f32[128,128]{1,0:T(8,128)S(1)} custom-call(f32[128,128]{1,0:T(8,128)S(1)} %cholesky.577), custom_call_target="Cholesky" | custom-call | tf_op jit(solution)/shard_map/jit(cholesky)/cholesky | solution.py:62
  386.5 9.8 %custom-call.63 = f32[1,128,128]{1,2,0:T(8,128)S(1)} custom-call(f32[1,128,128]{2,1,0:T(8,128)S(1)} %get-tuple-element.74), custom_call_target="InvertDiagBlocksLowerTriangular" | custom-call | tf_op jit(solution)/shard_map/jit(cholesky)/cholesky | solution.py:62
  400.2 12.1 %cholesky.243 = f32[128,128]{1,0:T(8,128)S(1)} custom-call(f32[128,128]{1,0:T(8,128)S(1)} %cholesky.581), custom_call_target="Cholesky" | custom-call | tf_op jit(solution)/shard_map/jit(cholesky)/cholesky | solution.py:62
  413.0 9.8 %custom-call.64 = f32[1,128,128]{1,2,0:T(8,128)S(1)} custom-call(f32[1,128,128]{2,1,0:T(8,128)S(1)} %get-tuple-element.71), custom_call_target="InvertDiagBlocksLowerTriangular" | custom-call | tf_op jit(solution)/shard_map/jit(cholesky)/cholesky | solution.py:62
  426.1 11.7 %cholesky.466 = f32[128,128]{1,0:T(8,128)S(1)} custom-call(f32[128,128]{1,0:T(8,128)S(1)} %cholesky.586), custom_call_target="Cholesky" | custom-call | tf_op jit(solution)/shard_map/jit(cholesky)/cholesky | solution.py:62
  439.1 9.8 %custom-call.65 = f32[1,128,128]{1,2,0:T(8,128)S(1)} custom-call(f32[1,128,128]{2,1,0:T(8,128)S(1)} %get-tuple-element.68), custom_call_target="InvertDiagBlocksLowerTriangular" | custom-call | tf_op jit(solution)/shard_map/jit(cholesky)/cholesky | solution.py:62
  452.4 11.8 %cholesky.485 = f32[128,128]{1,0:T(8,128)S(1)} custom-call(f32[128,128]{1,0:T(8,128)S(1)} %cholesky.591), custom_call_target="Cholesky" | custom-call | tf_op jit(solution)/shard_map/jit(cholesky)/cholesky | solution.py:62
  465.6 9.8 %custom-call.66 = f32[1,128,128]{1,2,0:T(8,128)S(1)} custom-call(f32[1,128,128]{2,1,0:T(8,128)S(1)} %get-tuple-element.65), custom_call_target="InvertDiagBlocksLowerTriangular" | custom-call | tf_op jit(solution)/shard_map/jit(cholesky)/cholesky | solution.py:62
  478.8 11.7 %cholesky.504 = f32[128,128]{1,0:T(8,128)S(1)} custom-call(f32[128,128]{1,0:T(8,128)S(1)} %cholesky.596), custom_call_target="Cholesky" | custom-call | tf_op jit(solution)/shard_map/jit(cholesky)/cholesky | solution.py:62
  491.8 10.0 %custom-call.67 = f32[1,128,128]{1,2,0:T(8,128)S(1)} custom-call(f32[1,128,128]{2,1,0:T(8,128)S(1)} %get-tuple-element.62), custom_call_target="InvertDiagBlocksLowerTriangular" | custom-call | tf_op jit(solution)/shard_map/jit(cholesky)/cholesky | solution.py:62
  505.2 11.7 %cholesky.524 = f32[128,128]{1,0:T(8,128)S(1)} custom-call(f32[128,128]{1,0:T(8,128)S(1)} %cholesky.601), custom_call_target="Cholesky" | custom-call | tf_op jit(solution)/shard_map/jit(cholesky)/cholesky | solution.py:62
  518.1 9.8 %custom-call.68 = f32[1,128,128]{1,2,0:T(8,128)S(1)} custom-call(f32[1,128,128]{2,1,0:T(8,128)S(1)} %get-tuple-element.59), custom_call_target="InvertDiagBlocksLowerTriangular" | custom-call | tf_op jit(solution)/shard_map/jit(cholesky)/cholesky | solution.py:62
  531.0 12.1 %cholesky.544 = f32[128,128]{1,0:T(8,128)S(1)} custom-call(f32[128,128]{1,0:T(8,128)S(1)} %cholesky.606), custom_call_target="Cholesky" | custom-call | tf_op jit(solution)/shard_map/jit(cholesky)/cholesky | solution.py:62
  544.3 9.8 %custom-call.69 = f32[1,128,128]{1,2,0:T(8,128)S(1)} custom-call(f32[1,128,128]{2,1,0:T(8,128)S(1)} %get-tuple-element.56), custom_call_target="InvertDiagBlocksLowerTriangular" | custom-call | tf_op jit(solution)/shard_map/jit(cholesky)/cholesky | solution.py:62
  556.7 11.7 %cholesky.562 = f32[128,128]{1,0:T(8,128)S(1)} custom-call(f32[128,128]{1,0:T(8,128)S(1)} %convolution_subtract_fusion.13), custom_call_target="Cholesky" | custom-call | tf_op jit(solution)/shard_map/jit(cholesky)/cholesky | solution.py:62
  575.3 5.8 fusion.2
  581.1 27.9 %while.1 = (s32[]{:T(128)}, f32[1024,1024]{1,0:T(8,128)}, s32[8,2]{0,1:T(2,128)S(1)}, f32[8,128,128]{2,1,0:T(8,128)}, s32[]{:T(128)}) while((s32[]{:T(128)}, f32[1024,1024]{1,0:T(8,128)}, s32[8,2]{0,1:T(2,128)S(1)}, f32[8,128,128]{2,1,0:T(8,128)}, s32[]{:T(128)}) %tuple.68), condition=%wide.while_cond, body=%wide.while_body.sunk | while | flops 2 | bytes 132705 | solution.py:65
  581.8 2.8 bitcast_dynamic-update-slice_fusion.2
  585.3 2.8 bitcast_dynamic-update-slice_fusion.2
  592.3 2.8 bitcast_dynamic-update-slice_fusion.2
  595.7 2.8 bitcast_dynamic-update-slice_fusion.2
  602.7 2.8 bitcast_dynamic-update-slice_fusion.2
  609.0 79.6 %custom-call.70 = f32[8,128,128]{1,2,0:T(8,128)S(1)} custom-call(f32[8,128,128]{2,1,0:T(8,128)} %get-tuple-element.9), custom_call_target="InvertDiagBlocksLowerTriangular" | custom-call | tf_op jit(solution)/shard_map/jit(_solve_triangular)/triangular_solve | solution.py:65
  712.3 2.9 convolution_subtract_fusion.3
  719.9 45.9 %all-reduce.5.cloned.1.call-done = bf16[1,4,128,1024]{3,2,1,0:T(8,128)(2,1)} async-done(((bf16[1,4,128,1024]{3,2,1,0:T(8,128)(2,1)}), bf16[1,4,128,1024]{3,2,1,0:T(8,128)(2,1)}) %all-reduce.5.cloned.1.call-update) | async-done | bytes 1048592 | tf_op jit(solution)/shard_map/psum | solution.py:11
  768.5 52.0 %all-gather.7.cloned.1.call-done = bf16[8,4,128,1024]{3,2,1,0:T(8,128)(2,1)} async-done(((bf16[1,4,128,1024]{3,2,1,0:T(8,128)(2,1)}), bf16[8,4,128,1024]{3,2,1,0:T(8,128)(2,1)}) %all-gather.7.cloned.1.call-update) | async-done | bytes 8388624 | tf_op jit(solution)/shard_map/all_gather | solution.py:82
  820.5 10.4 %convolution_bitcast_fusion = f32[512,4,8,128]{0,3,1,2:T(8,128)} fusion(bf16[8,4,128,1024]{3,2,1,0:T(8,128)(2,1)} %all-gather.7.cloned.1.call-done, bf16[384,1024]{1,0:T(8,128)(2,1)S(1)} %slice.280, bf16[128,1024]{1,0:T(8,128)(2,1)S(1)} %fusion.36), kind=kOutput, calls=%fused_computation.15 | convolution fusion | flops 4297064448 | bytes 17825792 | tf_op jit(solution)/shard_map/rk,nqbk->rqnb/dot_general | solution.py:79
  830.8 10.4 %copy.80 = f32[512,4,8,128]{3,2,1,0:T(8,128)} copy(f32[512,4,8,128]{0,3,1,2:T(8,128)} %convolution_bitcast_fusion) | data formatting | bytes 16777216 | tf_op jit(solution)/shard_map/rk,nqbk->rqnb/transpose | solution.py:79
  841.3 11.7 %fusion = f32[4,1,128,32,1,128]{5,3,0,2,4,1:T(8,128)} fusion(f32[4,128,32,128]{3,2,0,1:T(8,128)} %copy-done, f32[4,128,32,128]{3,2,1,0:T(8,128)} %bitcast.154, pred[4,32]{1,0:T(4,128)(4,1)S(1)} %broadcast_and_fusion), kind=kLoop, calls=%fused_computation.5 | loop fusion | flops 4194304 | bytes 25165952 | tf_op jit(solution)/shard_map/reshape | solution.py:92
  853.0 11.0 %copy.83 = f32[4,1,128,32,1,128]{5,4,3,2,1,0:T(1,128)} copy(f32[4,1,128,32,1,128]{5,3,0,2,4,1:T(8,128)} %fusion) | data formatting | bytes 16777216
  (138 shorter events, 106.4 us)
Async XLA Ops:
  21.3 37.7 %all-to-all-start.1 = ((s32[128,1,2]{2,1,0:T(1,128)}), s32[128,1,2]{2,1,0:T(1,128)S(1)}, u32[]{:S(2)}, u32[]{:S(2)}) async-start(s32[128,1,2]{2,1,0:T(1,128)} %copy.65), calls=%async_computation.1 | async-start | bytes 131072 | tf_op jit(solution)/shard_map/all_to_all | solution.py:38
  59.1 110.8 %all-to-all-start = ((bf16[128,2,128,128]{3,2,1,0:T(8,128)(2,1)}), bf16[128,2,128,128]{3,2,1,0:T(8,128)(2,1)}, u32[]{:S(2)}, u32[]{:S(2)}) async-start(bf16[128,2,128,128]{3,2,1,0:T(8,128)(2,1)} %scatter_fusion), calls=%async_computation | async-start | bytes 16777216 | tf_op jit(solution)/shard_map/all_to_all | solution.py:37
  69.3 165.9 %all-gather.9.cloned.1.call-start = ((), (), s32[]{:S(2)}) async-start(), calls=%async_computation.5 | async-start | bytes 2228224 | tf_op jit(solution)/shard_map/all_gather | solution.py:54
  187.2 3.4 copy-start
  191.4 77.1 %all-gather.5.cloned.1.call-start = ((), (), s32[]{:S(2)}) async-start(), calls=%async_computation.2 | async-start | bytes 2621440 | tf_op jit(solution)/shard_map/all_gather | solution.py:64
  194.2 148.1 %all-reduce.7.cloned.1.call-start = ((), (), s32[]{:S(2)}) async-start(), calls=%async_computation.6 | async-start | bytes 8388608 | tf_op jit(solution)/shard_map/psum | solution.py:11
  249.5 516.3 %all-reduce.5.cloned.1.call-start = ((), (), s32[]{:S(2)}) async-start(), calls=%async_computation.3 | async-start | bytes 2097152 | tf_op jit(solution)/shard_map/psum | solution.py:11
  342.2 2.2 copy-start.3
  344.7 1.9 copy-start.1
  370.3 1.9 copy-start.2
  688.6 8.2 copy-start.4
  719.9 100.6 %all-gather.7.cloned.1.call-start = ((), (), s32[]{:S(2)}) async-start(), calls=%async_computation.4 | async-start | bytes 9437184 | tf_op jit(solution)/shard_map/all_gather | solution.py:82
Sparse Core Ops, SparseCore 0:
  191.5 43.6 all-gather.8
  236.9 31.5 all-gather.4
  270.9 71.2 all-reduce.6
  720.0 45.8 all-reduce.4
  767.4 53.0 all-gather.6
where the time goes:
time: 878 us; the launch traced here: 871 us
  waiting for transfers between devices  329 us (37%)
  other arithmetic  291 us (33%)
  local copies, waits for them, and re-layouts  144 us (16%)
  matrix products  66.1 us (8%)
  starting transfers between devices  22.1 us (3%)
  between operations  19.5 us (2%)
    another operation x30, other arithmetic, local(): factor = jnp.linalg.cholesky(symmetric)  172 us
    psum x2, waiting for transfers between devices, broadcast(): return lax.psum(block, axis)  118 us
    all_to_all x1, waiting for transfers between devices, local(): lax.all_to_all(outgoing, ('sub', 'row', 'col'), split_axis=0, concat_axis...  99.1 us
    another operation x3, other arithmetic, local(): jax.scipy.linalg.solve_triangular(factor, widened.T, lower=True)  85.4 us
    all_gather x1, waiting for transfers between devices, local(): lax.all_gather(across.reshape(1, row_tiles, tile_size, NB), 'sub', axis=0...  52 us
    all_gather x1, waiting for transfers between devices, local(): beside_all = lax.all_gather(corner, ('row', 'col'), axis=0, tiled=True)  40.8 us
    another operation x24, local copies, waits for them, and re-layouts  27.9 us
    another operation x15, matrix products, local(): jax.scipy.linalg.solve_triangular(factor, widened.T, lower=True)  27.5 us
  transfers between devices with their start and end apart: 7, of which 6 were waited for; matrix products, arithmetic and copies ran while one was open for 6% of the time, Pallas kernels for 0%

commit v1 on v0

v1 whole, which is shorter than its diff:
```python
import jax
import jax.numpy as jnp
from jax import lax
from jax.experimental import pallas as pl
from jax.experimental.pallas import tpu as pltpu
from jax.sharding import PartitionSpec as P

F32, BF = jnp.float32, jnp.bfloat16
HI = lax.Precision.HIGHEST
V = pltpu.VMEM
ANY = pl.ANY


def nt(a, b):
    return lax.dot_general(a, b, (((1,), (1,)), ((), ())), precision=HI, preferred_element_type=F32)
def nn(a, b):
    return lax.dot_general(a, b, (((1,), (0,)), ((), ())), precision=HI, preferred_element_type=F32)

def split3(x):
    h = x.astype(BF).astype(F32)
    r = x - h
    m = r.astype(BF).astype(F32)
    return h, m, r - m

def diag_factor(d_ref, u_ref, x_ref, cb_ref, r_ref):
    def body(b, carry):
        r0 = pl.multiple_of(b * 8, 8)
        block = d_ref[pl.ds(r0, 8), 0:128]
        rolled = pltpu.roll(block, (128 - r0) % 128, 1)
        for j in range(8):
            cb_ref[j] = jnp.broadcast_to(rolled[:, j:j + 1], (8, 128))
        r_ref[:, 0:128] = block
        r_ref[:, 128:256] = d_ref[pl.ds(r0, 8), 128:256]
        e = {}
        for i in range(8):
            for j in range(i + 1):
                e[i, j] = cb_ref[j, i:i + 1, :]
        rows = []
        for i in range(8):
            rows.append([r_ref[i:i + 1, 0:128], r_ref[i:i + 1, 128:256]])
        for j in range(8):
            inv = lax.rsqrt(e[j, j])
            low = {}
            for i in range(j + 1, 8):
                low[i] = e[i, j] * inv
            for h in range(2):
                rows[j][h] = rows[j][h] * inv
            for i in range(j + 1, 8):
                for m in range(j + 1, i + 1):
                    e[i, m] = e[i, m] - low[i] * low[m]
                for h in range(2):
                    rows[i][h] = rows[i][h] - low[i] * rows[j][h]
        for i in range(8):
            r_ref[i:i + 1, 0:128] = rows[i][0]
            r_ref[i:i + 1, 128:256] = rows[i][1]
        r = r_ref[...]
        u_ref[pl.ds(r0, 8), :] = r[:, 0:128]
        x_ref[pl.ds(r0, 8), :] = r[:, 128:256]
        h, m, l = split3(r)
        left = jnp.concatenate([h, h, m, h, l, m], 0)[:, 0:128].astype(BF)
        right = jnp.concatenate([h, m, h, l, h, m], 0).astype(BF)
        d_ref[...] = d_ref[...] - lax.dot_general(left, right, (((0,), (0,)), ((), ())), preferred_element_type=F32)
        return carry
    lax.fori_loop(0, 16, body, 0)

def chol_kernel(lead_ref, l_ref, hi_ref, lo_ref, s_ref, w_ref, d_ref, u_ref, x_ref, cb_ref, r_ref):
    row = lax.broadcasted_iota(jnp.int32, (128, 128), 0)
    col = lax.broadcasted_iota(jnp.int32, (128, 128), 1)
    eye = (row == col).astype(F32)
    n = 8
    for i in range(n):
        for j in range(i + 1):
            t = lead_ref[i, j]
            if i == j:
                t = jnp.where(row >= col, t, t.T)
            s_ref[i * 128:(i + 1) * 128, j * 128:(j + 1) * 128] = t
    w_ref[...] = jnp.zeros_like(w_ref)
    l_ref[...] = jnp.zeros_like(l_ref)
    for k in range(n):
        a, b = k * 128, (k + 1) * 128
        d_ref[:, 0:128] = s_ref[a:b, a:b]
        d_ref[:, 128:256] = eye
        diag_factor(d_ref, u_ref, x_ref, cb_ref, r_ref)
        x = x_ref[...]
        l_ref[a:b, a:b] = jnp.where(row >= col, u_ref[...].T, 0.0).astype(BF)
        if k > 0:
            w_ref[a:b, 0:a] = nn(x, w_ref[a:b, 0:a])
        w_ref[a:b, a:b] = x
        if k < n - 1:
            p = nt(s_ref[b:, a:b], x)
            s_ref[b:, a:b] = p
            l_ref[b:, a:b] = p.astype(BF)
            for j in range(k + 1, n):
                c, d = j * 128, (j + 1) * 128
                s_ref[c:, c:d] = s_ref[c:, c:d] - nt(s_ref[c:, a:b], s_ref[c:d, a:b])
            w_ref[b:, 0:b] = w_ref[b:, 0:b] - nn(p, w_ref[a:b, 0:b])
    for k in range(n):
        a, b = k * 128, (k + 1) * 128
        y = w_ref[a:b, :]
        h = y.astype(BF)
        hi_ref[a:b, :] = h
        lo_ref[a:b, :] = (y - h.astype(F32)).astype(BF)

def chol(lead):
    return pl.pallas_call(
        chol_kernel,
        out_shape=[jax.ShapeDtypeStruct((1024, 1024), BF)] * 3,
        in_specs=[pl.BlockSpec(memory_space=V)],
        out_specs=[pl.BlockSpec(memory_space=V)] * 3,
        scratch_shapes=[V((1024, 1024), F32), V((1024, 1024), F32), V((128, 256), F32), V((128, 128), F32),
                        V((128, 128), F32), V((8, 8, 128), F32), V((8, 256), F32)],
        compiler_params=pltpu.CompilerParams(vmem_limit_bytes=60 << 20),
        name="chol",
    )(lead)


def route_kernel(own_ref, slot_ref, child_ref, out_ref, tgt_ref, idx_ref, cnt_ref):
    step = pl.program_id(0)

    @pl.when(step == 0)
    def _():
        def clear(k, c):
            cnt_ref[k] = 0
            for u in range(2):
                idx_ref[2 * k + u] = 0
                tgt_ref[2 * k + u] = -1
            return c
        lax.fori_loop(0, 128, clear, 0)

        def place(k, c):
            o = own_ref[k]
            n = cnt_ref[o]
            idx_ref[2 * o + n] = k
            tgt_ref[2 * o + n] = slot_ref[k]
            cnt_ref[o] = n + 1
            return c
        lax.fori_loop(0, 128, place, 0)

    def copy(j, c):
        for u in range(2):
            out_ref[j, u] = child_ref[idx_ref[step * 32 + 2 * j + u]]
        return c
    lax.fori_loop(0, 16, copy, 0)


def route(owner, slot, child):
    return pl.pallas_call(
        route_kernel,
        out_shape=(jax.ShapeDtypeStruct((128, 2, 128, 128), BF), jax.ShapeDtypeStruct((256,), jnp.int32)),
        grid_spec=pltpu.PrefetchScalarGridSpec(
            num_scalar_prefetch=2, grid=(8,),
            in_specs=[pl.BlockSpec((128, 128, 128), lambda g, a, b: (0, 0, 0), pipeline_mode=pl.Buffered(1))],
            out_specs=(pl.BlockSpec((16, 2, 128, 128), lambda g, a, b: (g, 0, 0, 0)),
                       pl.BlockSpec(memory_space=pltpu.SMEM)),
            scratch_shapes=[pltpu.SMEM((256,), jnp.int32), pltpu.SMEM((128,), jnp.int32)]),
        compiler_params=pltpu.CompilerParams(vmem_limit_bytes=24 << 20),
        name="route",
    )(owner, slot, child)


def head_kernel(land_ref, front_ref, arr_ref, out_ref, buf_ref, acc_ref, fsem, asem):
    def arrive(c):
        return pltpu.make_async_copy(arr_ref.at[pl.ds(c * 32, 32)], buf_ref.at[c], asem.at[c])
    def fetch(s):
        return pltpu.make_async_copy(front_ref.at[:, 0, :, s, 0, :], acc_ref.at[s], fsem.at[s])
    for s in range(2):
        fetch(s).start()
    for c in range(8):
        arrive(c).start()
    for s in range(2):
        fetch(s).wait()
    for c in range(8):
        arrive(c).wait()
        def add(k, carry):
            slot = land_ref[c * 32 + k]
            s, q = slot % 32, slot // 32
            @pl.when((slot >= 0) & (s < 2))
            def _():
                acc_ref[s, q] = acc_ref[s, q] + buf_ref[c, k].astype(F32)
            return carry
        lax.fori_loop(0, 32, add, 0)
    out_ref[...] = acc_ref[...]


def head(land, front, arrived):
    return pl.pallas_call(
        head_kernel,
        out_shape=jax.ShapeDtypeStruct((2, 4, 128, 128), F32),
        grid_spec=pltpu.PrefetchScalarGridSpec(
            num_scalar_prefetch=1, grid=(1,),
            in_specs=[pl.BlockSpec(memory_space=ANY)] * 2,
            out_specs=pl.BlockSpec((2, 4, 128, 128), lambda g, a: (0, 0, 0, 0)),
            scratch_shapes=[V((8, 32, 128, 128), BF), V((2, 4, 128, 128), F32),
                            pltpu.SemaphoreType.DMA((2,)), pltpu.SemaphoreType.DMA((8,))]),
        compiler_params=pltpu.CompilerParams(vmem_limit_bytes=60 << 20),
        name="head",
    )(land, front, arrived)


def fin_kernel(land_ref, front_ref, arr_ref, brow_ref, bcol_ref, out_ref, buf_ref, acc_ref, bc_ref, fsem, asem, bsem, osem):
    def arrive(c):
        return pltpu.make_async_copy(arr_ref.at[pl.ds(c * 32, 32)], buf_ref.at[c], asem.at[c])
    def fetch(s):
        return pltpu.make_async_copy(front_ref.at[:, 0, :, s, 0, :], acc_ref.at[s], fsem.at[s])
    def column(s):
        return pltpu.make_async_copy(bcol_ref.at[s % 8, s // 8], bc_ref.at[pl.ds(s * 128, 128)], bsem.at[s])
    def put(s):
        return pltpu.make_async_copy(acc_ref.at[s], out_ref.at[:, 0, :, s, 0, :], osem.at[s])
    def each(low, high, f):
        def go(s, c):
            f(s)
            return c
        lax.fori_loop(low, high, go, 0)
    each(0, 32, lambda s: fetch(s).start())
    for c in range(8):
        arrive(c).start()
    each(2, 32, lambda s: column(s).start())
    each(0, 32, lambda s: fetch(s).wait())
    for c in range(8):
        arrive(c).wait()
        def add(k, carry):
            slot = land_ref[c * 32 + k]
            @pl.when(slot >= 0)
            def _():
                s, q = slot % 32, slot // 32
                acc_ref[s, q] = acc_ref[s, q] + buf_ref[c, k].astype(F32)
            return carry
        lax.fori_loop(0, 32, add, 0)
    for s in range(2):
        put(s).start()
    def update(g, carry):
        s = 2 * g
        column(s).wait()
        column(s + 1).wait()
        y = lax.dot_general(brow_ref[...], bc_ref[pl.ds(pl.multiple_of(g * 256, 256), 256), :],
                            (((1,), (1,)), ((), ())), preferred_element_type=F32)
        for u in range(2):
            acc_ref[s + u] = acc_ref[s + u] - y[:, u * 128:(u + 1) * 128].reshape(4, 128, 128)
            put(s + u).start()
        return carry
    lax.fori_loop(1, 16, update, 0)
    each(0, 32, lambda s: put(s).wait())


def fin(land, front, arrived, brow, bcol):
    D = pltpu.SemaphoreType.DMA
    return pl.pallas_call(
        fin_kernel,
        out_shape=jax.ShapeDtypeStruct((4, 1, 128, 32, 1, 128), F32),
        grid_spec=pltpu.PrefetchScalarGridSpec(
            num_scalar_prefetch=1, grid=(1,),
            in_specs=[pl.BlockSpec(memory_space=ANY)] * 2
            + [pl.BlockSpec((512, 1024), lambda g, a: (0, 0), pipeline_mode=pl.Buffered(1)), pl.BlockSpec(memory_space=ANY)],
            out_specs=pl.BlockSpec(memory_space=ANY),
            scratch_shapes=[V((8, 32, 128, 128), BF), V((32, 4, 128, 128), F32), V((4096, 1024), BF),
                            D((32,)), D((8,)), D((32,)), D((32,))]),
        compiler_params=pltpu.CompilerParams(vmem_limit_bytes=60 << 20),
        name="fin",
    )(land, front, arrived, brow, bcol)


def solve_kernel(a_ref, hi_ref, lo_ref, b_ref):
    a = a_ref[...]
    ah = a.astype(BF)
    al = (a - ah.astype(F32)).astype(BF)
    def mm(x, y):
        return lax.dot_general(x, y, (((1,), (1,)), ((), ())), preferred_element_type=F32)
    b_ref[...] = (mm(ah, hi_ref[...]) + (mm(ah, lo_ref[...]) + mm(al, hi_ref[...]))).astype(BF)


def solve(a, hi, lo):
    full = pl.BlockSpec((1024, 1024), lambda g: (0, 0), pipeline_mode=pl.Buffered(1))
    return pl.pallas_call(
        solve_kernel,
        out_shape=jax.ShapeDtypeStruct((512, 1024), BF),
        grid=(4,),
        in_specs=[pl.BlockSpec((128, 1024), lambda g: (g, 0)), full, full],
        out_specs=pl.BlockSpec((128, 1024), lambda g: (g, 0)),
        compiler_params=pltpu.CompilerParams(vmem_limit_bytes=24 << 20),
        name="solve",
    )(a, hi, lo)


def local(front, child_tiles, tile_owner, tile_slot):
    sub = lax.axis_index("sub")
    row = lax.axis_index("row")
    col = lax.axis_index("col")
    group = sub * 4 + row
    outgoing, targets = route(tile_owner[:, 0], tile_slot, child_tiles)
    landing = lax.all_to_all(targets.reshape(128, 2), ("sub", "row", "col"), split_axis=0, concat_axis=0, tiled=True).reshape(256)
    corner = front[0, 0, :, :2, 0, :].transpose(1, 0, 2)
    held = jnp.stack([jnp.where(sub == g, corner, jnp.zeros_like(corner)) for g in range(2)])
    held = lax.psum(held, "sub")
    lead = lax.all_gather(held, ("row", "col"), axis=0, tiled=False)
    lead = lead.reshape(4, 4, 2, 2, 128, 128).transpose(2, 0, 3, 1, 4, 5).reshape(8, 8, 128, 128)
    outgoing, lead = lax.optimization_barrier((outgoing, lead))
    arrived = lax.all_to_all(outgoing, ("sub", "row", "col"), split_axis=0, concat_axis=0, tiled=True)
    arrived = arrived.reshape(256, 128, 128)
    factor, hi, lo = chol(lead)
    panel = head(landing, front, arrived)
    wide = lax.all_gather(panel, "col", axis=0, tiled=False)
    wide = wide.transpose(2, 3, 1, 0, 4).reshape(512, 1024) if False else wide.transpose(2, 3, 1, 0, 4).reshape(4 * 128, 1024)
    solved = solve(wide, hi, lo)
    return solved, factor, landing, arrived, front, sub, row, col, group


def finish(front, child_tiles, tile_owner, tile_slot):
    solved, factor, landing, arrived, front, sub, row, col, group = local(front, child_tiles, tile_owner, tile_slot)
    mine = lax.dynamic_slice_in_dim(factor, jnp.minimum(group, 7) * 128, 128, 0)
    top = group < 8
    brow = solved.reshape(4, 128, 1024)
    rows = brow.at[0].set(jnp.where(top, mine, brow[0]))
    panel_out = lax.dynamic_index_in_dim(rows.reshape(4, 128, 2, 4, 128), col, 3, keepdims=True)
    panel_out = panel_out.reshape(4, 1, 128, 2, 1, 128)
    brow = brow.at[0].set(jnp.where(top, jnp.zeros_like(mine), brow[0])).reshape(512, 1024)
    across = lax.psum(jnp.where(row == col, solved, jnp.zeros_like(solved)), "row")
    bcol = lax.all_gather(across.reshape(1, 4, 128, 1024), "sub", axis=0, tiled=True)
    return fin(landing, front, arrived, brow, bcol), panel_out


def solution(mesh):
    return jax.shard_map(
        finish,
        mesh=mesh,
        in_specs=(
            P(None, ("sub", "row"), None, None, "col", None),
            P(("sub", "row", "col"), None, None),
            P(("sub", "row", "col"), None),
            P(("sub", "row", "col")),
        ),
        out_specs=(
            P(None, ("sub", "row"), None, None, "col", None),
            P(None, ("sub", "row"), None, None, "col", None),
        ),
        check_vma=False,
    )
```

time: 878 us -> 474 us (0.54)
  other arithmetic: 291 us -> 3.67 us
  Pallas kernels: 0 us -> 120 us
  local copies, waits for them, and re-layouts: 144 us -> 28.3 us
  matrix products: 66.1 us -> 0 us
  waiting for transfers between devices: 329 us -> 288 us
    another operation x34 -> x1, other arithmetic: 258 us -> 0.02 us  [local(): jnp.stack([jnp.where(sub == g, corner, jnp.zeros_like(corner)) for g in r...]
    pallas_call x0 -> x5, Pallas kernels: none -> 120 us  [the longest x1 76.8 us: chol(): pl.pallas_call(chol_kernel, out_shape=[jax.ShapeDtypeStruct((1024, 1024),...]
    another operation x29 -> x0, matrix products: 50.5 us -> none  [the longest x15 27.5 us: local(): jax.scipy.linalg.solve_triangular(factor, widened.T, lower=True)]
    scatter x2 -> x0, local copies, waits for them, and re-layouts: 31.7 us -> none  [the longest x1 20.7 us: local(): outgoing = jnp.zeros((dev_count, capacity, tile_size, tile_size), jnp.bfl...]
    another operation x40 -> x0, local copies, waits for them, and re-layouts: 31.3 us -> none
    all_gather x3, waiting for transfers between devices: 112 us -> 81.1 us  [the longest x1 49.1 us: finish(): lax.all_gather(across.reshape(1, 4, 128, 1024), 'sub', axis=0, tiled=True)]
    select_n x5 -> x0, local copies, waits for them, and re-layouts: 16.9 us -> none  [the longest x4 11.6 us: broadcast(): jnp.where(lax.axis_index(axis) == source, block, jnp.zeros_like(block))]
    dot_general x2 -> x0, matrix products: 15.5 us -> none  [the longest x1 10.4 us: local(): jnp.einsum('rk,nqbk->rqnb', panel_rows, lax.all_gather(across.reshape(1,...]
  transfers between devices with their start and end apart: 7 -> 7, of which waited for: 6 -> 5; matrix products, arithmetic and copies ran while one was open for 6% -> 3% of each run, Pallas kernels for 0% -> 17%
where the time goes in v1:
time: 474 us; the launch traced here: 472 us
  waiting for transfers between devices  288 us (61%)
  Pallas kernels  120 us (25%)
  local copies, waits for them, and re-layouts  28.3 us (6%)
  starting transfers between devices  18.1 us (4%)
  between operations  14 us (3%)
    all_to_all x1, waiting for transfers between devices, local(): lax.all_to_all(outgoing, ('sub', 'row', 'col'), split_axis=0, concat_axis...  98.5 us
    pallas_call x1, Pallas kernels, chol(): pl.pallas_call(chol_kernel, out_shape=[jax.ShapeDtypeStruct((1024, 1024),...  76.8 us
    psum x1, waiting for transfers between devices, local(): held = lax.psum(held, 'sub')  63.5 us
    all_gather x1, waiting for transfers between devices, finish(): lax.all_gather(across.reshape(1, 4, 128, 1024), 'sub', axis=0, tiled=True)  49.1 us
    psum x1, waiting for transfers between devices, finish(): lax.psum(jnp.where(row == col, solved, jnp.zeros_like(solved)), 'row')  45.1 us
    all_gather x1, waiting for transfers between devices, local(): lead = lax.all_gather(held, ('row', 'col'), axis=0, tiled=False)  32 us
    pallas_call x1, Pallas kernels, fin(): pl.pallas_call(fin_kernel, out_shape=jax.ShapeDtypeStruct((4, 1, 128, 32,...  20.1 us
    unnamed x17, local copies, waits for them, and re-layouts  11.1 us
  transfers between devices with their start and end apart: 7, of which 5 were waited for; matrix products, arithmetic and copies ran while one was open for 3% of the time, Pallas kernels for 17%

profile of v1, /device:TPU:1, one launch (start us, length us, event | category | flops | bytes accessed | tf_op | source)
XLA Modules:
  0.0 472.2 jit_solution(8013481375054911930)
XLA Ops:
  7.2 0.0 all-reduce.3.cloned.1.call-start
  7.2 0.9 slice.48
  8.2 0.7 maximum_bitcast_fusion
  8.9 0.0 all-reduce.3.cloned.1.call-update
  8.9 0.0 all-gather.5.cloned.1.call-start
  9.0 63.5 %all-reduce.3.cloned.1.call-done = f32[1,2,2,128,128]{4,3,2,1,0:T(8,128)} async-done(((f32[1,2,2,128,128]{4,3,2,1,0:T(8,128)}), f32[1,2,2,128,128]{4,3,2,1,0:T(8,128)}) %all-reduce.3.cloned.1.call-update) | async-done | bytes 262160 | tf_op jit(solution)/shard_map/psum | solution.py:293
  72.5 0.0 all-gather.5.cloned.1.call-update
  72.5 0.0 copy-start.1
  72.5 2.2 copy-done.1
  74.7 0.7 copy-done.4
  75.4 0.7 copy-done.5
  76.0 5.4 %route.1 = (bf16[128,2,128,128]{3,2,1,0:T(8,128)(2,1)S(1)}, s32[256]{0:T(256)S(1)}) custom-call(s32[128]{0:T(128)S(1)} %bitcast.37, s32[128]{0:T(128)S(1)} %copy-done.5, bf16[128,128,128]{2,1,0:T(8,128)(2,1)S(1)} %copy-done.1), custom_call_target="tpu_custom_call" | custom-call | tf_op jit(solution)/shard_map/route/pallas_call | solution.py:147
  81.5 0.0 copy-start
  81.5 3.4 copy-done
  84.9 0.8 all_to_all.9
  85.6 9.3 %all-to-all-start = ((s32[128,1,2]{2,1,0:T(1,128)}), s32[128,1,2]{2,1,0:T(1,128)S(1)}, u32[]{:S(2)}, u32[]{:S(2)}) async-start(s32[128,1,2]{2,1,0:T(1,128)} %bitcast.1), calls=%async_computation | async-start | bytes 131072 | tf_op jit(solution)/shard_map/all_to_all | solution.py:290
  95.0 32.0 %all-gather.5.cloned.1.call-done = f32[16,2,2,128,128]{4,3,2,1,0:T(8,128)} async-done(((f32[1,2,2,128,128]{4,3,2,1,0:T(8,128)}), f32[16,2,2,128,128]{4,3,2,1,0:T(8,128)}) %all-gather.5.cloned.1.call-update) | async-done | bytes 4194320 | tf_op jit(solution)/shard_map/all_gather | solution.py:294
  127.0 4.7 copy.18
  131.6 0.0 all-to-all-done
  131.6 8.6 %all-to-all-start.1 = ((bf16[128,2,128,128]{3,2,1,0:T(8,128)(2,1)}), bf16[128,2,128,128]{3,2,1,0:T(8,128)(2,1)}, u32[]{:S(2)}, u32[]{:S(2)}) async-start(bf16[128,2,128,128]{3,2,1,0:T(8,128)(2,1)} %copy-done), calls=%async_computation.1 | async-start | bytes 16777216 | tf_op jit(solution)/shard_map/all_to_all | solution.py:297
  140.3 0.0 all-gather.9.cloned.1.call-start
  140.3 0.5 broadcast.60
  140.8 0.8 reduce.7
  141.6 0.7 reshape.110.land_ref
  142.3 98.5 %all-to-all-done.1 = bf16[128,2,128,128]{3,2,1,0:T(8,128)(2,1)} async-done(((bf16[128,2,128,128]{3,2,1,0:T(8,128)(2,1)}), bf16[128,2,128,128]{3,2,1,0:T(8,128)(2,1)}, u32[]{:S(2)}, u32[]{:S(2)}) %all-to-all-start.1) | async-done | bytes 8388640 | tf_op jit(solution)/shard_map/all_to_all | solution.py:297
  240.8 8.9 %head.1 = f32[2,4,128,128]{3,2,1,0:T(8,128)} custom-call(s32[256]{0:T(256)} %reshape.110.land_ref, f32[4,1,128,32,1,128]{5,4,3,2,1,0:T(1,128)} %front_ref.3, bf16[256,128,128]{2,1,0:T(8,128)(2,1)} %bitcast.12.arr_ref), custom_call_target="tpu_custom_call" | custom-call | tf_op jit(solution)/shard_map/head/pallas_call | solution.py:186
  249.7 0.0 all-gather.9.cloned.1.call-update
  249.7 0.0 all-reduce.5.cloned.1.call-start
  249.8 76.8 %chol.1 = (bf16[1024,1024]{1,0:T(8,128)(2,1)}, bf16[1024,1024]{1,0:T(8,128)(2,1)}, bf16[1024,1024]{1,0:T(8,128)(2,1)}) custom-call(f32[8,8,128,128]{3,2,1,0:T(8,128)} %bitcast.38), custom_call_target="tpu_custom_call" | custom-call | tf_op jit(solution)/shard_map/chol/pallas_call | solution.py:105
  326.6 4.3 copy.27
  330.8 2.1 reshape.114.a_ref
  332.9 0.0 copy-start.2
  332.9 1.6 copy-done.2
  334.5 1.6 copy-done.3
  336.1 8.7 %solve.1 = bf16[512,1024]{1,0:T(8,128)(2,1)S(1)} custom-call(f32[512,1024]{1,0:T(8,128)S(1)} %reshape.114.a_ref, bf16[1024,1024]{1,0:T(8,128)(2,1)S(1)} %copy-done.2, bf16[1024,1024]{1,0:T(8,128)(2,1)S(1)} %copy-done.3), custom_call_target="tpu_custom_call" | custom-call | tf_op jit(solution)/shard_map/solve/pallas_call | solution.py:273
  344.8 1.0 broadcast_select_fusion
  345.8 0.0 all-reduce.5.cloned.1.call-update
  345.9 0.0 all-gather.7.cloned.1.call-start
  345.9 45.1 %all-reduce.5.cloned.1.call-done = bf16[1,4,128,1024]{3,2,1,0:T(8,128)(2,1)} async-done(((bf16[1,4,128,1024]{3,2,1,0:T(8,128)(2,1)}), bf16[1,4,128,1024]{3,2,1,0:T(8,128)(2,1)}) %all-reduce.5.cloned.1.call-update) | async-done | bytes 1048592 | tf_op jit(solution)/shard_map/psum | solution.py:316
  391.0 0.0 all-gather.7.cloned.1.call-update
  391.0 0.1 copy.32
  391.1 0.1 copy.30
  391.2 1.0 bitcast_dynamic-update-slice_fusion
  392.2 1.5 reshape.120
  393.7 1.8 constant_dynamic-slice_fusion
  395.5 0.9 copy.28
  396.5 49.1 %all-gather.7.cloned.1.call-done.bcol_ref = bf16[8,4,128,1024]{3,2,1,0:T(8,128)(2,1)} async-done(((bf16[1,4,128,1024]{3,2,1,0:T(8,128)(2,1)}), bf16[8,4,128,1024]{3,2,1,0:T(8,128)(2,1)}) %all-gather.7.cloned.1.call-update) | async-done | bytes 8388624 | tf_op jit(solution)/shard_map/all_gather | solution.py:317
  445.6 20.1 %fin.1 = f32[4,1,128,32,1,128]{5,4,3,2,1,0:T(1,128)} custom-call(s32[256]{0:T(256)} %reshape.110.land_ref, f32[4,1,128,32,1,128]{5,4,3,2,1,0:T(1,128)} %front_ref.3, bf16[256,128,128]{2,1,0:T(8,128)(2,1)} %bitcast.12.arr_ref, bf16[512,1024]{1,0:T(8,128)(2,1)} %bitcast.40, bf16[8,4,128,1024]{3,2,1,0:T(8,128)(2,1)} %all-gather.7.cloned.1.call-done.bcol_ref), custom_call_target="tpu_custom_call" | custom-call | tf_op jit(solution)/shard_map/fin/pallas_call | solution.py:247
  (8 shorter events, 0.1 us)
Async XLA Ops:
  7.2 65.3 %all-reduce.3.cloned.1.call-start = ((), (), s32[]{:S(2)}) async-start(), calls=%async_computation.2 | async-start | bytes 524288 | tf_op jit(solution)/shard_map/psum | solution.py:293
  8.9 118.0 %all-gather.5.cloned.1.call-start = ((), (), s32[]{:S(2)}) async-start(), calls=%async_computation.3 | async-start | bytes 4456448 | tf_op jit(solution)/shard_map/all_gather | solution.py:294
  72.5 2.2 copy-start.1
  74.7 0.7 copy-start.4
  75.4 0.7 copy-start.5
  81.5 3.4 copy-start
  85.6 46.0 %all-to-all-start = ((s32[128,1,2]{2,1,0:T(1,128)}), s32[128,1,2]{2,1,0:T(1,128)S(1)}, u32[]{:S(2)}, u32[]{:S(2)}) async-start(s32[128,1,2]{2,1,0:T(1,128)} %bitcast.1), calls=%async_computation | async-start | bytes 131072 | tf_op jit(solution)/shard_map/all_to_all | solution.py:290
  131.6 109.2 %all-to-all-start.1 = ((bf16[128,2,128,128]{3,2,1,0:T(8,128)(2,1)}), bf16[128,2,128,128]{3,2,1,0:T(8,128)(2,1)}, u32[]{:S(2)}, u32[]{:S(2)}) async-start(bf16[128,2,128,128]{3,2,1,0:T(8,128)(2,1)} %copy-done), calls=%async_computation.1 | async-start | bytes 16777216 | tf_op jit(solution)/shard_map/all_to_all | solution.py:297
  140.3 186.3 %all-gather.9.cloned.1.call-start = ((), (), s32[]{:S(2)}) async-start(), calls=%async_computation.6 | async-start | bytes 2621440 | tf_op jit(solution)/shard_map/all_gather | solution.py:301
  249.7 141.2 %all-reduce.5.cloned.1.call-start = ((), (), s32[]{:S(2)}) async-start(), calls=%async_computation.4 | async-start | bytes 2097152 | tf_op jit(solution)/shard_map/psum | solution.py:316
  332.9 1.6 copy-start.2
  334.5 1.6 copy-start.3
  345.9 99.7 %all-gather.7.cloned.1.call-start = ((), (), s32[]{:S(2)}) async-start(), calls=%async_computation.5 | async-start | bytes 9437184 | tf_op jit(solution)/shard_map/all_gather | solution.py:317
  396.4 49.2 %copy-start.6 = (bf16[4,128,1024]{2,1,0:T(8,128)(2,1)}, bf16[4,128,1024]{2,1,0:T(8,128)(2,1)S(1)}, u32[]{:S(2)}) copy-start(bf16[4,128,1024]{2,1,0:T(8,128)(2,1)S(1)} %bitcast_dynamic-update-slice_fusion.1) | copy-start | bytes 3145732
Sparse Core Ops, SparseCore 0:
  10.9 61.5 all-reduce.2
  74.6 52.2 all-gather.4
  249.9 31.3 all-gather.8
  346.0 44.9 all-reduce.4
  392.5 53.0 all-gather.6

commit v2 on v1

--- a/solution.py
+++ b/solution.py
@@ -9,18 +9,23 @@
 HI = lax.Precision.HIGHEST
 V = pltpu.VMEM
 ANY = pl.ANY
+MESH = pl.DeviceIdType.MESH
 
 
 def nt(a, b):
     return lax.dot_general(a, b, (((1,), (1,)), ((), ())), precision=HI, preferred_element_type=F32)
+
+
 def nn(a, b):
     return lax.dot_general(a, b, (((1,), (0,)), ((), ())), precision=HI, preferred_element_type=F32)
+
 
 def split3(x):
     h = x.astype(BF).astype(F32)
     r = x - h
     m = r.astype(BF).astype(F32)
     return h, m, r - m
+
 
 def diag_factor(d_ref, u_ref, x_ref, cb_ref, r_ref):
     def body(b, carry):
@@ -63,6 +68,7 @@
         return carry
     lax.fori_loop(0, 16, body, 0)
 
+
 def chol_kernel(lead_ref, l_ref, hi_ref, lo_ref, s_ref, w_ref, d_ref, u_ref, x_ref, cb_ref, r_ref):
     row = lax.broadcasted_iota(jnp.int32, (128, 128), 0)
     col = lax.broadcasted_iota(jnp.int32, (128, 128), 1)
@@ -101,6 +107,7 @@
         hi_ref[a:b, :] = h
         lo_ref[a:b, :] = (y - h.astype(F32)).astype(BF)
 
+
 def chol(lead):
     return pl.pallas_call(
         chol_kernel,
@@ -109,12 +116,12 @@
         out_specs=[pl.BlockSpec(memory_space=V)] * 3,
         scratch_shapes=[V((1024, 1024), F32), V((1024, 1024), F32), V((128, 256), F32), V((128, 128), F32),
                         V((128, 128), F32), V((8, 8, 128), F32), V((8, 256), F32)],
-        compiler_params=pltpu.CompilerParams(vmem_limit_bytes=60 << 20),
+        compiler_params=pltpu.CompilerParams(vmem_limit_bytes=30 << 20),
         name="chol",
     )(lead)
 
 
-def route_kernel(own_ref, slot_ref, child_ref, out_ref, tgt_ref, idx_ref, cnt_ref):
+def route_kernel(own_ref, child_ref, out_ref, idx_ref, cnt_ref):
     step = pl.program_id(0)
 
     @pl.when(step == 0)
@@ -123,7 +130,6 @@
             cnt_ref[k] = 0
             for u in range(2):
                 idx_ref[2 * k + u] = 0
-                tgt_ref[2 * k + u] = -1
             return c
         lax.fori_loop(0, 128, clear, 0)
 
@@ -131,7 +137,6 @@
             o = own_ref[k]
             n = cnt_ref[o]
             idx_ref[2 * o + n] = k
-            tgt_ref[2 * o + n] = slot_ref[k]
             cnt_ref[o] = n + 1
             return c
         lax.fori_loop(0, 128, place, 0)
@@ -143,19 +148,18 @@
     lax.fori_loop(0, 16, copy, 0)
 
 
-def route(owner, slot, child):
+def route(owner, child):
     return pl.pallas_call(
         route_kernel,
-        out_shape=(jax.ShapeDtypeStruct((128, 2, 128, 128), BF), jax.ShapeDtypeStruct((256,), jnp.int32)),
+        out_shape=jax.ShapeDtypeStruct((128, 2, 128, 128), BF),
         grid_spec=pltpu.PrefetchScalarGridSpec(
-            num_scalar_prefetch=2, grid=(8,),
-            in_specs=[pl.BlockSpec((128, 128, 128), lambda g, a, b: (0, 0, 0), pipeline_mode=pl.Buffered(1))],
-            out_specs=(pl.BlockSpec((16, 2, 128, 128), lambda g, a, b: (g, 0, 0, 0)),
-                       pl.BlockSpec(memory_space=pltpu.SMEM)),
+            num_scalar_prefetch=1, grid=(8,),
+            in_specs=[pl.BlockSpec((128, 128, 128), lambda g, a: (0, 0, 0), pipeline_mode=pl.Buffered(1))],
+            out_specs=pl.BlockSpec((16, 2, 128, 128), lambda g, a: (g, 0, 0, 0)),
             scratch_shapes=[pltpu.SMEM((256,), jnp.int32), pltpu.SMEM((128,), jnp.int32)]),
-        compiler_params=pltpu.CompilerParams(vmem_limit_bytes=24 << 20),
+        compiler_params=pltpu.CompilerParams(vmem_limit_bytes=60 << 20),
         name="route",
-    )(owner, slot, child)
+    )(owner, child)
 
 
 def head_kernel(land_ref, front_ref, arr_ref, out_ref, buf_ref, acc_ref, fsem, asem):
@@ -281,41 +285,227 @@
     )(a, hi, lo)
 
 
+def lead_kernel(front_ref, code_ref, lead_ref, codes_ref, own_ref, lsem, zs, zr, zls, zlr, xs, xr, ys, yr, as_, ar, bs, br, cs, cr):
+    sub, row, col = lax.axis_index("sub"), lax.axis_index("row"), lax.axis_index("col")
+    par = lax.rem(sub, 2)
+    mate = sub + 1 - 2 * par
+    line = 4 * par + row
+    need = (par == 1) | (col <= row)
+
+    def remote(src, dst, send, recv, **where):
+        return pltpu.make_async_remote_copy(src, dst, send, recv, device_id=where, device_id_type=MESH)
+
+    barrier = pltpu.get_barrier_semaphore()
+    for d in range(1, 8):
+        pl.semaphore_signal(barrier, inc=1, device_id={"sub": lax.rem(sub + d, 8)}, device_id_type=MESH)
+    for d in range(1, 4):
+        pl.semaphore_signal(barrier, inc=1, device_id={"row": lax.rem(row + d, 4)}, device_id_type=MESH)
+        pl.semaphore_signal(barrier, inc=1, device_id={"col": lax.rem(col + d, 4)}, device_id_type=MESH)
+
+    mine = [pltpu.make_async_copy(front_ref.at[0, 0, :, s, 0, :], own_ref.at[s], lsem.at[s]) for s in range(2)]
+    code = pltpu.make_async_copy(code_ref, codes_ref.at[col, row, sub], lsem.at[2])
+    code.start()
+    mine[0].start()
+    mine[1].start()
+    mine[0].wait()
+    mine[1].wait()
+    keep = [pltpu.make_async_copy(own_ref.at[s], lead_ref.at[line, 4 * s + col], lsem.at[3 + s]) for s in range(2)]
+
+    @pl.when(sub < 2)
+    def _():
+        keep[0].start()
+        keep[1].start()
+    pl.semaphore_wait(barrier, 13)
+
+    def zcode(d):
+        return remote(code_ref, codes_ref.at[col, row, sub], zs.at[d - 1], zr.at[d - 1], sub=lax.rem(sub + d, 8))
+    def zcode_in(d):
+        return remote(code_ref, codes_ref.at[col, row, lax.rem(sub + 8 - d, 8)], zs.at[d - 1], zr.at[d - 1], sub=lax.rem(sub + d, 8))
+    need1 = (par == 1) & (col <= row)
+
+    @pl.when(sub < 2)
+    def _():
+        for d in (1, 3, 2):
+            @pl.when(need)
+            def _():
+                remote(own_ref.at[0], lead_ref.at[line, col], zls.at[d - 1, 0], zlr.at[0], sub=sub + 2 * d).start()
+            @pl.when(need1)
+            def _():
+                remote(own_ref.at[1], lead_ref.at[line, 4 + col], zls.at[d - 1, 1], zlr.at[1], sub=sub + 2 * d).start()
+    for d in range(1, 8):
+        zcode(d).start()
+
+    @pl.when(sub < 2)
+    def _():
+        keep[0].wait()
+        keep[1].wait()
+
+    @pl.when(sub >= 2)
+    def _():
+        @pl.when(need)
+        def _():
+            remote(own_ref.at[0], lead_ref.at[line, col], zls.at[0, 0], zlr.at[0], sub=par).wait_recv()
+        @pl.when(need1)
+        def _():
+            remote(own_ref.at[1], lead_ref.at[line, 4 + col], zls.at[0, 1], zlr.at[1], sub=par).wait_recv()
+
+    def ax(d, r):
+        return remote(lead_ref.at[4 + r, col], lead_ref.at[4 + r, col], as_.at[0, d - 1], ar.at[0, d - 1], row=lax.rem(row + d, 4))
+    def ay(d, c):
+        return remote(lead_ref.at[pl.ds(4, 4), c], lead_ref.at[pl.ds(4, 4), c], as_.at[1, d - 1], ar.at[1, d - 1], col=lax.rem(col + d, 4))
+    def by(d, c):
+        at = lead_ref.at[line, 4 * par + c]
+        return remote(at, at, bs.at[d - 1, 4], br.at[d - 1, 4], col=lax.rem(col + d, 4))
+    def bx(d, r, c):
+        at = lead_ref.at[4 * par + r, 4 * par + c]
+        return remote(at, at, bs.at[d - 1, c], br.at[d - 1, c], row=lax.rem(row + d, 4))
+    for d in (1, 3, 2):
+        @pl.when(par == 1)
+        def _():
+            ax(d, row).start()
+        @pl.when(col <= row)
+        def _():
+            by(d, col).start()
+    code.wait()
+    for d in range(1, 8):
+        zcode_in(d).wait_recv()
+    def cx(d, r):
+        return remote(codes_ref.at[col, r], codes_ref.at[col, r], xs.at[d - 1], xr.at[d - 1], row=lax.rem(row + d, 4))
+    def cy(d, c):
+        return remote(codes_ref.at[c], codes_ref.at[c], ys.at[d - 1], yr.at[d - 1], col=lax.rem(col + d, 4))
+    for d in range(1, 4):
+        cx(d, row).start()
+    for d in range(1, 4):
+        @pl.when(par == 1)
+        def _():
+            ax(d, lax.rem(row + 4 - d, 4)).wait_recv()
+        @pl.when(lax.rem(col + 4 - d, 4) <= row)
+        def _():
+            by(d, lax.rem(col + 4 - d, 4)).wait_recv()
+    for d in (1, 3, 2):
+        @pl.when(par == 1)
+        def _():
+            ay(d, col).start()
+        for c in range(4):
+            @pl.when(c <= row)
+            def _():
+                bx(d, row, c).start()
+    for d in range(1, 4):
+        cx(d, lax.rem(row + 4 - d, 4)).wait_recv()
+    for d in range(1, 4):
+        cy(d, col).start()
+    for d in range(1, 4):
+        @pl.when(par == 1)
+        def _():
+            ay(d, lax.rem(col + 4 - d, 4)).wait_recv()
+        for c in range(4):
+            r = lax.rem(row + 4 - d, 4)
+            @pl.when(c <= r)
+            def _():
+                bx(d, r, c).wait_recv()
+
+    def swap(i):
+        at = lead_ref.at[i, pl.ds(0, i + 1)]
+        return remote(at, at, cs.at[i % 4], cr.at[i % 4], sub=mate)
+    for i in range(8):
+        @pl.when(par == i // 4)
+        def _():
+            swap(i).start()
+    for i in range(8):
+        @pl.when(par != i // 4)
+        def _():
+            swap(i).wait_recv()
+    for d in range(1, 4):
+        cy(d, lax.rem(col + 4 - d, 4)).wait_recv()
+
+    for d in range(1, 8):
+        zcode(d).wait_send()
+    @pl.when(sub < 2)
+    def _():
+        for d in (1, 2, 3):
+            @pl.when(need)
+            def _():
+                remote(own_ref.at[0], lead_ref.at[line, col], zls.at[d - 1, 0], zlr.at[0], sub=sub + 2 * d).wait_send()
+            @pl.when(need1)
+            def _():
+                remote(own_ref.at[1], lead_ref.at[line, 4 + col], zls.at[d - 1, 1], zlr.at[1], sub=sub + 2 * d).wait_send()
+    for d in range(1, 4):
+        cx(d, row).wait_send()
+        cy(d, col).wait_send()
+        @pl.when(par == 1)
+        def _():
+            ax(d, row).wait_send()
+            ay(d, col).wait_send()
+        @pl.when(col <= row)
+        def _():
+            by(d, col).wait_send()
+        for c in range(4):
+            @pl.when(c <= row)
+            def _():
+                bx(d, row, c).wait_send()
+    for i in range(8):
+        @pl.when(par == i // 4)
+        def _():
+            swap(i).wait_send()
+
+
+def lead_gather(front, code):
+    D = pltpu.SemaphoreType.DMA
+    return pl.pallas_call(
+        lead_kernel,
+        out_shape=(jax.ShapeDtypeStruct((8, 8, 128, 128), F32), jax.ShapeDtypeStruct((4, 4, 8, 1, 128), jnp.int32)),
+        in_specs=[pl.BlockSpec(memory_space=pltpu.HBM), pl.BlockSpec(memory_space=V)],
+        out_specs=(pl.BlockSpec(memory_space=V), pl.BlockSpec(memory_space=V)),
+        scratch_shapes=[V((2, 128, 128), F32), D((5,)), D((7,)), D((7,)), D((3, 2)), D((2,)), D((3,)), D((3,)), D((3,)), D((3,)),
+                        D((2, 3)), D((2, 3)), D((3, 5)), D((3, 5)), D((4,)), D((4,))],
+        compiler_params=pltpu.CompilerParams(vmem_limit_bytes=24 << 20, collective_id=1, has_side_effects=True),
+        name="lead",
+    )(front, code)
+
+
+def landings(codes, me):
+    codes = codes[:, :, :, 0, :].transpose(2, 1, 0, 3).reshape(128, 128)
+    place = lax.broadcasted_iota(jnp.int32, (128, 128), 1) * 128 + codes % 128
+    match = codes // 128 == me
+    first = jnp.min(jnp.where(match, place, 1 << 20), 1)
+    last = jnp.max(jnp.where(match, place, -1), 1)
+    one = jnp.where(last >= 0, first % 128, -1)
+    two = jnp.where(last > first, last % 128, -1)
+    return jnp.stack([one, two], 1).reshape(256)
+
+
 def local(front, child_tiles, tile_owner, tile_slot):
     sub = lax.axis_index("sub")
     row = lax.axis_index("row")
     col = lax.axis_index("col")
     group = sub * 4 + row
-    outgoing, targets = route(tile_owner[:, 0], tile_slot, child_tiles)
-    landing = lax.all_to_all(targets.reshape(128, 2), ("sub", "row", "col"), split_axis=0, concat_axis=0, tiled=True).reshape(256)
-    corner = front[0, 0, :, :2, 0, :].transpose(1, 0, 2)
-    held = jnp.stack([jnp.where(sub == g, corner, jnp.zeros_like(corner)) for g in range(2)])
-    held = lax.psum(held, "sub")
-    lead = lax.all_gather(held, ("row", "col"), axis=0, tiled=False)
-    lead = lead.reshape(4, 4, 2, 2, 128, 128).transpose(2, 0, 3, 1, 4, 5).reshape(8, 8, 128, 128)
+    owner = tile_owner[:, 0]
+    outgoing = route(owner, child_tiles)
+    lead, codes = lead_gather(front, (owner * 128 + tile_slot).reshape(1, 128))
     outgoing, lead = lax.optimization_barrier((outgoing, lead))
     arrived = lax.all_to_all(outgoing, ("sub", "row", "col"), split_axis=0, concat_axis=0, tiled=True)
     arrived = arrived.reshape(256, 128, 128)
     factor, hi, lo = chol(lead)
+    landing = landings(codes, group * 4 + col)
     panel = head(landing, front, arrived)
     wide = lax.all_gather(panel, "col", axis=0, tiled=False)
-    wide = wide.transpose(2, 3, 1, 0, 4).reshape(512, 1024) if False else wide.transpose(2, 3, 1, 0, 4).reshape(4 * 128, 1024)
+    wide = wide.transpose(2, 3, 1, 0, 4).reshape(512, 1024)
     solved = solve(wide, hi, lo)
     return solved, factor, landing, arrived, front, sub, row, col, group
 
 
 def finish(front, child_tiles, tile_owner, tile_slot):
-    solved, factor, landing, arrived, front, sub, row, col, group = local(front, child_tiles, tile_owner, tile_slot)
-    mine = lax.dynamic_slice_in_dim(factor, jnp.minimum(group, 7) * 128, 128, 0)
-    top = group < 8
-    brow = solved.reshape(4, 128, 1024)
-    rows = brow.at[0].set(jnp.where(top, mine, brow[0]))
-    panel_out = lax.dynamic_index_in_dim(rows.reshape(4, 128, 2, 4, 128), col, 3, keepdims=True)
-    panel_out = panel_out.reshape(4, 1, 128, 2, 1, 128)
-    brow = brow.at[0].set(jnp.where(top, jnp.zeros_like(mine), brow[0])).reshape(512, 1024)
-    across = lax.psum(jnp.where(row == col, solved, jnp.zeros_like(solved)), "row")
-    bcol = lax.all_gather(across.reshape(1, 4, 128, 1024), "sub", axis=0, tiled=True)
-    return fin(landing, front, arrived, brow, bcol), panel_out
+  solved, factor, landing, arrived, front, _, row, col, group = local(front, child_tiles, tile_owner, tile_slot)
+  mine = lax.dynamic_slice_in_dim(factor, jnp.minimum(group, 7) * 128, 128, 0)
+  top = group < 8
+  brow = solved.reshape(4, 128, 1024)
+  rows = brow.at[0].set(jnp.where(top, mine, brow[0]))
+  panel_out = lax.dynamic_index_in_dim(rows.reshape(4, 128, 2, 4, 128), col, 3, keepdims=True)
+  panel_out = panel_out.reshape(4, 1, 128, 2, 1, 128)
+  brow = brow.at[0].set(jnp.where(top, jnp.zeros_like(mine), brow[0])).reshape(512, 1024)
+  across = lax.psum(jnp.where(row == col, solved, jnp.zeros_like(solved)), "row")
+  bcol = lax.all_gather(across.reshape(1, 4, 128, 1024), "sub", axis=0, tiled=True)
+  return fin(landing, front, arrived, brow, bcol), panel_out
 
 
 def solution(mesh):

time: 474 us -> 398 us (0.84)
  waiting for transfers between devices: 288 us -> 193 us
  Pallas kernels: 120 us -> 146 us
    psum x1 -> x0, waiting for transfers between devices: 63.5 us -> none  [local(): held = lax.psum(held, 'sub')]
    all_gather x1 -> x0, waiting for transfers between devices: 32 us -> none  [local(): lead = lax.all_gather(held, ('row', 'col'), axis=0, tiled=False)]
    pallas_call x1 -> x2, Pallas kernels: 5.43 us -> 36 us  [the longest x1 27.9 us: lead_gather(): pl.pallas_call(lead_kernel, out_shape=(jax.ShapeDtypeStruct((8, 8, 128, 1...]
    all_to_all x1 -> x0, starting transfers between devices: 9.32 us -> none  [local(): lax.all_to_all(targets.reshape(128, 2), ('sub', 'row', 'col'), split_axis...]
    all_to_all x1, starting transfers between devices: 8.62 us -> 13.5 us  [local(): lax.all_to_all(outgoing, ('sub', 'row', 'col'), split_axis=0, concat_axis...]
    unnamed x17 -> x21, local copies, waits for them, and re-layouts: 11.1 us -> 15.7 us
  transfers between devices with their start and end apart: 7 -> 4, of which waited for: 5 -> 3; matrix products, arithmetic and copies ran while one was open for 3% -> 2% of each run, Pallas kernels for 17% -> 18%
where the time goes in v2:
time: 398 us; the launch traced here: 397 us
  waiting for transfers between devices  193 us (48%)
  Pallas kernels  146 us (37%)
  local copies, waits for them, and re-layouts  26.7 us (7%)
  between operations  13.9 us (3%)
  starting transfers between devices  13.6 us (3%)
    all_to_all x1, waiting for transfers between devices, local(): lax.all_to_all(outgoing, ('sub', 'row', 'col'), split_axis=0, concat_axis...  98.5 us
    pallas_call x1, Pallas kernels, chol(): pl.pallas_call(chol_kernel, out_shape=[jax.ShapeDtypeStruct((1024, 1024),...  72.7 us
    all_gather x1, waiting for transfers between devices, finish(): lax.all_gather(across.reshape(1, 4, 128, 1024), 'sub', axis=0, tiled=True)  49.3 us
    psum x1, waiting for transfers between devices, finish(): lax.psum(jnp.where(row == col, solved, jnp.zeros_like(solved)), 'row')  45.5 us
    pallas_call x1, Pallas kernels, lead_gather(): pl.pallas_call(lead_kernel, out_shape=(jax.ShapeDtypeStruct((8, 8, 128, 1...  27.9 us
    pallas_call x1, Pallas kernels, fin(): pl.pallas_call(fin_kernel, out_shape=jax.ShapeDtypeStruct((4, 1, 128, 32,...  20.1 us
    unnamed x21, local copies, waits for them, and re-layouts  15.7 us
    all_to_all x1, starting transfers between devices, local(): lax.all_to_all(outgoing, ('sub', 'row', 'col'), split_axis=0, concat_axis...  13.5 us
  transfers between devices with their start and end apart: 4, of which 3 were waited for; matrix products, arithmetic and copies ran while one was open for 2% of the time, Pallas kernels for 18%

profile of v2, /device:TPU:1, one launch (start us, length us, event | category | flops | bytes accessed | tf_op | source)
XLA Modules:
  0.0 397.1 jit_solution(12695488457554745580)
XLA Ops:
  7.2 0.7 add_bitcast_fusion.code_ref
  7.8 0.0 copy-start
  7.8 3.4 copy-done
  11.2 27.9 %lead.1 = (f32[8,8,128,128]{3,2,1,0:T(8,128)S(1)}, s32[4,4,8,1,128]{4,3,2,1,0:T(1,128)S(1)}) custom-call(f32[4,1,128,32,1,128]{5,4,3,2,1,0:T(1,128)S(1)} %copy-done, s32[1,128]{1,0:T(1,128)S(1)} %add_bitcast_fusion.code_ref), custom_call_target="tpu_custom_call" | custom-call | tf_op jit(solution)/shard_map/lead/pallas_call | solution.py:454
  39.2 0.0 copy-start.1
  39.2 2.0 copy-done.1
  41.1 8.1 %route.1 = bf16[128,2,128,128]{3,2,1,0:T(8,128)(2,1)} custom-call(s32[128]{0:T(128)} %bitcast.30, bf16[128,128,128]{2,1,0:T(8,128)(2,1)} %child_ref.1), custom_call_target="tpu_custom_call" | custom-call | tf_op jit(solution)/shard_map/route/pallas_call | solution.py:152
  49.2 13.5 %all-to-all-start = ((bf16[128,2,128,128]{3,2,1,0:T(8,128)(2,1)}), bf16[128,2,128,128]{3,2,1,0:T(8,128)(2,1)}, u32[]{:S(2)}, u32[]{:S(2)}) async-start(bf16[128,2,128,128]{3,2,1,0:T(8,128)(2,1)} %route.1), calls=%async_computation | async-start | bytes 16777216 | tf_op jit(solution)/shard_map/all_to_all | solution.py:486
  62.7 0.0 all-gather.6.cloned.1.call-start
  62.8 0.6 select_reduce_fusion
  63.5 0.1 copy.12
  63.6 0.1 reduce_min.12
  63.7 0.1 copy.11
  63.8 0.1 reduce_max.12
  63.9 0.1 copy.13
  64.0 0.7 reshape.248.land_ref
  64.8 98.5 %all-to-all-done = bf16[128,2,128,128]{3,2,1,0:T(8,128)(2,1)} async-done(((bf16[128,2,128,128]{3,2,1,0:T(8,128)(2,1)}), bf16[128,2,128,128]{3,2,1,0:T(8,128)(2,1)}, u32[]{:S(2)}, u32[]{:S(2)}) %all-to-all-start) | async-done | bytes 8388640 | tf_op jit(solution)/shard_map/all_to_all | solution.py:486
  163.3 8.6 %head.1 = f32[2,4,128,128]{3,2,1,0:T(8,128)} custom-call(s32[256]{0:T(256)} %reshape.248.land_ref, f32[4,1,128,32,1,128]{5,4,3,2,1,0:T(1,128)} %front_ref.5, bf16[256,128,128]{2,1,0:T(8,128)(2,1)} %bitcast.5.arr_ref), custom_call_target="tpu_custom_call" | custom-call | tf_op jit(solution)/shard_map/head/pallas_call | solution.py:190
  171.9 0.0 all-gather.6.cloned.1.call-update
  171.9 0.0 all-reduce.2.cloned.1.call-start
  172.0 0.0 copy-start.2
  172.0 2.2 copy-done.2
  174.2 72.7 %chol.1 = (bf16[1024,1024]{1,0:T(8,128)(2,1)S(1)}, bf16[1024,1024]{1,0:T(8,128)(2,1)S(1)}, bf16[1024,1024]{1,0:T(8,128)(2,1)S(1)}) custom-call(f32[8,8,128,128]{3,2,1,0:T(8,128)S(1)} %copy-done.2), custom_call_target="tpu_custom_call" | custom-call | tf_op jit(solution)/shard_map/chol/pallas_call | solution.py:112
  246.9 0.0 copy-start.3
  246.9 1.3 copy-done.3
  248.2 1.4 copy-done.5
  249.5 1.3 copy-done.7
  250.9 4.3 %copy.19 = f32[4,2,4,128,128]{4,0,1,3,2:T(4,128)} copy(f32[4,2,4,128,128]{4,3,2,1,0:T(8,128)} %bitcast.28) | data formatting | bytes 4194304 | tf_op jit(solution)/shard_map/all_gather | solution.py:491
  255.1 2.1 reshape.250.a_ref
  257.2 0.0 copy-start.4
  257.2 1.6 copy-done.4
  258.8 1.6 copy-done.6
  260.4 8.7 %solve.1 = bf16[512,1024]{1,0:T(8,128)(2,1)S(1)} custom-call(f32[512,1024]{1,0:T(8,128)S(1)} %reshape.250.a_ref, bf16[1024,1024]{1,0:T(8,128)(2,1)S(1)} %copy-done.4, bf16[1024,1024]{1,0:T(8,128)(2,1)S(1)} %copy-done.6), custom_call_target="tpu_custom_call" | custom-call | tf_op jit(solution)/shard_map/solve/pallas_call | solution.py:277
  269.1 1.0 broadcast_select_fusion
  270.1 0.0 all-reduce.2.cloned.1.call-update
  270.2 0.0 all-gather.4.cloned.1.call-start
  270.2 45.5 %all-reduce.2.cloned.1.call-done = bf16[1,4,128,1024]{3,2,1,0:T(8,128)(2,1)} async-done(((bf16[1,4,128,1024]{3,2,1,0:T(8,128)(2,1)}), bf16[1,4,128,1024]{3,2,1,0:T(8,128)(2,1)}) %all-reduce.2.cloned.1.call-update) | async-done | bytes 1048592 | tf_op jit(solution)/shard_map/psum | solution.py:506
  315.7 0.0 all-gather.4.cloned.1.call-update
  315.7 0.1 copy.23
  315.8 0.1 copy.21
  315.9 1.0 bitcast_dynamic-update-slice_fusion
  316.9 1.5 reshape.256
  318.5 1.8 constant_dynamic-slice_fusion
  320.2 0.9 copy.20
  321.2 0.0 copy-start.8
  321.2 49.3 %all-gather.4.cloned.1.call-done.bcol_ref = bf16[8,4,128,1024]{3,2,1,0:T(8,128)(2,1)} async-done(((bf16[1,4,128,1024]{3,2,1,0:T(8,128)(2,1)}), bf16[8,4,128,1024]{3,2,1,0:T(8,128)(2,1)}) %all-gather.4.cloned.1.call-update) | async-done | bytes 8388624 | tf_op jit(solution)/shard_map/all_gather | solution.py:507
  370.5 0.0 copy-done.8
  370.5 20.1 %fin.1 = f32[4,1,128,32,1,128]{5,4,3,2,1,0:T(1,128)} custom-call(s32[256]{0:T(256)} %reshape.248.land_ref, f32[4,1,128,32,1,128]{5,4,3,2,1,0:T(1,128)} %front_ref.5, bf16[256,128,128]{2,1,0:T(8,128)(2,1)} %bitcast.5.arr_ref, bf16[512,1024]{1,0:T(8,128)(2,1)} %bitcast.26, bf16[8,4,128,1024]{3,2,1,0:T(8,128)(2,1)} %all-gather.4.cloned.1.call-done.bcol_ref), custom_call_target="tpu_custom_call" | custom-call | tf_op jit(solution)/shard_map/fin/pallas_call | solution.py:251
  (8 shorter events, 0.1 us)
Async XLA Ops:
  7.8 3.4 copy-start
  39.2 2.0 copy-start.1
  49.2 114.1 %all-to-all-start = ((bf16[128,2,128,128]{3,2,1,0:T(8,128)(2,1)}), bf16[128,2,128,128]{3,2,1,0:T(8,128)(2,1)}, u32[]{:S(2)}, u32[]{:S(2)}) async-start(bf16[128,2,128,128]{3,2,1,0:T(8,128)(2,1)} %route.1), calls=%async_computation | async-start | bytes 16777216 | tf_op jit(solution)/shard_map/all_to_all | solution.py:486
  62.7 188.1 %all-gather.6.cloned.1.call-start = ((), (), s32[]{:S(2)}) async-start(), calls=%async_computation.3 | async-start | bytes 2621440 | tf_op jit(solution)/shard_map/all_gather | solution.py:491
  171.9 143.8 %all-reduce.2.cloned.1.call-start = ((), (), s32[]{:S(2)}) async-start(), calls=%async_computation.1 | async-start | bytes 2097152 | tf_op jit(solution)/shard_map/psum | solution.py:506
  172.0 2.2 copy-start.2
  246.9 1.3 copy-start.3
  248.2 1.4 copy-start.5
  249.5 1.3 copy-start.7
  257.2 1.6 copy-start.4
  258.8 1.6 copy-start.6
  270.2 100.3 %all-gather.4.cloned.1.call-start = ((), (), s32[]{:S(2)}) async-start(), calls=%async_computation.2 | async-start | bytes 9437184 | tf_op jit(solution)/shard_map/all_gather | solution.py:507
  321.2 49.3 %copy-start.8 = (bf16[4,128,1024]{2,1,0:T(8,128)(2,1)}, bf16[4,128,1024]{2,1,0:T(8,128)(2,1)S(1)}, u32[]{:S(2)}) copy-start(bf16[4,128,1024]{2,1,0:T(8,128)(2,1)S(1)} %bitcast_dynamic-update-slice_fusion.1) | copy-start | bytes 3145732
Sparse Core Ops, SparseCore 0:
  172.0 31.7 all-gather.5
  270.3 45.3 all-reduce.1
  317.4 53.0 all-gather.3

commit v3 on v2

--- a/solution.py
+++ b/solution.py
@@ -239,7 +239,9 @@
         y = lax.dot_general(brow_ref[...], bc_ref[pl.ds(pl.multiple_of(g * 256, 256), 256), :],
                             (((1,), (1,)), ((), ())), preferred_element_type=F32)
         for u in range(2):
-            acc_ref[s + u] = acc_ref[s + u] - y[:, u * 128:(u + 1) * 128].reshape(4, 128, 128)
+            z = y[:, u * 128:(u + 1) * 128].reshape(4, 128, 128)
+            acc_ref[s + u, 0] = acc_ref[s + u, 0] - jnp.where(land_ref[256] > 0, z[0], 0.0)
+            acc_ref[s + u, 1:4] = acc_ref[s + u, 1:4] - z[1:4]
             put(s + u).start()
         return carry
     lax.fori_loop(1, 16, update, 0)
@@ -263,26 +265,211 @@
     )(land, front, arrived, brow, bcol)
 
 
-def solve_kernel(a_ref, hi_ref, lo_ref, b_ref):
-    a = a_ref[...]
-    ah = a.astype(BF)
-    al = (a - ah.astype(F32)).astype(BF)
+def panel_kernel(panel_ref, hi_hbm, lo_hbm, low_hbm, brow_ref, bcol_ref, arow, ah, al, hi, lo, low, xb, rl,
+                 lsem, ps, pr, xs, xr, ws, wr, ys, yr, rs, rr, zs, zr, fs, fr, ms, mr):
+    sub, row, col = lax.axis_index("sub"), lax.axis_index("row"), lax.axis_index("col")
+    group = 4 * sub + row
+    mate = sub + 1 - 2 * lax.rem(sub, 2)
+
+    def n4(x, d):
+        return lax.rem(x + 4 + d, 4)
+
+    def n8(x, d):
+        return lax.rem(x + 8 + d, 8)
+
+    def remote(src, dst, send, recv, **where):
+        return pltpu.make_async_remote_copy(src, dst, send, recv, device_id=where, device_id_type=MESH)
+
+    loads = [pltpu.make_async_copy(hi_hbm, hi, lsem.at[0]), pltpu.make_async_copy(lo_hbm, lo, lsem.at[1]),
+             pltpu.make_async_copy(low_hbm.at[pl.ds(pl.multiple_of(lax.min(group, 7) * 128, 128), 128)], low, lsem.at[2]),
+             pltpu.make_async_copy(panel_ref.at[:, col], arow.at[col], lsem.at[3])]
+    barrier = pltpu.get_barrier_semaphore()
+    for d in (1, 3):
+        pl.semaphore_signal(barrier, inc=1, device_id={"row": n4(row, d)}, device_id_type=MESH)
+        pl.semaphore_signal(barrier, inc=1, device_id={"sub": n8(sub, 2 * d if d == 1 else -2)}, device_id_type=MESH)
+    for d in (1, 2, 3):
+        pl.semaphore_signal(barrier, inc=1, device_id={"col": n4(col, d)}, device_id_type=MESH)
+    pl.semaphore_signal(barrier, inc=1, device_id={"sub": mate}, device_id_type=MESH)
+    for copy in loads:
+        copy.start()
+    pl.semaphore_wait(barrier, 8)
+
+    def take(d):
+        return remote(panel_ref.at[:, n4(col, d)], arow.at[col], ps.at[d - 1], pr.at[d - 1], col=n4(col, d))
+    def taken(d):
+        return remote(panel_ref.at[:, n4(col, d)], arow.at[n4(col, -d)], ps.at[d - 1], pr.at[d - 1], col=n4(col, d))
+    for d in (1, 3, 2):
+        take(d).start()
+    loads[3].wait()
+    for d in (1, 3, 2):
+        taken(d).wait_recv()
+    for s in range(2):
+        for t in range(4):
+            a = arow[t, s]
+            h = a.astype(BF)
+            at = (4 * s + t) * 128
+            ah[:, at:at + 128] = h
+            al[:, at:at + 128] = (a - h.astype(F32)).astype(BF)
+    for copy in loads[:3]:
+        copy.wait()
+    top = (group < 8) & (col == 0)
+
     def mm(x, y):
         return lax.dot_general(x, y, (((1,), (1,)), ((), ())), preferred_element_type=F32)
-    b_ref[...] = (mm(ah, hi_ref[...]) + (mm(ah, lo_ref[...]) + mm(al, hi_ref[...]))).astype(BF)
-
-
-def solve(a, hi, lo):
-    full = pl.BlockSpec((1024, 1024), lambda g: (0, 0), pipeline_mode=pl.Buffered(1))
+    for b in range(4):
+        w = 256 * (b + 1)
+        rows = pl.ds(256 * b, 256)
+        y = mm(ah[:, 0:w], hi[rows, 0:w]) + (mm(ah[:, 0:w], lo[rows, 0:w]) + mm(al[:, 0:w], hi[rows, 0:w]))
+        y = jnp.where(top, low[:, 256 * b:w], y.astype(BF))
+        xb[row, :, 256 * b:w] = y
+        brow_ref[col, :, 256 * b:w] = y
+
+    half = [pl.ds(0, 64), pl.ds(64, 64)]
+    step = [1, -1]
+    def xsend(i):
+        return remote(xb.at[row], xb.at[row], xs.at[i], xr.at[i], row=n4(row, step[i]))
+    def xrecv(i):
+        at = xb.at[n4(row, -step[i])]
+        return remote(at, at, xs.at[i], xr.at[i], row=n4(row, step[i]))
+    def xforward(i, r):
+        at = xb.at[r, half[i]]
+        return remote(at, at, xs.at[2 + i], xr.at[2 + i], row=n4(row, step[i]))
+    def wsend(i):
+        return remote(brow_ref.at[col], brow_ref.at[col], ws.at[i], wr.at[i], col=n4(col, step[i]))
+    def wrecv(i):
+        at = brow_ref.at[n4(col, -step[i])]
+        return remote(at, at, ws.at[i], wr.at[i], col=n4(col, step[i]))
+    def wforward(i, c):
+        at = brow_ref.at[c, half[i]]
+        return remote(at, at, ws.at[2 + i], wr.at[2 + i], col=n4(col, step[i]))
+
+    def ynear(i):
+        return remote(xb.at[n4(col, step[i])], bcol_ref.at[sub, col], ys.at[i], yr.at[i], col=n4(col, step[i]))
+    def ynear_in(i):
+        return remote(xb.at[0], bcol_ref.at[sub, n4(col, -step[i])], ys.at[i], yr.at[i], col=n4(col, step[i]))
+    def yfar(i):
+        return remote(xb.at[n4(col, 2), half[i]], rl.at[i], rs.at[i], rr.at[i], col=n4(col, step[i]))
+    def yrelay(i):
+        return remote(rl.at[i], bcol_ref.at[sub, n4(col, -step[i]), half[i]], ys.at[2 + i], yr.at[2 + i], col=n4(col, step[i]))
+    def yfar_in(i):
+        return remote(rl.at[i], bcol_ref.at[sub, n4(col, 2), half[i]], ys.at[2 + i], yr.at[2 + i], col=n4(col, step[i]))
+    home = pltpu.make_async_copy(xb.at[col], bcol_ref.at[sub, col], lsem.at[4])
+
+    def ysend(c):
+        d = n4(c, -col)
+        @pl.when(d == 0)
+        def _():
+            home.start()
+        for i in range(2):
+            @pl.when(d == (1, 3)[i])
+            def _():
+                ynear(i).start()
+        @pl.when(d == 2)
+        def _():
+            yfar(0).start()
+            yfar(1).start()
+
+    for i in range(2):
+        xsend(i).start()
+    for i in range(2):
+        wsend(i).start()
+    ysend(row)
+    for i in range(2):
+        xrecv(i).wait_recv()
+        xforward(i, n4(row, -step[i])).start()
+        ysend(n4(row, -step[i]))
+    for i in range(2):
+        wrecv(i).wait_recv()
+        wforward(i, n4(col, -step[i])).start()
+    for i in range(2):
+        xforward(i, n4(row, 2)).wait_recv()
+    ysend(n4(row, 2))
+    for i in range(2):
+        yfar(i).wait_recv()
+        yrelay(i).start()
+
+    def own(e, i):
+        at = bcol_ref.at[sub, n4(col, e)]
+        return remote(at, at, zs.at[i, e], zr.at[i, e], sub=n8(sub, 2 * step[i]))
+    def arrive(e, i):
+        at = bcol_ref.at[n8(sub, -2 * step[i]), n4(col, e)]
+        return remote(at, at, zs.at[i, e], zr.at[i, e], sub=n8(sub, 2 * step[i]))
+    side = [0, 0, 1, 1]
+    def onward(e, z):
+        at = bcol_ref.at[n8(sub, z), n4(col, e)]
+        return remote(at, at, fs.at[e], fr.at[e], sub=n8(sub, 2 * step[side[e]]))
+    def swap(e, k, z):
+        at = bcol_ref.at[n8(sub, z), n4(col, e)]
+        return remote(at, at, ms.at[k, e], mr.at[k, e], sub=mate)
+    def swapped(e, k, z):
+        at = bcol_ref.at[n8(mate, z), n4(col, e)]
+        return remote(at, at, ms.at[k, e], mr.at[k, e], sub=mate)
+
+    def launch(e):
+        own(e, 0).start()
+        own(e, 1).start()
+        swap(e, 0, 0).start()
+    home.wait()
+    launch(0)
+    ynear_in(1).wait_recv()
+    launch(1)
+    ynear_in(0).wait_recv()
+    launch(3)
+    yfar_in(0).wait_recv()
+    yfar_in(1).wait_recv()
+    launch(2)
+    for e in (0, 1, 3, 2):
+        for i in range(2):
+            arrive(e, i).wait_recv()
+            if side[e] == i:
+                onward(e, -2 * step[i]).start()
+            swap(e, 1 + i, -2 * step[i]).start()
+    for e in (0, 1, 3, 2):
+        onward(e, 4).wait_recv()
+        swap(e, 3, 4).start()
+    for e in range(4):
+        swapped(e, 0, 0).wait_recv()
+        swapped(e, 1, -2).wait_recv()
+        swapped(e, 2, 2).wait_recv()
+        swapped(e, 3, 4).wait_recv()
+    for i in range(2):
+        wforward(i, n4(col, 2)).wait_recv()
+
+    for d in (1, 2, 3):
+        take(d).wait_send()
+    for i in range(2):
+        xsend(i).wait_send()
+        wsend(i).wait_send()
+        xforward(i, n4(row, -step[i])).wait_send()
+        wforward(i, n4(col, -step[i])).wait_send()
+        ynear(i).wait_send()
+        yfar(i).wait_send()
+        yrelay(i).wait_send()
+    for e in range(4):
+        own(e, 0).wait_send()
+        own(e, 1).wait_send()
+        onward(e, -2 * step[side[e]]).wait_send()
+        swap(e, 0, 0).wait_send()
+        swap(e, 1, -2).wait_send()
+        swap(e, 2, 2).wait_send()
+        swap(e, 3, 4).wait_send()
+
+
+def panel_exchange(panel, hi, lo, low):
+    D = pltpu.SemaphoreType.DMA
+    H = pltpu.HBM
     return pl.pallas_call(
-        solve_kernel,
-        out_shape=jax.ShapeDtypeStruct((512, 1024), BF),
-        grid=(4,),
-        in_specs=[pl.BlockSpec((128, 1024), lambda g: (g, 0)), full, full],
-        out_specs=pl.BlockSpec((128, 1024), lambda g: (g, 0)),
-        compiler_params=pltpu.CompilerParams(vmem_limit_bytes=24 << 20),
-        name="solve",
-    )(a, hi, lo)
+        panel_kernel,
+        out_shape=(jax.ShapeDtypeStruct((4, 128, 1024), BF), jax.ShapeDtypeStruct((8, 4, 128, 1024), BF)),
+        in_specs=[pl.BlockSpec(memory_space=V)] + [pl.BlockSpec(memory_space=H)] * 3,
+        out_specs=(pl.BlockSpec(memory_space=V), pl.BlockSpec(memory_space=H)),
+        scratch_shapes=[V((4, 2, 128, 128), F32), V((128, 1024), BF), V((128, 1024), BF), V((1024, 1024), BF), V((1024, 1024), BF),
+                        V((128, 1024), BF), V((4, 128, 1024), BF), V((2, 64, 1024), BF),
+                        D((5,)), D((3,)), D((3,)), D((4,)), D((4,)), D((4,)), D((4,)), D((4,)), D((4,)), D((2,)), D((2,)),
+                        D((2, 4)), D((2, 4)), D((4,)), D((4,)), D((4, 4)), D((4, 4))],
+        compiler_params=pltpu.CompilerParams(vmem_limit_bytes=60 << 20, collective_id=2, has_side_effects=True),
+        name="panel",
+    )(panel, hi, lo, low)
 
 
 def lead_kernel(front_ref, code_ref, lead_ref, codes_ref, own_ref, lsem, zs, zr, zls, zlr, xs, xr, ys, yr, as_, ar, bs, br, cs, cr):
@@ -458,7 +645,7 @@
         out_specs=(pl.BlockSpec(memory_space=V), pl.BlockSpec(memory_space=V)),
         scratch_shapes=[V((2, 128, 128), F32), D((5,)), D((7,)), D((7,)), D((3, 2)), D((2,)), D((3,)), D((3,)), D((3,)), D((3,)),
                         D((2, 3)), D((2, 3)), D((3, 5)), D((3, 5)), D((4,)), D((4,))],
-        compiler_params=pltpu.CompilerParams(vmem_limit_bytes=24 << 20, collective_id=1, has_side_effects=True),
+        compiler_params=pltpu.CompilerParams(vmem_limit_bytes=60 << 20, collective_id=1, has_side_effects=True),
         name="lead",
     )(front, code)
 
@@ -488,29 +675,16 @@
     factor, hi, lo = chol(lead)
     landing = landings(codes, group * 4 + col)
     panel = head(landing, front, arrived)
-    wide = lax.all_gather(panel, "col", axis=0, tiled=False)
-    wide = wide.transpose(2, 3, 1, 0, 4).reshape(512, 1024)
-    solved = solve(wide, hi, lo)
-    return solved, factor, landing, arrived, front, sub, row, col, group
-
-
-def finish(front, child_tiles, tile_owner, tile_slot):
-  solved, factor, landing, arrived, front, _, row, col, group = local(front, child_tiles, tile_owner, tile_slot)
-  mine = lax.dynamic_slice_in_dim(factor, jnp.minimum(group, 7) * 128, 128, 0)
-  top = group < 8
-  brow = solved.reshape(4, 128, 1024)
-  rows = brow.at[0].set(jnp.where(top, mine, brow[0]))
-  panel_out = lax.dynamic_index_in_dim(rows.reshape(4, 128, 2, 4, 128), col, 3, keepdims=True)
-  panel_out = panel_out.reshape(4, 1, 128, 2, 1, 128)
-  brow = brow.at[0].set(jnp.where(top, jnp.zeros_like(mine), brow[0])).reshape(512, 1024)
-  across = lax.psum(jnp.where(row == col, solved, jnp.zeros_like(solved)), "row")
-  bcol = lax.all_gather(across.reshape(1, 4, 128, 1024), "sub", axis=0, tiled=True)
-  return fin(landing, front, arrived, brow, bcol), panel_out
+    brow, bcol = panel_exchange(panel, hi, lo, factor)
+    panel_out = lax.dynamic_index_in_dim(brow.reshape(4, 128, 2, 4, 128), col, 3, keepdims=True)
+    panel_out = panel_out.reshape(4, 1, 128, 2, 1, 128)
+    notes = jnp.concatenate([landing, jnp.where(group < 8, 0, 1).astype(jnp.int32).reshape(1)])
+    return fin(notes, front, arrived, brow.reshape(512, 1024), bcol), panel_out
 
 
 def solution(mesh):
     return jax.shard_map(
-        finish,
+        local,
         mesh=mesh,
         in_specs=(
             P(None, ("sub", "row"), None, None, "col", None),

time: 398 us -> 263 us (0.66)
  the two profiles are of different devices: /device:TPU:1 before, /device:TPU:9 now
where the time goes in v3:
time: 263 us
  Pallas kernels  217 us (83%)
  waiting for transfers between devices  17.5 us (7%)
  starting transfers between devices  14.4 us (5%)
  local copies, waits for them, and re-layouts  10.2 us (4%)
    pallas_call x1, Pallas kernels, panel_exchange(): pl.pallas_call(panel_kernel, out_shape=(jax.ShapeDtypeStruct((4, 128, 102...  78.7 us
    pallas_call x1, Pallas kernels, chol(): pl.pallas_call(chol_kernel, out_shape=[jax.ShapeDtypeStruct((1024, 1024),...  72.5 us
    pallas_call x1, Pallas kernels, lead_gather(): pl.pallas_call(lead_kernel, out_shape=(jax.ShapeDtypeStruct((8, 8, 128, 1...  28.9 us
    pallas_call x1, Pallas kernels, fin(): pl.pallas_call(fin_kernel, out_shape=jax.ShapeDtypeStruct((4, 1, 128, 32,...  20.1 us
    all_to_all x1, waiting for transfers between devices, local(): lax.all_to_all(outgoing, ('sub', 'row', 'col'), split_axis=0, concat_axis...  17.5 us
    all_to_all x1, starting transfers between devices, local(): lax.all_to_all(outgoing, ('sub', 'row', 'col'), split_axis=0, concat_axis...  14.4 us
    pallas_call x1, Pallas kernels, head(): pl.pallas_call(head_kernel, out_shape=jax.ShapeDtypeStruct((2, 4, 128, 12...  9.12 us
    pallas_call x1, Pallas kernels, route(): pl.pallas_call(route_kernel, out_shape=jax.ShapeDtypeStruct((128, 2, 128,...  8.1 us
  transfers between devices with their start and end apart: 1, of which 1 were waited for; matrix products, arithmetic and copies ran while one was open for 1% of the time, Pallas kernels for 28%

profile of v3, /device:TPU:9, one launch (start us, length us, event | category | flops | bytes accessed | tf_op | source)
XLA Modules:
  0.0 262.8 jit_solution(17289695565509077215)
XLA Ops:
  0.6 1.2 add_bitcast_fusion.code_ref
  1.8 28.9 %lead.1 = (f32[8,8,128,128]{3,2,1,0:T(8,128)}, s32[4,4,8,1,128]{4,3,2,1,0:T(1,128)}) custom-call(f32[4,1,128,32,1,128]{5,4,3,2,1,0:T(1,128)} %front_ref.5, s32[1,128]{1,0:T(1,128)} %add_bitcast_fusion.code_ref), custom_call_target="tpu_custom_call" | custom-call | tf_op jit(solution)/shard_map/lead/pallas_call | solution.py:641
  30.7 8.1 %route.1 = bf16[128,2,128,128]{3,2,1,0:T(8,128)(2,1)} custom-call(s32[128]{0:T(128)} %bitcast.16, bf16[128,128,128]{2,1,0:T(8,128)(2,1)} %child_ref.1), custom_call_target="tpu_custom_call" | custom-call | tf_op jit(solution)/shard_map/route/pallas_call | solution.py:152
  38.8 0.0 copy-start.4
  38.8 14.4 %all-to-all-start = ((bf16[128,2,128,128]{3,2,1,0:T(8,128)(2,1)}), bf16[128,2,128,128]{3,2,1,0:T(8,128)(2,1)}, u32[]{:S(2)}, u32[]{:S(2)}) async-start(bf16[128,2,128,128]{3,2,1,0:T(8,128)(2,1)} %route.1), calls=%async_computation | async-start | bytes 16777216 | tf_op jit(solution)/shard_map/all_to_all | solution.py:673
  53.3 0.0 copy-done.4
  53.3 0.6 select_reduce_fusion
  53.9 0.1 copy.10
  54.0 0.1 reduce_min.12
  54.1 0.1 copy.9
  54.3 0.1 reduce_max.12
  54.4 0.1 copy.11
  54.5 0.1 reshape.177.land_ref
  54.7 0.0 copy-start
  54.7 2.2 copy-done
  56.9 0.0 copy-start.5
  56.9 72.5 %chol.1 = (bf16[1024,1024]{1,0:T(8,128)(2,1)S(1)}, bf16[1024,1024]{1,0:T(8,128)(2,1)S(1)}, bf16[1024,1024]{1,0:T(8,128)(2,1)S(1)}) custom-call(f32[8,8,128,128]{3,2,1,0:T(8,128)S(1)} %copy-done), custom_call_target="tpu_custom_call" | custom-call | tf_op jit(solution)/shard_map/chol/pallas_call | solution.py:112
  129.3 0.0 copy-start.1
  129.4 1.3 copy-done.1
  130.7 0.0 copy-start.2
  130.7 1.3 copy-done.2
  132.0 0.0 copy-start.3
  132.0 1.3 copy-done.3
  133.3 0.6 pad_add_fusion.land_ref
  133.9 17.5 %all-to-all-done = bf16[128,2,128,128]{3,2,1,0:T(8,128)(2,1)} async-done(((bf16[128,2,128,128]{3,2,1,0:T(8,128)(2,1)}), bf16[128,2,128,128]{3,2,1,0:T(8,128)(2,1)}, u32[]{:S(2)}, u32[]{:S(2)}) %all-to-all-start) | async-done | bytes 8388640 | tf_op jit(solution)/shard_map/all_to_all | solution.py:673
  151.4 0.0 copy-done.5
  151.4 9.1 %head.1.panel_ref = f32[2,4,128,128]{3,2,1,0:T(8,128)} custom-call(s32[256]{0:T(256)} %copy-done.5, f32[4,1,128,32,1,128]{5,4,3,2,1,0:T(1,128)} %front_ref.5, bf16[256,128,128]{2,1,0:T(8,128)(2,1)} %bitcast.6.arr_ref), custom_call_target="tpu_custom_call" | custom-call | tf_op jit(solution)/shard_map/head/pallas_call | solution.py:190
  160.5 78.7 %panel.1 = (bf16[4,128,1024]{2,1,0:T(8,128)(2,1)}, bf16[8,4,128,1024]{3,2,1,0:T(8,128)(2,1)}) custom-call(f32[2,4,128,128]{3,2,1,0:T(8,128)} %head.1.panel_ref, bf16[1024,1024]{1,0:T(8,128)(2,1)} %copy-done.2, bf16[1024,1024]{1,0:T(8,128)(2,1)} %copy-done.3, bf16[1024,1024]{1,0:T(8,128)(2,1)} %copy-done.1), custom_call_target="tpu_custom_call" | custom-call | tf_op jit(solution)/shard_map/panel/pallas_call | solution.py:461
  239.2 1.8 reshape.181
  241.0 0.5 constant_dynamic-slice_fusion
  241.6 1.0 copy.13
  242.6 20.1 %fin.1 = f32[4,1,128,32,1,128]{5,4,3,2,1,0:T(1,128)} custom-call(s32[257]{0:T(512)} %pad_add_fusion.land_ref, f32[4,1,128,32,1,128]{5,4,3,2,1,0:T(1,128)} %front_ref.5, bf16[256,128,128]{2,1,0:T(8,128)(2,1)} %bitcast.6.arr_ref, bf16[512,1024]{1,0:T(8,128)(2,1)} %bitcast.13, bf16[8,4,128,1024]{3,2,1,0:T(8,128)(2,1)} %get-tuple-element.19.bcol_ref), custom_call_target="tpu_custom_call" | custom-call | tf_op jit(solution)/shard_map/fin/pallas_call | solution.py:253
  (4 shorter events, 0.1 us)
Async XLA Ops:
  38.8 14.4 %copy-start.4 = (s32[4,4,8,1,128]{4,3,2,1,0:T(1,128)S(1)}, s32[4,4,8,1,128]{4,3,2,1,0:T(1,128)}, u32[]{:S(2)}) copy-start(s32[4,4,8,1,128]{4,3,2,1,0:T(1,128)} %get-tuple-element.11) | copy-start | bytes 196612
  38.8 112.6 %all-to-all-start = ((bf16[128,2,128,128]{3,2,1,0:T(8,128)(2,1)}), bf16[128,2,128,128]{3,2,1,0:T(8,128)(2,1)}, u32[]{:S(2)}, u32[]{:S(2)}) async-start(bf16[128,2,128,128]{3,2,1,0:T(8,128)(2,1)} %route.1), calls=%async_computation | async-start | bytes 16777216 | tf_op jit(solution)/shard_map/all_to_all | solution.py:673
  54.7 2.2 copy-start
  56.9 94.6 %copy-start.5 = (s32[256]{0:T(256)}, s32[256]{0:T(256)S(1)}, u32[]{:S(2)}) copy-start(s32[256]{0:T(256)S(1)} %reshape.177.land_ref) | copy-start | bytes 3076
  129.3 1.3 copy-start.1
  130.7 1.3 copy-start.2
  132.0 1.3 copy-start.3

commit v4 on v3

--- a/solution.py
+++ b/solution.py
@@ -162,46 +162,74 @@
     )(owner, child)
 
 
-def head_kernel(land_ref, front_ref, arr_ref, out_ref, buf_ref, acc_ref, fsem, asem):
-    def arrive(c):
-        return pltpu.make_async_copy(arr_ref.at[pl.ds(c * 32, 32)], buf_ref.at[c], asem.at[c])
+def plan_kernel(land_ref, list_ref):
+    def look(k, n):
+        slot = land_ref[k]
+        hit = (slot >= 0) & (lax.rem(lax.max(slot, 0), 32) < 2)
+        @pl.when(hit)
+        def _():
+            list_ref[n + 1] = k
+        return n + hit.astype(jnp.int32)
+    list_ref[0] = lax.fori_loop(0, 256, look, 0)
+
+
+def plan(land):
+    return pl.pallas_call(
+        plan_kernel,
+        out_shape=jax.ShapeDtypeStruct((264,), jnp.int32),
+        in_specs=[pl.BlockSpec(memory_space=pltpu.SMEM)],
+        out_specs=pl.BlockSpec(memory_space=pltpu.SMEM),
+        name="plan",
+    )(land)
+
+
+def head_kernel(land_ref, list_ref, front_ref, arr_ref, out_ref, buf_ref, acc_ref, fsem, asem):
+    count = list_ref[0]
+    def arrive(n, i):
+        return pltpu.make_async_copy(arr_ref.at[list_ref[n + 1]], buf_ref.at[i], asem.at[i])
     def fetch(s):
         return pltpu.make_async_copy(front_ref.at[:, 0, :, s, 0, :], acc_ref.at[s], fsem.at[s])
     for s in range(2):
         fetch(s).start()
-    for c in range(8):
-        arrive(c).start()
-    for s in range(2):
-        fetch(s).wait()
-    for c in range(8):
-        arrive(c).wait()
-        def add(k, carry):
-            slot = land_ref[c * 32 + k]
+    def batch(b, carry):
+        def begin(i, c):
+            arrive(b * 16 + i, i).start()
+            return c
+        def end(i, c):
+            n = b * 16 + i
+            slot = land_ref[list_ref[n + 1]]
             s, q = slot % 32, slot // 32
-            @pl.when((slot >= 0) & (s < 2))
-            def _():
-                acc_ref[s, q] = acc_ref[s, q] + buf_ref[c, k].astype(F32)
-            return carry
-        lax.fori_loop(0, 32, add, 0)
+            arrive(n, i).wait()
+            acc_ref[s, q] = acc_ref[s, q] + buf_ref[i].astype(F32)
+            return c
+        here = lax.min(count - b * 16, 16)
+        lax.fori_loop(0, here, begin, 0)
+        @pl.when(b == 0)
+        def _():
+            for s in range(2):
+                fetch(s).wait()
+        lax.fori_loop(0, here, end, 0)
+        return carry
+    lax.fori_loop(0, lax.max((count + 15) // 16, 1), batch, 0)
     out_ref[...] = acc_ref[...]
 
 
-def head(land, front, arrived):
+def head(land, listed, front, arrived):
     return pl.pallas_call(
         head_kernel,
         out_shape=jax.ShapeDtypeStruct((2, 4, 128, 128), F32),
         grid_spec=pltpu.PrefetchScalarGridSpec(
-            num_scalar_prefetch=1, grid=(1,),
+            num_scalar_prefetch=2, grid=(1,),
             in_specs=[pl.BlockSpec(memory_space=ANY)] * 2,
-            out_specs=pl.BlockSpec((2, 4, 128, 128), lambda g, a: (0, 0, 0, 0)),
-            scratch_shapes=[V((8, 32, 128, 128), BF), V((2, 4, 128, 128), F32),
-                            pltpu.SemaphoreType.DMA((2,)), pltpu.SemaphoreType.DMA((8,))]),
+            out_specs=pl.BlockSpec((2, 4, 128, 128), lambda g, a, b: (0, 0, 0, 0)),
+            scratch_shapes=[V((16, 128, 128), BF), V((2, 4, 128, 128), F32),
+                            pltpu.SemaphoreType.DMA((2,)), pltpu.SemaphoreType.DMA((16,))]),
         compiler_params=pltpu.CompilerParams(vmem_limit_bytes=60 << 20),
         name="head",
-    )(land, front, arrived)
-
-
-def fin_kernel(land_ref, front_ref, arr_ref, brow_ref, bcol_ref, out_ref, buf_ref, acc_ref, bc_ref, fsem, asem, bsem, osem):
+    )(land, listed, front, arrived)
+
+
+def fin_kernel(land_ref, front_ref, arr_ref, brow_ref, bcol_ref, out_ref, pout_ref, buf_ref, acc_ref, bc_ref, fsem, asem, bsem, osem):
     def arrive(c):
         return pltpu.make_async_copy(arr_ref.at[pl.ds(c * 32, 32)], buf_ref.at[c], asem.at[c])
     def fetch(s):
@@ -219,6 +247,9 @@
     for c in range(8):
         arrive(c).start()
     each(2, 32, lambda s: column(s).start())
+    for q in range(4):
+        pair = [brow_ref[q * 128:(q + 1) * 128, pl.ds(pl.multiple_of((4 * s + land_ref[257]) * 128, 128), 128)] for s in range(2)]
+        pout_ref[q] = jnp.stack([x.astype(F32) for x in pair], 1).astype(BF)
     each(0, 32, lambda s: fetch(s).wait())
     for c in range(8):
         arrive(c).wait()
@@ -252,12 +283,12 @@
     D = pltpu.SemaphoreType.DMA
     return pl.pallas_call(
         fin_kernel,
-        out_shape=jax.ShapeDtypeStruct((4, 1, 128, 32, 1, 128), F32),
+        out_shape=(jax.ShapeDtypeStruct((4, 1, 128, 32, 1, 128), F32), jax.ShapeDtypeStruct((4, 128, 2, 128), BF)),
         grid_spec=pltpu.PrefetchScalarGridSpec(
             num_scalar_prefetch=1, grid=(1,),
             in_specs=[pl.BlockSpec(memory_space=ANY)] * 2
             + [pl.BlockSpec((512, 1024), lambda g, a: (0, 0), pipeline_mode=pl.Buffered(1)), pl.BlockSpec(memory_space=ANY)],
-            out_specs=pl.BlockSpec(memory_space=ANY),
+            out_specs=(pl.BlockSpec(memory_space=ANY), pl.BlockSpec((4, 128, 2, 128), lambda g, a: (0, 0, 0, 0))),
             scratch_shapes=[V((8, 32, 128, 128), BF), V((32, 4, 128, 128), F32), V((4096, 1024), BF),
                             D((32,)), D((8,)), D((32,)), D((32,))]),
         compiler_params=pltpu.CompilerParams(vmem_limit_bytes=60 << 20),
@@ -369,28 +400,9 @@
             yfar(0).start()
             yfar(1).start()
 
-    for i in range(2):
-        xsend(i).start()
-    for i in range(2):
-        wsend(i).start()
-    ysend(row)
-    for i in range(2):
-        xrecv(i).wait_recv()
-        xforward(i, n4(row, -step[i])).start()
-        ysend(n4(row, -step[i]))
-    for i in range(2):
-        wrecv(i).wait_recv()
-        wforward(i, n4(col, -step[i])).start()
-    for i in range(2):
-        xforward(i, n4(row, 2)).wait_recv()
-    ysend(n4(row, 2))
-    for i in range(2):
-        yfar(i).wait_recv()
-        yrelay(i).start()
-
     def own(e, i):
         at = bcol_ref.at[sub, n4(col, e)]
-        return remote(at, at, zs.at[i, e], zr.at[i, e], sub=n8(sub, 2 * step[i]))
+        return remote(at if e else xb.at[col], at, zs.at[i, e], zr.at[i, e], sub=n8(sub, 2 * step[i]))
     def arrive(e, i):
         at = bcol_ref.at[n8(sub, -2 * step[i]), n4(col, e)]
         return remote(at, at, zs.at[i, e], zr.at[i, e], sub=n8(sub, 2 * step[i]))
@@ -400,7 +412,7 @@
         return remote(at, at, fs.at[e], fr.at[e], sub=n8(sub, 2 * step[side[e]]))
     def swap(e, k, z):
         at = bcol_ref.at[n8(sub, z), n4(col, e)]
-        return remote(at, at, ms.at[k, e], mr.at[k, e], sub=mate)
+        return remote(at if e or k else xb.at[col], at, ms.at[k, e], mr.at[k, e], sub=mate)
     def swapped(e, k, z):
         at = bcol_ref.at[n8(mate, z), n4(col, e)]
         return remote(at, at, ms.at[k, e], mr.at[k, e], sub=mate)
@@ -409,12 +421,44 @@
         own(e, 0).start()
         own(e, 1).start()
         swap(e, 0, 0).start()
-    home.wait()
-    launch(0)
-    ynear_in(1).wait_recv()
-    launch(1)
-    ynear_in(0).wait_recv()
-    launch(3)
+    apart = n4(col, -row)
+
+    def near():
+        ynear_in(1).wait_recv()
+        launch(1)
+        ynear_in(0).wait_recv()
+        launch(3)
+
+    def reach(d):
+        ysend(n4(row, d))
+        @pl.when(apart == d)
+        def _():
+            launch(0)
+
+    for i in range(2):
+        xsend(i).start()
+    for i in range(2):
+        wsend(i).start()
+    reach(0)
+    for i in range(2):
+        xrecv(i).wait_recv()
+        xforward(i, n4(row, -step[i])).start()
+        reach(3 if i == 0 else 1)
+    for i in range(2):
+        wrecv(i).wait_recv()
+        wforward(i, n4(col, -step[i])).start()
+    @pl.when(apart == 0)
+    def _():
+        near()
+    for i in range(2):
+        xforward(i, n4(row, 2)).wait_recv()
+    reach(2)
+    for i in range(2):
+        yfar(i).wait_recv()
+        yrelay(i).start()
+    @pl.when(apart != 0)
+    def _():
+        near()
     yfar_in(0).wait_recv()
     yfar_in(1).wait_recv()
     launch(2)
@@ -435,6 +479,8 @@
     for i in range(2):
         wforward(i, n4(col, 2)).wait_recv()
 
+    home.wait()
+
     for d in (1, 2, 3):
         take(d).wait_send()
     for i in range(2):
@@ -674,12 +720,12 @@
     arrived = arrived.reshape(256, 128, 128)
     factor, hi, lo = chol(lead)
     landing = landings(codes, group * 4 + col)
-    panel = head(landing, front, arrived)
+    listed = plan(landing)
+    panel = head(landing, listed, front, arrived)
     brow, bcol = panel_exchange(panel, hi, lo, factor)
-    panel_out = lax.dynamic_index_in_dim(brow.reshape(4, 128, 2, 4, 128), col, 3, keepdims=True)
-    panel_out = panel_out.reshape(4, 1, 128, 2, 1, 128)
-    notes = jnp.concatenate([landing, jnp.where(group < 8, 0, 1).astype(jnp.int32).reshape(1)])
-    return fin(notes, front, arrived, brow.reshape(512, 1024), bcol), panel_out
+    extra = jnp.stack([jnp.where(group < 8, 0, 1), col]).astype(jnp.int32)
+    out, panel_out = fin(jnp.concatenate([landing, extra]), front, arrived, brow.reshape(512, 1024), bcol)
+    return out, panel_out.reshape(4, 1, 128, 2, 1, 128)
 
 
 def solution(mesh):

time: 263 us -> 249 us (0.947)
  the two profiles are of different devices: /device:TPU:9 before, /device:TPU:16 now
where the time goes in v4:
time: 249 us; the launch traced here: 248 us
  Pallas kernels  207 us (83%)
  starting transfers between devices  16.6 us (7%)
  waiting for transfers between devices  12.7 us (5%)
  local copies, waits for them, and re-layouts  7.44 us (3%)
  other arithmetic  3.19 us (1%)
    pallas_call x1, Pallas kernels, chol(): pl.pallas_call(chol_kernel, out_shape=[jax.ShapeDtypeStruct((1024, 1024),...  72.5 us
    pallas_call x1, Pallas kernels, panel_exchange(): pl.pallas_call(panel_kernel, out_shape=(jax.ShapeDtypeStruct((4, 128, 102...  69.5 us
    pallas_call x1, Pallas kernels, lead_gather(): pl.pallas_call(lead_kernel, out_shape=(jax.ShapeDtypeStruct((8, 8, 128, 1...  26.4 us
    pallas_call x1, Pallas kernels, fin(): pl.pallas_call(fin_kernel, out_shape=(jax.ShapeDtypeStruct((4, 1, 128, 32...  22.3 us
    all_to_all x1, starting transfers between devices, local(): lax.all_to_all(outgoing, ('sub', 'row', 'col'), split_axis=0, concat_axis...  16.6 us
    all_to_all x1, waiting for transfers between devices, local(): lax.all_to_all(outgoing, ('sub', 'row', 'col'), split_axis=0, concat_axis...  12.7 us
    pallas_call x1, Pallas kernels, route(): pl.pallas_call(route_kernel, out_shape=jax.ShapeDtypeStruct((128, 2, 128,...  8.1 us
    unnamed x10, local copies, waits for them, and re-layouts  6.15 us
  transfers between devices with their start and end apart: 1, of which 1 were waited for; matrix products, arithmetic and copies ran while one was open for 1% of the time, Pallas kernels for 31%

profile of v4, /device:TPU:16, one launch (start us, length us, event | category | flops | bytes accessed | tf_op | source)
XLA Modules:
  0.0 248.2 jit_solution(14458120946042852368)
XLA Ops:
  0.6 1.2 add_bitcast_fusion.code_ref
  1.8 26.4 %lead.1 = (f32[8,8,128,128]{3,2,1,0:T(8,128)}, s32[4,4,8,1,128]{4,3,2,1,0:T(1,128)}) custom-call(f32[4,1,128,32,1,128]{5,4,3,2,1,0:T(1,128)} %front_ref.5, s32[1,128]{1,0:T(1,128)} %add_bitcast_fusion.code_ref), custom_call_target="tpu_custom_call" | custom-call | tf_op jit(solution)/shard_map/lead/pallas_call | solution.py:687
  28.2 8.1 %route.1 = bf16[128,2,128,128]{3,2,1,0:T(8,128)(2,1)} custom-call(s32[128]{0:T(128)} %bitcast.16, bf16[128,128,128]{2,1,0:T(8,128)(2,1)} %child_ref.1), custom_call_target="tpu_custom_call" | custom-call | tf_op jit(solution)/shard_map/route/pallas_call | solution.py:152
  36.3 0.0 copy-start.4
  36.3 16.6 %all-to-all-start = ((bf16[128,2,128,128]{3,2,1,0:T(8,128)(2,1)}), bf16[128,2,128,128]{3,2,1,0:T(8,128)(2,1)}, u32[]{:S(2)}, u32[]{:S(2)}) async-start(bf16[128,2,128,128]{3,2,1,0:T(8,128)(2,1)} %route.1), calls=%async_computation | async-start | bytes 16777216 | tf_op jit(solution)/shard_map/all_to_all | solution.py:719
  52.9 0.0 copy-done.4
  52.9 0.6 select_reduce_fusion
  53.5 0.1 copy.10
  53.6 0.1 reduce_min.12
  53.8 0.1 copy.9
  53.9 0.1 reduce_max.12
  54.0 0.1 copy.11
  54.1 0.7 reshape.171.land_ref
  54.9 4.6 %plan.1.list_ref = s32[264]{0:T(512)} custom-call(s32[256]{0:T(256)} %reshape.171.land_ref), custom_call_target="tpu_custom_call" | custom-call | tf_op jit(solution)/shard_map/plan/pallas_call | solution.py:177
  59.5 0.0 copy-start
  59.5 2.2 copy-done
  61.7 72.5 %chol.1 = (bf16[1024,1024]{1,0:T(8,128)(2,1)S(1)}, bf16[1024,1024]{1,0:T(8,128)(2,1)S(1)}, bf16[1024,1024]{1,0:T(8,128)(2,1)S(1)}) custom-call(f32[8,8,128,128]{3,2,1,0:T(8,128)S(1)} %copy-done), custom_call_target="tpu_custom_call" | custom-call | tf_op jit(solution)/shard_map/chol/pallas_call | solution.py:112
  134.2 0.0 copy-start.1
  134.2 1.3 copy-done.1
  135.5 0.0 copy-start.2
  135.5 1.3 copy-done.2
  136.8 0.0 copy-start.3
  136.8 1.3 copy-done.3
  138.1 1.3 pad_add_fusion.land_ref
  139.5 12.7 %all-to-all-done = bf16[128,2,128,128]{3,2,1,0:T(8,128)(2,1)} async-done(((bf16[128,2,128,128]{3,2,1,0:T(8,128)(2,1)}), bf16[128,2,128,128]{3,2,1,0:T(8,128)(2,1)}, u32[]{:S(2)}, u32[]{:S(2)}) %all-to-all-start) | async-done | bytes 8388640 | tf_op jit(solution)/shard_map/all_to_all | solution.py:719
  152.2 4.0 %head.1.panel_ref = f32[2,4,128,128]{3,2,1,0:T(8,128)} custom-call(s32[256]{0:T(256)} %reshape.171.land_ref, s32[264]{0:T(512)} %plan.1.list_ref, f32[4,1,128,32,1,128]{5,4,3,2,1,0:T(1,128)} %front_ref.5, bf16[256,128,128]{2,1,0:T(8,128)(2,1)} %bitcast.7.arr_ref), custom_call_target="tpu_custom_call" | custom-call | tf_op jit(solution)/shard_map/head/pallas_call | solution.py:218
  156.1 69.5 %panel.1 = (bf16[4,128,1024]{2,1,0:T(8,128)(2,1)}, bf16[8,4,128,1024]{3,2,1,0:T(8,128)(2,1)}) custom-call(f32[2,4,128,128]{3,2,1,0:T(8,128)} %head.1.panel_ref, bf16[1024,1024]{1,0:T(8,128)(2,1)} %copy-done.2, bf16[1024,1024]{1,0:T(8,128)(2,1)} %copy-done.3, bf16[1024,1024]{1,0:T(8,128)(2,1)} %copy-done.1), custom_call_target="tpu_custom_call" | custom-call | tf_op jit(solution)/shard_map/panel/pallas_call | solution.py:507
  225.7 22.3 %fin.1 = (f32[4,1,128,32,1,128]{5,4,3,2,1,0:T(1,128)}, bf16[4,128,2,128]{3,2,1,0:T(2,128)(2,1)}) custom-call(s32[258]{0:T(512)} %pad_add_fusion.land_ref, f32[4,1,128,32,1,128]{5,4,3,2,1,0:T(1,128)} %front_ref.5, bf16[256,128,128]{2,1,0:T(8,128)(2,1)} %bitcast.7.arr_ref, bf16[512,1024]{1,0:T(8,128)(2,1)} %bitcast.14, ...), custom_call_target="tpu_custom_call" | custom-call | tf_op jit(solution)/shard_map/fin/pallas_call | solution.py:284
  (3 shorter events, 0.0 us)
Async XLA Ops:
  36.3 16.6 %copy-start.4 = (s32[4,4,8,1,128]{4,3,2,1,0:T(1,128)S(1)}, s32[4,4,8,1,128]{4,3,2,1,0:T(1,128)}, u32[]{:S(2)}) copy-start(s32[4,4,8,1,128]{4,3,2,1,0:T(1,128)} %get-tuple-element.13) | copy-start | bytes 196612
  36.3 115.9 %all-to-all-start = ((bf16[128,2,128,128]{3,2,1,0:T(8,128)(2,1)}), bf16[128,2,128,128]{3,2,1,0:T(8,128)(2,1)}, u32[]{:S(2)}, u32[]{:S(2)}) async-start(bf16[128,2,128,128]{3,2,1,0:T(8,128)(2,1)} %route.1), calls=%async_computation | async-start | bytes 16777216 | tf_op jit(solution)/shard_map/all_to_all | solution.py:719
  59.5 2.2 copy-start
  134.2 1.3 copy-start.1
  135.5 1.3 copy-start.2
  136.8 1.3 copy-start.3

commit v5 on v4

--- a/solution.py
+++ b/solution.py
@@ -162,9 +162,19 @@
     )(owner, child)
 
 
-def plan_kernel(land_ref, list_ref):
+def plan_kernel(land_ref, list_ref, order_ref, cnt_ref, pos_ref):
+    def clear(k, c):
+        cnt_ref[k] = 0
+        for u in range(4):
+            order_ref[4 * k + u] = 0
+        return c
+    lax.fori_loop(0, 128, clear, 0)
+
     def look(k, n):
         slot = land_ref[k]
+        @pl.when(slot >= 0)
+        def _():
+            cnt_ref[slot] = cnt_ref[slot] + 1
         hit = (slot >= 0) & (lax.rem(lax.max(slot, 0), 32) < 2)
         @pl.when(hit)
         def _():
@@ -172,13 +182,35 @@
         return n + hit.astype(jnp.int32)
     list_ref[0] = lax.fori_loop(0, 256, look, 0)
 
+    def bounds(j, n):
+        here = cnt_ref[j]
+        pos_ref[j] = n
+        order_ref[512 + j] = lax.max(n + here - 1, 0)
+        order_ref[640 + j] = lax.min(here, 1)
+        cnt_ref[j] = 0
+        return n + here
+    lax.fori_loop(0, 128, bounds, 0)
+
+    def place(k, c):
+        slot = land_ref[k]
+        @pl.when(slot >= 0)
+        def _():
+            p = pos_ref[slot]
+            order_ref[p] = k
+            order_ref[256 + p] = cnt_ref[slot]
+            cnt_ref[slot] = 1
+            pos_ref[slot] = p + 1
+        return c
+    lax.fori_loop(0, 256, place, 0)
+
 
 def plan(land):
     return pl.pallas_call(
         plan_kernel,
-        out_shape=jax.ShapeDtypeStruct((264,), jnp.int32),
+        out_shape=(jax.ShapeDtypeStruct((264,), jnp.int32), jax.ShapeDtypeStruct((768,), jnp.int32)),
         in_specs=[pl.BlockSpec(memory_space=pltpu.SMEM)],
-        out_specs=pl.BlockSpec(memory_space=pltpu.SMEM),
+        out_specs=(pl.BlockSpec(memory_space=pltpu.SMEM),) * 2,
+        scratch_shapes=[pltpu.SMEM((128,), jnp.int32)] * 2,
         name="plan",
     )(land)
 
@@ -229,75 +261,8 @@
     )(land, listed, front, arrived)
 
 
-def fin_kernel(land_ref, front_ref, arr_ref, brow_ref, bcol_ref, out_ref, pout_ref, buf_ref, acc_ref, bc_ref, fsem, asem, bsem, osem):
-    def arrive(c):
-        return pltpu.make_async_copy(arr_ref.at[pl.ds(c * 32, 32)], buf_ref.at[c], asem.at[c])
-    def fetch(s):
-        return pltpu.make_async_copy(front_ref.at[:, 0, :, s, 0, :], acc_ref.at[s], fsem.at[s])
-    def column(s):
-        return pltpu.make_async_copy(bcol_ref.at[s % 8, s // 8], bc_ref.at[pl.ds(s * 128, 128)], bsem.at[s])
-    def put(s):
-        return pltpu.make_async_copy(acc_ref.at[s], out_ref.at[:, 0, :, s, 0, :], osem.at[s])
-    def each(low, high, f):
-        def go(s, c):
-            f(s)
-            return c
-        lax.fori_loop(low, high, go, 0)
-    each(0, 32, lambda s: fetch(s).start())
-    for c in range(8):
-        arrive(c).start()
-    each(2, 32, lambda s: column(s).start())
-    for q in range(4):
-        pair = [brow_ref[q * 128:(q + 1) * 128, pl.ds(pl.multiple_of((4 * s + land_ref[257]) * 128, 128), 128)] for s in range(2)]
-        pout_ref[q] = jnp.stack([x.astype(F32) for x in pair], 1).astype(BF)
-    each(0, 32, lambda s: fetch(s).wait())
-    for c in range(8):
-        arrive(c).wait()
-        def add(k, carry):
-            slot = land_ref[c * 32 + k]
-            @pl.when(slot >= 0)
-            def _():
-                s, q = slot % 32, slot // 32
-                acc_ref[s, q] = acc_ref[s, q] + buf_ref[c, k].astype(F32)
-            return carry
-        lax.fori_loop(0, 32, add, 0)
-    for s in range(2):
-        put(s).start()
-    def update(g, carry):
-        s = 2 * g
-        column(s).wait()
-        column(s + 1).wait()
-        y = lax.dot_general(brow_ref[...], bc_ref[pl.ds(pl.multiple_of(g * 256, 256), 256), :],
-                            (((1,), (1,)), ((), ())), preferred_element_type=F32)
-        for u in range(2):
-            z = y[:, u * 128:(u + 1) * 128].reshape(4, 128, 128)
-            acc_ref[s + u, 0] = acc_ref[s + u, 0] - jnp.where(land_ref[256] > 0, z[0], 0.0)
-            acc_ref[s + u, 1:4] = acc_ref[s + u, 1:4] - z[1:4]
-            put(s + u).start()
-        return carry
-    lax.fori_loop(1, 16, update, 0)
-    each(0, 32, lambda s: put(s).wait())
-
-
-def fin(land, front, arrived, brow, bcol):
-    D = pltpu.SemaphoreType.DMA
-    return pl.pallas_call(
-        fin_kernel,
-        out_shape=(jax.ShapeDtypeStruct((4, 1, 128, 32, 1, 128), F32), jax.ShapeDtypeStruct((4, 128, 2, 128), BF)),
-        grid_spec=pltpu.PrefetchScalarGridSpec(
-            num_scalar_prefetch=1, grid=(1,),
-            in_specs=[pl.BlockSpec(memory_space=ANY)] * 2
-            + [pl.BlockSpec((512, 1024), lambda g, a: (0, 0), pipeline_mode=pl.Buffered(1)), pl.BlockSpec(memory_space=ANY)],
-            out_specs=(pl.BlockSpec(memory_space=ANY), pl.BlockSpec((4, 128, 2, 128), lambda g, a: (0, 0, 0, 0))),
-            scratch_shapes=[V((8, 32, 128, 128), BF), V((32, 4, 128, 128), F32), V((4096, 1024), BF),
-                            D((32,)), D((8,)), D((32,)), D((32,))]),
-        compiler_params=pltpu.CompilerParams(vmem_limit_bytes=60 << 20),
-        name="fin",
-    )(land, front, arrived, brow, bcol)
-
-
-def panel_kernel(panel_ref, hi_hbm, lo_hbm, low_hbm, brow_ref, bcol_ref, arow, ah, al, hi, lo, low, xb, rl,
-                 lsem, ps, pr, xs, xr, ws, wr, ys, yr, rs, rr, zs, zr, fs, fr, ms, mr):
+def panel_kernel(order_ref, panel_ref, hi_hbm, lo_hbm, low_hbm, front_ref, arr_ref, out_ref, pout_ref,
+                 brow_ref, bcol_ref, acc_ref, buf_ref, run_ref, arow, ah, al, hi, lo, low, xb, rl, fsem, asem, osem, lsem, ps, pr, xs, xr, ws, wr, ys, yr, rs, rr, zs, zr, fs, fr, ms, mr):
     sub, row, col = lax.axis_index("sub"), lax.axis_index("row"), lax.axis_index("col")
     group = 4 * sub + row
     mate = sub + 1 - 2 * lax.rem(sub, 2)
@@ -325,12 +290,28 @@
         copy.start()
     pl.semaphore_wait(barrier, 8)
 
+    def fetch(s):
+        return pltpu.make_async_copy(front_ref.at[:, 0, :, s, 0, :], acc_ref.at[s], fsem.at[s])
+    def arrived(c):
+        return pltpu.make_async_copy(arr_ref.at[pl.ds(c * 32, 32)], buf_ref.at[pl.ds(c * 32, 32)], asem.at[c])
+    def put(s):
+        return pltpu.make_async_copy(acc_ref.at[s], out_ref.at[:, 0, :, s, 0, :], osem.at[s])
+    def early(s):
+        return pltpu.make_async_copy(panel_ref.at[s], out_ref.at[:, 0, :, s, 0, :], osem.at[s])
+    def each(low, high, f):
+        def go(s, c):
+            f(s)
+            return c
+        lax.fori_loop(low, high, go, 0)
+
     def take(d):
         return remote(panel_ref.at[:, n4(col, d)], arow.at[col], ps.at[d - 1], pr.at[d - 1], col=n4(col, d))
     def taken(d):
         return remote(panel_ref.at[:, n4(col, d)], arow.at[n4(col, -d)], ps.at[d - 1], pr.at[d - 1], col=n4(col, d))
     for d in (1, 3, 2):
         take(d).start()
+    each(0, 8, lambda c: arrived(c).start())
+    each(2, 32, lambda s: fetch(s).start())
     loads[3].wait()
     for d in (1, 3, 2):
         taken(d).wait_recv()
@@ -375,16 +356,16 @@
         return remote(at, at, ws.at[2 + i], wr.at[2 + i], col=n4(col, step[i]))
 
     def ynear(i):
-        return remote(xb.at[n4(col, step[i])], bcol_ref.at[sub, col], ys.at[i], yr.at[i], col=n4(col, step[i]))
+        return remote(xb.at[n4(col, step[i])], bcol_ref.at[col, sub], ys.at[i], yr.at[i], col=n4(col, step[i]))
     def ynear_in(i):
-        return remote(xb.at[0], bcol_ref.at[sub, n4(col, -step[i])], ys.at[i], yr.at[i], col=n4(col, step[i]))
+        return remote(xb.at[0], bcol_ref.at[n4(col, -step[i]), sub], ys.at[i], yr.at[i], col=n4(col, step[i]))
     def yfar(i):
         return remote(xb.at[n4(col, 2), half[i]], rl.at[i], rs.at[i], rr.at[i], col=n4(col, step[i]))
     def yrelay(i):
-        return remote(rl.at[i], bcol_ref.at[sub, n4(col, -step[i]), half[i]], ys.at[2 + i], yr.at[2 + i], col=n4(col, step[i]))
+        return remote(rl.at[i], bcol_ref.at[n4(col, -step[i]), sub, half[i]], ys.at[2 + i], yr.at[2 + i], col=n4(col, step[i]))
     def yfar_in(i):
-        return remote(rl.at[i], bcol_ref.at[sub, n4(col, 2), half[i]], ys.at[2 + i], yr.at[2 + i], col=n4(col, step[i]))
-    home = pltpu.make_async_copy(xb.at[col], bcol_ref.at[sub, col], lsem.at[4])
+        return remote(rl.at[i], bcol_ref.at[n4(col, 2), sub, half[i]], ys.at[2 + i], yr.at[2 + i], col=n4(col, step[i]))
+    home = pltpu.make_async_copy(xb.at[col], bcol_ref.at[col, sub], lsem.at[4])
 
     def ysend(c):
         d = n4(c, -col)
@@ -401,20 +382,20 @@
             yfar(1).start()
 
     def own(e, i):
-        at = bcol_ref.at[sub, n4(col, e)]
+        at = bcol_ref.at[n4(col, e), sub]
         return remote(at if e else xb.at[col], at, zs.at[i, e], zr.at[i, e], sub=n8(sub, 2 * step[i]))
     def arrive(e, i):
-        at = bcol_ref.at[n8(sub, -2 * step[i]), n4(col, e)]
+        at = bcol_ref.at[n4(col, e), n8(sub, -2 * step[i])]
         return remote(at, at, zs.at[i, e], zr.at[i, e], sub=n8(sub, 2 * step[i]))
     side = [0, 0, 1, 1]
-    def onward(e, z):
-        at = bcol_ref.at[n8(sub, z), n4(col, e)]
-        return remote(at, at, fs.at[e], fr.at[e], sub=n8(sub, 2 * step[side[e]]))
+    def onward(e, i, z):
+        at = bcol_ref.at[n4(col, e), n8(sub, z)]
+        return remote(at, at, fs.at[e], fr.at[e], sub=n8(sub, 2 * step[i]))
     def swap(e, k, z):
-        at = bcol_ref.at[n8(sub, z), n4(col, e)]
-        return remote(at if e or k else xb.at[col], at, ms.at[k, e], mr.at[k, e], sub=mate)
+        at = bcol_ref.at[n4(col, e), n8(sub, z)]
+        return remote(at if k or e else xb.at[col], at, ms.at[k, e], mr.at[k, e], sub=mate)
     def swapped(e, k, z):
-        at = bcol_ref.at[n8(mate, z), n4(col, e)]
+        at = bcol_ref.at[n4(col, e), n8(mate, z)]
         return remote(at, at, ms.at[k, e], mr.at[k, e], sub=mate)
 
     def launch(e):
@@ -423,6 +404,35 @@
         swap(e, 0, 0).start()
     apart = n4(col, -row)
 
+    def gather(c):
+        def go(k, total):
+            i = c * 32 + k
+            total = buf_ref[order_ref[i]].astype(F32) + order_ref[256 + i].astype(F32) * total
+            run_ref[i] = total
+            return total
+        first = jnp.zeros((128, 128), F32) if c == 0 else run_ref[c * 32 - 1]
+        lax.fori_loop(0, 32, go, first)
+
+    def settle(s):
+        for q in range(4):
+            slot = q * 32 + s
+            acc_ref[s, q] = acc_ref[s, q] + order_ref[640 + slot].astype(F32) * run_ref[order_ref[512 + slot]]
+
+    keep = jnp.where(group < 8, 0.0, 1.0)
+    pair0 = sub - lax.rem(sub, 2)
+
+    def update(e, dz):
+        q, z = n4(col, e), n8(pair0, dz)
+        s = q * 8 + z
+        @pl.when(s >= 2)
+        def _():
+            y = mm(brow_ref[...].reshape(512, 1024), bcol_ref[q, pl.ds(z, 2)].reshape(256, 1024))
+            for u in range(2):
+                t = y[:, u * 128:(u + 1) * 128].reshape(4, 128, 128)
+                acc_ref[s + u, 0] = acc_ref[s + u, 0] - keep * t[0]
+                acc_ref[s + u, 1:4] = acc_ref[s + u, 1:4] - t[1:4]
+                put(s + u).start()
+
     def near():
         ynear_in(1).wait_recv()
         launch(1)
@@ -440,6 +450,11 @@
     for i in range(2):
         wsend(i).start()
     reach(0)
+    early(0).start()
+    early(1).start()
+    each(0, 8, lambda c: arrived(c).wait())
+    for c in range(5):
+        gather(c)
     for i in range(2):
         xrecv(i).wait_recv()
         xforward(i, n4(row, -step[i])).start()
@@ -450,9 +465,13 @@
     @pl.when(apart == 0)
     def _():
         near()
+    for c in range(5, 8):
+        gather(c)
     for i in range(2):
         xforward(i, n4(row, 2)).wait_recv()
     reach(2)
+    each(2, 32, lambda s: fetch(s).wait())
+    each(2, 12, settle)
     for i in range(2):
         yfar(i).wait_recv()
         yrelay(i).start()
@@ -462,24 +481,51 @@
     yfar_in(0).wait_recv()
     yfar_in(1).wait_recv()
     launch(2)
-    for e in (0, 1, 3, 2):
+    for i in range(2):
+        wforward(i, n4(col, 2)).wait_recv()
+    each(12, 32, settle)
+    for q in range(4):
+        pair = [brow_ref[q, :, pl.ds(pl.multiple_of((4 * s + col) * 128, 128), 128)] for s in range(2)]
+        pout_ref[q] = jnp.stack([x.astype(F32) for x in pair], 1).astype(BF)
+    home.wait()
+
+    def gray(k):
+        return k + jnp.where(k == 2, 1, 0) - jnp.where(k == 3, 1, 0)
+
+    def pass_on(k, carry):
+        e = gray(k)
         for i in range(2):
             arrive(e, i).wait_recv()
-            if side[e] == i:
-                onward(e, -2 * step[i]).start()
+            @pl.when((e < 2) if i == 0 else (e >= 2))
+            def _():
+                onward(e, i, -2 * step[i]).start()
             swap(e, 1 + i, -2 * step[i]).start()
-    for e in (0, 1, 3, 2):
-        onward(e, 4).wait_recv()
+        swapped(e, 0, 0).wait_recv()
+        update(e, 0)
+        return carry
+    lax.fori_loop(0, 4, pass_on, 0)
+
+    def last(k, carry):
+        e = gray(k)
+        onward(e, 0, 4).wait_recv()
         swap(e, 3, 4).start()
-    for e in range(4):
-        swapped(e, 0, 0).wait_recv()
-        swapped(e, 1, -2).wait_recv()
-        swapped(e, 2, 2).wait_recv()
+        def sides(j, c):
+            swapped(e, 1 + j, 4 * j - 2).wait_recv()
+            update(e, 4 * j - 2)
+            return c
+        lax.fori_loop(0, 2, sides, 0)
+        return carry
+    lax.fori_loop(0, 4, last, 0)
+
+    def far(k, carry):
+        e = gray(k)
         swapped(e, 3, 4).wait_recv()
-    for i in range(2):
-        wforward(i, n4(col, 2)).wait_recv()
-
-    home.wait()
+        update(e, 4)
+        return carry
+    lax.fori_loop(0, 4, far, 0)
+    early(0).wait()
+    early(1).wait()
+    each(2, 32, lambda s: put(s).wait())
 
     for d in (1, 2, 3):
         take(d).wait_send()
@@ -494,28 +540,30 @@
     for e in range(4):
         own(e, 0).wait_send()
         own(e, 1).wait_send()
-        onward(e, -2 * step[side[e]]).wait_send()
+        onward(e, side[e], -2 * step[side[e]]).wait_send()
         swap(e, 0, 0).wait_send()
         swap(e, 1, -2).wait_send()
         swap(e, 2, 2).wait_send()
         swap(e, 3, 4).wait_send()
 
 
-def panel_exchange(panel, hi, lo, low):
+def panel_exchange(order, panel, hi, lo, low, front, arrived):
     D = pltpu.SemaphoreType.DMA
     H = pltpu.HBM
     return pl.pallas_call(
         panel_kernel,
-        out_shape=(jax.ShapeDtypeStruct((4, 128, 1024), BF), jax.ShapeDtypeStruct((8, 4, 128, 1024), BF)),
-        in_specs=[pl.BlockSpec(memory_space=V)] + [pl.BlockSpec(memory_space=H)] * 3,
-        out_specs=(pl.BlockSpec(memory_space=V), pl.BlockSpec(memory_space=H)),
-        scratch_shapes=[V((4, 2, 128, 128), F32), V((128, 1024), BF), V((128, 1024), BF), V((1024, 1024), BF), V((1024, 1024), BF),
-                        V((128, 1024), BF), V((4, 128, 1024), BF), V((2, 64, 1024), BF),
+        out_shape=(jax.ShapeDtypeStruct((4, 1, 128, 32, 1, 128), F32), jax.ShapeDtypeStruct((4, 128, 2, 128), BF)),
+        in_specs=[pl.BlockSpec(memory_space=pltpu.SMEM), pl.BlockSpec(memory_space=V)] + [pl.BlockSpec(memory_space=H)] * 5,
+        out_specs=(pl.BlockSpec(memory_space=H), pl.BlockSpec(memory_space=V)),
+        scratch_shapes=[V((4, 128, 1024), BF), V((4, 8, 128, 1024), BF), V((32, 4, 128, 128), F32), V((256, 128, 128), BF),
+                        V((256, 128, 128), F32), V((4, 2, 128, 128), F32), V((128, 1024), BF), V((128, 1024), BF),
+                        V((1024, 1024), BF), V((1024, 1024), BF),
+                        V((128, 1024), BF), V((4, 128, 1024), BF), V((2, 64, 1024), BF), D((32,)), D((8,)), D((32,)),
                         D((5,)), D((3,)), D((3,)), D((4,)), D((4,)), D((4,)), D((4,)), D((4,)), D((4,)), D((2,)), D((2,)),
                         D((2, 4)), D((2, 4)), D((4,)), D((4,)), D((4, 4)), D((4, 4))],
         compiler_params=pltpu.CompilerParams(vmem_limit_bytes=60 << 20, collective_id=2, has_side_effects=True),
         name="panel",
-    )(panel, hi, lo, low)
+    )(order, panel, hi, lo, low, front, arrived)
 
 
 def lead_kernel(front_ref, code_ref, lead_ref, codes_ref, own_ref, lsem, zs, zr, zls, zlr, xs, xr, ys, yr, as_, ar, bs, br, cs, cr):
@@ -720,11 +768,9 @@
     arrived = arrived.reshape(256, 128, 128)
     factor, hi, lo = chol(lead)
     landing = landings(codes, group * 4 + col)
-    listed = plan(landing)
+    listed, order = plan(landing)
     panel = head(landing, listed, front, arrived)
-    brow, bcol = panel_exchange(panel, hi, lo, factor)
-    extra = jnp.stack([jnp.where(group < 8, 0, 1), col]).astype(jnp.int32)
-    out, panel_out = fin(jnp.concatenate([landing, extra]), front, arrived, brow.reshape(512, 1024), bcol)
+    out, panel_out = panel_exchange(order, panel, hi, lo, factor, front, arrived)
     return out, panel_out.reshape(4, 1, 128, 2, 1, 128)
 
 

time: 249 us -> 238 us (0.956)
  the two profiles are of different devices: /device:TPU:16 before, /device:TPU:26 now
where the time goes in v5:
time: 238 us; the launch traced here: 237 us
  Pallas kernels  198 us (83%)
  local copies, waits for them, and re-layouts  15.1 us (6%)
  starting transfers between devices  14.5 us (6%)
  waiting for transfers between devices  7.51 us (3%)
    pallas_call x1, Pallas kernels, panel_exchange(): pl.pallas_call(panel_kernel, out_shape=(jax.ShapeDtypeStruct((4, 1, 128,...  74.7 us
    pallas_call x1, Pallas kernels, chol(): pl.pallas_call(chol_kernel, out_shape=[jax.ShapeDtypeStruct((1024, 1024),...  72.5 us
    pallas_call x1, Pallas kernels, lead_gather(): pl.pallas_call(lead_kernel, out_shape=(jax.ShapeDtypeStruct((8, 8, 128, 1...  28.4 us
    all_to_all x1, starting transfers between devices, local(): lax.all_to_all(outgoing, ('sub', 'row', 'col'), split_axis=0, concat_axis...  14.5 us
    unnamed x14, local copies, waits for them, and re-layouts  13.8 us
    pallas_call x1, Pallas kernels, plan(): pl.pallas_call(plan_kernel, out_shape=(jax.ShapeDtypeStruct((264,), jnp.i...  11.4 us
    pallas_call x1, Pallas kernels, route(): pl.pallas_call(route_kernel, out_shape=jax.ShapeDtypeStruct((128, 2, 128,...  8.1 us
    all_to_all x1, waiting for transfers between devices, local(): lax.all_to_all(outgoing, ('sub', 'row', 'col'), split_axis=0, concat_axis...  7.51 us
  transfers between devices with their start and end apart: 1, of which 1 were waited for; matrix products, arithmetic and copies ran while one was open for 1% of the time, Pallas kernels for 35%

profile of v5, /device:TPU:26, one launch (start us, length us, event | category | flops | bytes accessed | tf_op | source)
XLA Modules:
  0.0 237.5 jit_solution(15676214160145968915)
XLA Ops:
  0.6 1.2 add_bitcast_fusion.code_ref
  1.8 28.4 %lead.1 = (f32[8,8,128,128]{3,2,1,0:T(8,128)}, s32[4,4,8,1,128]{4,3,2,1,0:T(1,128)}) custom-call(f32[4,1,128,32,1,128]{5,4,3,2,1,0:T(1,128)} %front_ref.5, s32[1,128]{1,0:T(1,128)} %add_bitcast_fusion.code_ref), custom_call_target="tpu_custom_call" | custom-call | tf_op jit(solution)/shard_map/lead/pallas_call | solution.py:735
  30.2 8.1 %route.1 = bf16[128,2,128,128]{3,2,1,0:T(8,128)(2,1)} custom-call(s32[128]{0:T(128)} %bitcast.13, bf16[128,128,128]{2,1,0:T(8,128)(2,1)} %child_ref.1), custom_call_target="tpu_custom_call" | custom-call | tf_op jit(solution)/shard_map/route/pallas_call | solution.py:152
  38.3 0.0 copy-start.5
  38.3 14.5 %all-to-all-start = ((bf16[128,2,128,128]{3,2,1,0:T(8,128)(2,1)}), bf16[128,2,128,128]{3,2,1,0:T(8,128)(2,1)}, u32[]{:S(2)}, u32[]{:S(2)}) async-start(bf16[128,2,128,128]{3,2,1,0:T(8,128)(2,1)} %route.1), calls=%async_computation | async-start | bytes 16777216 | tf_op jit(solution)/shard_map/all_to_all | solution.py:767
  52.8 0.0 copy-done.5
  52.8 0.6 select_reduce_fusion
  53.5 0.1 copy.10
  53.6 0.1 reduce_min.12
  53.7 0.1 copy.9
  53.8 0.1 reduce_max.12
  53.9 0.1 copy.11
  54.0 0.7 reshape.168.land_ref
  54.7 11.4 %plan.1 = (s32[264]{0:T(512)}, s32[768]{0:T(1024)}) custom-call(s32[256]{0:T(256)} %reshape.168.land_ref), custom_call_target="tpu_custom_call" | custom-call | tf_op jit(solution)/shard_map/plan/pallas_call | solution.py:208
  66.1 0.0 copy-start
  66.1 2.2 copy-done
  68.3 72.5 %chol.1 = (bf16[1024,1024]{1,0:T(8,128)(2,1)S(1)}, bf16[1024,1024]{1,0:T(8,128)(2,1)S(1)}, bf16[1024,1024]{1,0:T(8,128)(2,1)S(1)}) custom-call(f32[8,8,128,128]{3,2,1,0:T(8,128)S(1)} %copy-done), custom_call_target="tpu_custom_call" | custom-call | tf_op jit(solution)/shard_map/chol/pallas_call | solution.py:112
  140.8 0.0 copy-start.1
  140.8 1.3 copy-done.1
  142.1 0.0 copy-start.2
  142.1 1.3 copy-done.2
  143.5 0.0 copy-start.3
  143.5 1.3 copy-done.3
  144.8 7.5 %all-to-all-done = bf16[128,2,128,128]{3,2,1,0:T(8,128)(2,1)} async-done(((bf16[128,2,128,128]{3,2,1,0:T(8,128)(2,1)}), bf16[128,2,128,128]{3,2,1,0:T(8,128)(2,1)}, u32[]{:S(2)}, u32[]{:S(2)}) %all-to-all-start) | async-done | bytes 8388640 | tf_op jit(solution)/shard_map/all_to_all | solution.py:767
  152.3 2.8 %head.1.panel_ref = f32[2,4,128,128]{3,2,1,0:T(8,128)} custom-call(s32[256]{0:T(256)} %reshape.168.land_ref, s32[264]{0:T(512)} %get-tuple-element.15.list_ref, f32[4,1,128,32,1,128]{5,4,3,2,1,0:T(1,128)} %front_ref.5, bf16[256,128,128]{2,1,0:T(8,128)(2,1)} %bitcast.5.arr_ref), custom_call_target="tpu_custom_call" | custom-call | tf_op jit(solution)/shard_map/head/pallas_call | solution.py:250
  155.1 74.7 %panel.1 = (f32[4,1,128,32,1,128]{5,4,3,2,1,0:T(1,128)}, bf16[4,128,2,128]{3,2,1,0:T(2,128)(2,1)}) custom-call(s32[768]{0:T(1024)} %get-tuple-element.14.order_ref, f32[2,4,128,128]{3,2,1,0:T(8,128)} %head.1.panel_ref, bf16[1024,1024]{1,0:T(8,128)(2,1)} %copy-done.2, bf16[1024,1024]{1,0:T(8,128)(2,1)} %copy-done.3, bf16[1024,1024]{1,0:T(8,128)(2,1)} %copy-done.1, ...), custom_call_target="tpu_custom_call" | custom-call | tf_op jit(solution)/shard_map/panel/pallas_call | solution.py:553
  229.8 0.0 copy-start.4
  229.8 7.0 %copy.15 = f32[4,1,128,32,1,128]{5,4,3,2,1,0:T(1,128)} copy(f32[4,1,128,32,1,128]{5,4,3,2,1,0:T(1,128)} %get-tuple-element.36) | data formatting | bytes 16777216
  236.8 0.0 copy-done.4
  236.8 0.7 copy.16
  (3 shorter events, 0.0 us)
Async XLA Ops:
  38.3 14.5 %copy-start.5 = (s32[4,4,8,1,128]{4,3,2,1,0:T(1,128)S(1)}, s32[4,4,8,1,128]{4,3,2,1,0:T(1,128)}, u32[]{:S(2)}) copy-start(s32[4,4,8,1,128]{4,3,2,1,0:T(1,128)} %get-tuple-element.13) | copy-start | bytes 196612
  38.3 114.0 %all-to-all-start = ((bf16[128,2,128,128]{3,2,1,0:T(8,128)(2,1)}), bf16[128,2,128,128]{3,2,1,0:T(8,128)(2,1)}, u32[]{:S(2)}, u32[]{:S(2)}) async-start(bf16[128,2,128,128]{3,2,1,0:T(8,128)(2,1)} %route.1), calls=%async_computation | async-start | bytes 16777216 | tf_op jit(solution)/shard_map/all_to_all | solution.py:767
  66.1 2.2 copy-start
  140.8 1.3 copy-start.1
  142.1 1.3 copy-start.2
  143.5 1.3 copy-start.3
  229.8 7.0 %copy-start.4 = (bf16[4,128,2,128]{3,2,1,0:T(2,128)(2,1)S(1)}, bf16[4,128,2,128]{3,2,1,0:T(2,128)(2,1)}, u32[]{:S(2)}) copy-start(bf16[4,128,2,128]{3,2,1,0:T(2,128)(2,1)} %get-tuple-element.23) | copy-start | bytes 786436

commit v6 on v5

--- a/solution.py
+++ b/solution.py
@@ -121,104 +121,76 @@
     )(lead)
 
 
-def route_kernel(own_ref, child_ref, out_ref, idx_ref, cnt_ref):
-    step = pl.program_id(0)
-
-    @pl.when(step == 0)
-    def _():
-        def clear(k, c):
-            cnt_ref[k] = 0
-            for u in range(2):
-                idx_ref[2 * k + u] = 0
-            return c
-        lax.fori_loop(0, 128, clear, 0)
-
-        def place(k, c):
-            o = own_ref[k]
-            n = cnt_ref[o]
-            idx_ref[2 * o + n] = k
-            cnt_ref[o] = n + 1
-            return c
-        lax.fori_loop(0, 128, place, 0)
-
-    def copy(j, c):
-        for u in range(2):
-            out_ref[j, u] = child_ref[idx_ref[step * 32 + 2 * j + u]]
-        return c
-    lax.fori_loop(0, 16, copy, 0)
-
-
-def route(owner, child):
+def index_kernel(owner_ref, slot_ref, idx_ref, code_ref):
+    owner = owner_ref[...]
+    code_ref[...] = owner * 128 + slot_ref[...]
+    wide = jnp.broadcast_to(owner.astype(F32), (128, 128)).T
+    k = lax.broadcasted_iota(jnp.int32, (128, 128), 0).astype(F32)
+    match = wide == lax.broadcasted_iota(jnp.int32, (128, 128), 1).astype(F32)
+    first = jnp.min(jnp.where(match, k, 127.0), 0, keepdims=True)
+    last = jnp.max(jnp.where(match, k, 0.0), 0, keepdims=True)
+    idx_ref[0:1, :] = first.astype(jnp.int32)
+    idx_ref[1:2, :] = last.astype(jnp.int32)
+
+
+def index(owner, slot):
     return pl.pallas_call(
-        route_kernel,
-        out_shape=jax.ShapeDtypeStruct((128, 2, 128, 128), BF),
-        grid_spec=pltpu.PrefetchScalarGridSpec(
-            num_scalar_prefetch=1, grid=(8,),
-            in_specs=[pl.BlockSpec((128, 128, 128), lambda g, a: (0, 0, 0), pipeline_mode=pl.Buffered(1))],
-            out_specs=pl.BlockSpec((16, 2, 128, 128), lambda g, a: (g, 0, 0, 0)),
-            scratch_shapes=[pltpu.SMEM((256,), jnp.int32), pltpu.SMEM((128,), jnp.int32)]),
-        compiler_params=pltpu.CompilerParams(vmem_limit_bytes=60 << 20),
-        name="route",
-    )(owner, child)
-
-
-def plan_kernel(land_ref, list_ref, order_ref, cnt_ref, pos_ref):
-    def clear(k, c):
-        cnt_ref[k] = 0
-        for u in range(4):
-            order_ref[4 * k + u] = 0
-        return c
-    lax.fori_loop(0, 128, clear, 0)
-
-    def look(k, n):
-        slot = land_ref[k]
-        @pl.when(slot >= 0)
-        def _():
-            cnt_ref[slot] = cnt_ref[slot] + 1
-        hit = (slot >= 0) & (lax.rem(lax.max(slot, 0), 32) < 2)
-        @pl.when(hit)
-        def _():
-            list_ref[n + 1] = k
-        return n + hit.astype(jnp.int32)
-    list_ref[0] = lax.fori_loop(0, 256, look, 0)
-
-    def bounds(j, n):
-        here = cnt_ref[j]
-        pos_ref[j] = n
-        order_ref[512 + j] = lax.max(n + here - 1, 0)
-        order_ref[640 + j] = lax.min(here, 1)
-        cnt_ref[j] = 0
-        return n + here
-    lax.fori_loop(0, 128, bounds, 0)
-
-    def place(k, c):
-        slot = land_ref[k]
-        @pl.when(slot >= 0)
-        def _():
-            p = pos_ref[slot]
-            order_ref[p] = k
-            order_ref[256 + p] = cnt_ref[slot]
-            cnt_ref[slot] = 1
-            pos_ref[slot] = p + 1
-        return c
-    lax.fori_loop(0, 256, place, 0)
+        index_kernel,
+        out_shape=(jax.ShapeDtypeStruct((2, 128), jnp.int32), jax.ShapeDtypeStruct((1, 128), jnp.int32)),
+        in_specs=[pl.BlockSpec(memory_space=V)] * 2,
+        out_specs=[pl.BlockSpec(memory_space=V)] * 2,
+        name="index",
+    )(owner, slot)
+
+
+def plan_kernel(col_ref, row_ref, out_ref):
+    def at(shape, axis):
+        return lax.broadcasted_iota(jnp.int32, shape, axis).astype(F32)
+    square = (256, 256)
+    own = jnp.broadcast_to(col_ref[...], square).astype(F32)
+    other = jnp.broadcast_to(row_ref[...], square).astype(F32)
+    k, j = at(square, 0), at(square, 1)
+    one = jnp.ones(square, F32)
+    zero = jnp.zeros(square, F32)
+    key, other_key = jnp.where(own < 0, 1000.0, own), jnp.where(other < 0, 1000.0, other)
+    before = (other_key < key) | ((other_key == key) & (j < k))
+    rank = jnp.sum(jnp.where(before, one, zero), 1, keepdims=True)
+    here = jnp.broadcast_to(rank, square) == j
+    order = jnp.sum(jnp.where(here, k, zero), 0, keepdims=True)
+    slots = jnp.sum(jnp.where(here, key, zero), 0, keepdims=True)
+    lane = at((1, 256), 1)
+    same = jnp.where((slots == pltpu.roll(slots, 1, 1)) & (lane > 0) & (slots < 1000.0), 1.0, 0.0)
+    half = (256, 128)
+    slot = at(half, 1)
+    own_key = key[:, 0:128]
+    last = jnp.sum(jnp.where(own_key <= slot, 1.0, 0.0), 0, keepdims=True) - 1.0
+    some = jnp.max(jnp.where(own_key == slot, 1.0, 0.0), 0, keepdims=True)
+
+    def panel_column(x):
+        return (x >= 0) & (x - 32.0 * jnp.floor(x * (1 / 32)) < 2.0)
+    hit, other_hit = panel_column(own), panel_column(other)
+    turn = jnp.sum(jnp.where(other_hit & (j < k), one, zero), 1, keepdims=True)
+    listed = jnp.sum(jnp.where(hit & (jnp.broadcast_to(turn, square) == j), k, zero), 0, keepdims=True)
+    count = jnp.sum(jnp.where(hit, one, zero), 0, keepdims=True)
+    rows = [order, same, jnp.concatenate([jnp.maximum(last, 0.0), some], 1), listed, count]
+    for r in range(5):
+        out_ref[r:r + 1, :] = rows[r].astype(jnp.int32)
 
 
 def plan(land):
     return pl.pallas_call(
         plan_kernel,
-        out_shape=(jax.ShapeDtypeStruct((264,), jnp.int32), jax.ShapeDtypeStruct((768,), jnp.int32)),
-        in_specs=[pl.BlockSpec(memory_space=pltpu.SMEM)],
-        out_specs=(pl.BlockSpec(memory_space=pltpu.SMEM),) * 2,
-        scratch_shapes=[pltpu.SMEM((128,), jnp.int32)] * 2,
+        out_shape=jax.ShapeDtypeStruct((5, 256), jnp.int32),
+        in_specs=[pl.BlockSpec(memory_space=V)] * 2,
+        out_specs=pl.BlockSpec(memory_space=V),
         name="plan",
-    )(land)
+    )(land.reshape(256, 1), land.reshape(1, 256))
 
 
 def head_kernel(land_ref, list_ref, front_ref, arr_ref, out_ref, buf_ref, acc_ref, fsem, asem):
-    count = list_ref[0]
+    count = list_ref[4, 0]
     def arrive(n, i):
-        return pltpu.make_async_copy(arr_ref.at[list_ref[n + 1]], buf_ref.at[i], asem.at[i])
+        return pltpu.make_async_copy(arr_ref.at[list_ref[3, n]], buf_ref.at[i], asem.at[i])
     def fetch(s):
         return pltpu.make_async_copy(front_ref.at[:, 0, :, s, 0, :], acc_ref.at[s], fsem.at[s])
     for s in range(2):
@@ -229,7 +201,7 @@
             return c
         def end(i, c):
             n = b * 16 + i
-            slot = land_ref[list_ref[n + 1]]
+            slot = land_ref[list_ref[3, n]]
             s, q = slot % 32, slot // 32
             arrive(n, i).wait()
             acc_ref[s, q] = acc_ref[s, q] + buf_ref[i].astype(F32)
@@ -407,7 +379,7 @@
     def gather(c):
         def go(k, total):
             i = c * 32 + k
-            total = buf_ref[order_ref[i]].astype(F32) + order_ref[256 + i].astype(F32) * total
+            total = buf_ref[order_ref[0, i]].astype(F32) + order_ref[1, i].astype(F32) * total
             run_ref[i] = total
             return total
         first = jnp.zeros((128, 128), F32) if c == 0 else run_ref[c * 32 - 1]
@@ -416,7 +388,7 @@
     def settle(s):
         for q in range(4):
             slot = q * 32 + s
-            acc_ref[s, q] = acc_ref[s, q] + order_ref[640 + slot].astype(F32) * run_ref[order_ref[512 + slot]]
+            acc_ref[s, q] = acc_ref[s, q] + order_ref[2, 128 + slot].astype(F32) * run_ref[order_ref[2, slot]]
 
     keep = jnp.where(group < 8, 0.0, 1.0)
     pair0 = sub - lax.rem(sub, 2)
@@ -566,7 +538,7 @@
     )(order, panel, hi, lo, low, front, arrived)
 
 
-def lead_kernel(front_ref, code_ref, lead_ref, codes_ref, own_ref, lsem, zs, zr, zls, zlr, xs, xr, ys, yr, as_, ar, bs, br, cs, cr):
+def lead_kernel(idx_ref, front_ref, code_ref, child_ref, lead_ref, codes_ref, sent_ref, own_ref, tile_ref, pack_ref, tsem, psem, lsem, zs, zr, zls, zlr, xs, xr, ys, yr, as_, ar, bs, br, cas, car, cbs, cbr):
     sub, row, col = lax.axis_index("sub"), lax.axis_index("row"), lax.axis_index("col")
     par = lax.rem(sub, 2)
     mate = sub + 1 - 2 * par
@@ -585,9 +557,22 @@
 
     mine = [pltpu.make_async_copy(front_ref.at[0, 0, :, s, 0, :], own_ref.at[s], lsem.at[s]) for s in range(2)]
     code = pltpu.make_async_copy(code_ref, codes_ref.at[col, row, sub], lsem.at[2])
+    tiles = [pltpu.make_async_copy(child_ref.at[pl.ds(32 * g, 32)], tile_ref.at[pl.ds(32 * g, 32)], tsem.at[g]) for g in range(4)]
+    packs = [pltpu.make_async_copy(pack_ref.at[pl.ds(16 * g, 16)], sent_ref.at[pl.ds(16 * g, 16)], psem.at[g]) for g in range(8)]
+
+    def pack(g):
+        def go(j, c):
+            for u in range(2):
+                pack_ref[16 * g + j, u] = tile_ref[idx_ref[u, 16 * g + j]]
+            return c
+        lax.fori_loop(0, 16, go, 0)
+        packs[g].start()
+
     code.start()
     mine[0].start()
     mine[1].start()
+    for copy in tiles:
+        copy.start()
     mine[0].wait()
     mine[1].wait()
     keep = [pltpu.make_async_copy(own_ref.at[s], lead_ref.at[line, 4 * s + col], lsem.at[3 + s]) for s in range(2)]
@@ -615,6 +600,10 @@
                 remote(own_ref.at[1], lead_ref.at[line, 4 + col], zls.at[d - 1, 1], zlr.at[1], sub=sub + 2 * d).start()
     for d in range(1, 8):
         zcode(d).start()
+    for copy in tiles:
+        copy.wait()
+    for g in range(4):
+        pack(g)
 
     @pl.when(sub < 2)
     def _():
@@ -656,7 +645,7 @@
         return remote(codes_ref.at[c], codes_ref.at[c], ys.at[d - 1], yr.at[d - 1], col=lax.rem(col + d, 4))
     for d in range(1, 4):
         cx(d, row).start()
-    for d in range(1, 4):
+    for d in (1, 3, 2):
         @pl.when(par == 1)
         def _():
             ax(d, lax.rem(row + 4 - d, 4)).wait_recv()
@@ -671,31 +660,45 @@
             @pl.when(c <= row)
             def _():
                 bx(d, row, c).start()
+
+    def swap_a(c):
+        at = lead_ref.at[pl.ds(4, 4), c]
+        return remote(at, at, cas.at[c], car.at[c], sub=mate)
+    def swap_b(p, r, c):
+        at = lead_ref.at[4 * p + r, 4 * p + c]
+        return remote(at, at, cbs.at[r, c], cbr.at[r, c], sub=mate)
+    def hand(r, c):
+        @pl.when(par == 1)
+        def _():
+            swap_a(c).start()
+        for u in range(4):
+            @pl.when(u <= r)
+            def _():
+                swap_b(par, r, u).start()
+    hand(row, col)
+    for g in range(4, 8):
+        pack(g)
     for d in range(1, 4):
         cx(d, lax.rem(row + 4 - d, 4)).wait_recv()
     for d in range(1, 4):
         cy(d, col).start()
-    for d in range(1, 4):
+    for d in (1, 3, 2):
+        r = lax.rem(row + 4 - d, 4)
         @pl.when(par == 1)
         def _():
             ay(d, lax.rem(col + 4 - d, 4)).wait_recv()
         for c in range(4):
-            r = lax.rem(row + 4 - d, 4)
             @pl.when(c <= r)
             def _():
                 bx(d, r, c).wait_recv()
-
-    def swap(i):
-        at = lead_ref.at[i, pl.ds(0, i + 1)]
-        return remote(at, at, cs.at[i % 4], cr.at[i % 4], sub=mate)
-    for i in range(8):
-        @pl.when(par == i // 4)
-        def _():
-            swap(i).start()
-    for i in range(8):
-        @pl.when(par != i // 4)
-        def _():
-            swap(i).wait_recv()
+        hand(r, lax.rem(col + 4 - d, 4))
+    @pl.when(par == 0)
+    def _():
+        for c in range(4):
+            swap_a(c).wait_recv()
+    for r in range(4):
+        for c in range(r + 1):
+            swap_b(1 - par, r, c).wait_recv()
     for d in range(1, 4):
         cy(d, lax.rem(col + 4 - d, 4)).wait_recv()
 
@@ -724,24 +727,31 @@
             @pl.when(c <= row)
             def _():
                 bx(d, row, c).wait_send()
-    for i in range(8):
-        @pl.when(par == i // 4)
-        def _():
-            swap(i).wait_send()
-
-
-def lead_gather(front, code):
+    @pl.when(par == 1)
+    def _():
+        for c in range(4):
+            swap_a(c).wait_send()
+    for r in range(4):
+        for c in range(r + 1):
+            swap_b(par, r, c).wait_send()
+    for copy in packs:
+        copy.wait()
+
+
+def lead_gather(idx, front, code, child):
     D = pltpu.SemaphoreType.DMA
     return pl.pallas_call(
         lead_kernel,
-        out_shape=(jax.ShapeDtypeStruct((8, 8, 128, 128), F32), jax.ShapeDtypeStruct((4, 4, 8, 1, 128), jnp.int32)),
-        in_specs=[pl.BlockSpec(memory_space=pltpu.HBM), pl.BlockSpec(memory_space=V)],
-        out_specs=(pl.BlockSpec(memory_space=V), pl.BlockSpec(memory_space=V)),
-        scratch_shapes=[V((2, 128, 128), F32), D((5,)), D((7,)), D((7,)), D((3, 2)), D((2,)), D((3,)), D((3,)), D((3,)), D((3,)),
-                        D((2, 3)), D((2, 3)), D((3, 5)), D((3, 5)), D((4,)), D((4,))],
+        out_shape=(jax.ShapeDtypeStruct((8, 8, 128, 128), F32), jax.ShapeDtypeStruct((4, 4, 8, 1, 128), jnp.int32),
+                   jax.ShapeDtypeStruct((128, 2, 128, 128), BF)),
+        in_specs=[pl.BlockSpec(memory_space=pltpu.SMEM), pl.BlockSpec(memory_space=pltpu.HBM), pl.BlockSpec(memory_space=V),
+                  pl.BlockSpec(memory_space=pltpu.HBM)],
+        out_specs=(pl.BlockSpec(memory_space=V), pl.BlockSpec(memory_space=V), pl.BlockSpec(memory_space=pltpu.HBM)),
+        scratch_shapes=[V((2, 128, 128), F32), V((128, 128, 128), BF), V((128, 2, 128, 128), BF), D((4,)), D((8,)), D((5,)), D((7,)), D((7,)), D((3, 2)), D((2,)), D((3,)), D((3,)), D((3,)), D((3,)),
+                        D((2, 3)), D((2, 3)), D((3, 5)), D((3, 5)), D((4,)), D((4,)), D((4, 4)), D((4, 4))],
         compiler_params=pltpu.CompilerParams(vmem_limit_bytes=60 << 20, collective_id=1, has_side_effects=True),
         name="lead",
-    )(front, code)
+    )(idx, front, code, child)
 
 
 def landings(codes, me):
@@ -760,16 +770,14 @@
     row = lax.axis_index("row")
     col = lax.axis_index("col")
     group = sub * 4 + row
-    owner = tile_owner[:, 0]
-    outgoing = route(owner, child_tiles)
-    lead, codes = lead_gather(front, (owner * 128 + tile_slot).reshape(1, 128))
-    outgoing, lead = lax.optimization_barrier((outgoing, lead))
+    idx, code = index(tile_owner.reshape(1, 128), tile_slot.reshape(1, 128))
+    lead, codes, outgoing = lead_gather(idx, front, code, child_tiles)
     arrived = lax.all_to_all(outgoing, ("sub", "row", "col"), split_axis=0, concat_axis=0, tiled=True)
     arrived = arrived.reshape(256, 128, 128)
     factor, hi, lo = chol(lead)
     landing = landings(codes, group * 4 + col)
-    listed, order = plan(landing)
-    panel = head(landing, listed, front, arrived)
+    order = plan(landing)
+    panel = head(landing, order, front, arrived)
     out, panel_out = panel_exchange(order, panel, hi, lo, factor, front, arrived)
     return out, panel_out.reshape(4, 1, 128, 2, 1, 128)
 

time: 238 us -> 229 us (0.962)
  Pallas kernels: 198 us -> 182 us
  waiting for transfers between devices: 7.51 us -> 15.6 us
    pallas_call x2, Pallas kernels: 19.5 us -> 3.18 us  [the longest x1 1.83 us: plan(): pl.pallas_call(plan_kernel, out_shape=jax.ShapeDtypeStruct((5, 256), jnp....]
    all_to_all x1, waiting for transfers between devices: 7.51 us -> 15.6 us  [local(): lax.all_to_all(outgoing, ('sub', 'row', 'col'), split_axis=0, concat_axis...]
  transfers between devices with their start and end apart: 1 -> 1, of which waited for: 1 -> 1; matrix products, arithmetic and copies ran while one was open for 1% -> 1% of each run, Pallas kernels for 35% -> 32%
where the time goes in v6:
time: 229 us
  Pallas kernels  182 us (79%)
  local copies, waits for them, and re-layouts  16.6 us (7%)
  waiting for transfers between devices  15.6 us (7%)
  starting transfers between devices  13.3 us (6%)
    pallas_call x1, Pallas kernels, panel_exchange(): pl.pallas_call(panel_kernel, out_shape=(jax.ShapeDtypeStruct((4, 1, 128,...  74.7 us
    pallas_call x1, Pallas kernels, chol(): pl.pallas_call(chol_kernel, out_shape=[jax.ShapeDtypeStruct((1024, 1024),...  72.5 us
    pallas_call x1, Pallas kernels, lead_gather(): pl.pallas_call(lead_kernel, out_shape=(jax.ShapeDtypeStruct((8, 8, 128, 1...  28.6 us
    all_to_all x1, waiting for transfers between devices, local(): lax.all_to_all(outgoing, ('sub', 'row', 'col'), split_axis=0, concat_axis...  15.6 us
    unnamed x14, local copies, waits for them, and re-layouts  13.8 us
    all_to_all x1, starting transfers between devices, local(): lax.all_to_all(outgoing, ('sub', 'row', 'col'), split_axis=0, concat_axis...  13.3 us
  transfers between devices with their start and end apart: 1, of which 1 were waited for; matrix products, arithmetic and copies ran while one was open for 1% of the time, Pallas kernels for 32%

profile of v6, /device:TPU:26, one launch (start us, length us, event | category | flops | bytes accessed | tf_op | source)
XLA Modules:
  0.0 228.7 jit_solution(8602224190751219264)
XLA Ops:
  0.6 1.4 index.1
  2.0 28.6 %lead.1 = (f32[8,8,128,128]{3,2,1,0:T(8,128)}, s32[4,4,8,1,128]{4,3,2,1,0:T(1,128)}, bf16[128,2,128,128]{3,2,1,0:T(8,128)(2,1)}) custom-call(s32[2,128]{1,0:T(2,128)} %get-tuple-element.12.idx_ref, f32[4,1,128,32,1,128]{5,4,3,2,1,0:T(1,128)} %front_ref.5, s32[1,128]{1,0:T(1,128)} %get-tuple-element.13.code_ref, bf16[128,128,128]{2,1,0:T(8,128)(2,1)} %child_ref.1), custom_call_target="tpu_custom_call" | custom-call | tf_op jit(solution)/shard_map/lead/pallas_call | solution.py:743
  30.5 0.0 copy-start.5
  30.5 13.3 %all-to-all-start = ((bf16[128,2,128,128]{3,2,1,0:T(8,128)(2,1)}), bf16[128,2,128,128]{3,2,1,0:T(8,128)(2,1)}, u32[]{:S(2)}, u32[]{:S(2)}) async-start(bf16[128,2,128,128]{3,2,1,0:T(8,128)(2,1)} %get-tuple-element.15), calls=%async_computation | async-start | bytes 16777216 | tf_op jit(solution)/shard_map/all_to_all | solution.py:775
  43.9 0.0 copy-done.5
  43.9 0.6 select_reduce_fusion
  44.6 0.1 copy.15
  44.7 0.1 reduce_min.12
  44.8 0.1 copy.14
  44.9 0.1 reduce_max.12
  45.0 0.1 copy.16
  45.1 0.7 reshape.172.land_ref
  45.8 0.7 reshape_reshape.7.row_ref
  46.6 0.7 reshape_reshape.8.col_ref
  47.3 0.0 copy-start
  47.3 2.2 copy-done
  49.5 72.5 %chol.1 = (bf16[1024,1024]{1,0:T(8,128)(2,1)S(1)}, bf16[1024,1024]{1,0:T(8,128)(2,1)S(1)}, bf16[1024,1024]{1,0:T(8,128)(2,1)S(1)}) custom-call(f32[8,8,128,128]{3,2,1,0:T(8,128)S(1)} %copy-done), custom_call_target="tpu_custom_call" | custom-call | tf_op jit(solution)/shard_map/chol/pallas_call | solution.py:112
  122.0 0.0 copy-start.1
  122.0 1.3 copy-done.1
  123.3 0.0 copy-start.2
  123.3 1.3 copy-done.2
  124.6 0.0 copy-start.3
  124.6 1.3 copy-done.3
  126.0 1.8 plan.1.list_ref.order_ref
  127.8 15.6 %all-to-all-done = bf16[128,2,128,128]{3,2,1,0:T(8,128)(2,1)} async-done(((bf16[128,2,128,128]{3,2,1,0:T(8,128)(2,1)}), bf16[128,2,128,128]{3,2,1,0:T(8,128)(2,1)}, u32[]{:S(2)}, u32[]{:S(2)}) %all-to-all-start) | async-done | bytes 8388640 | tf_op jit(solution)/shard_map/all_to_all | solution.py:775
  143.4 2.9 %head.1.panel_ref = f32[2,4,128,128]{3,2,1,0:T(8,128)} custom-call(s32[256]{0:T(256)} %reshape.172.land_ref, s32[5,256]{1,0:T(8,128)} %plan.1.list_ref.order_ref, f32[4,1,128,32,1,128]{5,4,3,2,1,0:T(1,128)} %front_ref.5, bf16[256,128,128]{2,1,0:T(8,128)(2,1)} %bitcast.5.arr_ref), custom_call_target="tpu_custom_call" | custom-call | tf_op jit(solution)/shard_map/head/pallas_call | solution.py:222
  146.3 74.7 %panel.1 = (f32[4,1,128,32,1,128]{5,4,3,2,1,0:T(1,128)}, bf16[4,128,2,128]{3,2,1,0:T(2,128)(2,1)}) custom-call(s32[5,256]{1,0:T(8,128)} %plan.1.list_ref.order_ref, f32[2,4,128,128]{3,2,1,0:T(8,128)} %head.1.panel_ref, bf16[1024,1024]{1,0:T(8,128)(2,1)} %copy-done.2, bf16[1024,1024]{1,0:T(8,128)(2,1)} %copy-done.3, bf16[1024,1024]{1,0:T(8,128)(2,1)} %copy-done.1, ...), custom_call_target="tpu_custom_call" | custom-call | tf_op jit(solution)/shard_map/panel/pallas_call | solution.py:525
  221.0 0.0 copy-start.4
  221.0 7.0 %copy.23 = f32[4,1,128,32,1,128]{5,4,3,2,1,0:T(1,128)} copy(f32[4,1,128,32,1,128]{5,4,3,2,1,0:T(1,128)} %get-tuple-element.34) | data formatting | bytes 16777216
  228.0 0.0 copy-done.4
  228.0 0.7 copy.24
  (3 shorter events, 0.0 us)
Async XLA Ops:
  30.5 13.4 %copy-start.5 = (s32[4,4,8,1,128]{4,3,2,1,0:T(1,128)S(1)}, s32[4,4,8,1,128]{4,3,2,1,0:T(1,128)}, u32[]{:S(2)}) copy-start(s32[4,4,8,1,128]{4,3,2,1,0:T(1,128)} %get-tuple-element.14) | copy-start | bytes 196612
  30.5 112.8 %all-to-all-start = ((bf16[128,2,128,128]{3,2,1,0:T(8,128)(2,1)}), bf16[128,2,128,128]{3,2,1,0:T(8,128)(2,1)}, u32[]{:S(2)}, u32[]{:S(2)}) async-start(bf16[128,2,128,128]{3,2,1,0:T(8,128)(2,1)} %get-tuple-element.15), calls=%async_computation | async-start | bytes 16777216 | tf_op jit(solution)/shard_map/all_to_all | solution.py:775
  47.3 2.2 copy-start
  122.0 1.3 copy-start.1
  123.3 1.3 copy-start.2
  124.6 1.3 copy-start.3
  221.0 7.0 %copy-start.4 = (bf16[4,128,2,128]{3,2,1,0:T(2,128)(2,1)S(1)}, bf16[4,128,2,128]{3,2,1,0:T(2,128)(2,1)}, u32[]{:S(2)}) copy-start(bf16[4,128,2,128]{3,2,1,0:T(2,128)(2,1)} %get-tuple-element.21) | copy-start | bytes 786436

commit v7 on v6

--- a/solution.py
+++ b/solution.py
@@ -398,6 +398,8 @@
         s = q * 8 + z
         @pl.when(s >= 2)
         def _():
+            settle(s)
+            settle(s + 1)
             y = mm(brow_ref[...].reshape(512, 1024), bcol_ref[q, pl.ds(z, 2)].reshape(256, 1024))
             for u in range(2):
                 t = y[:, u * 128:(u + 1) * 128].reshape(4, 128, 128)
@@ -443,7 +445,6 @@
         xforward(i, n4(row, 2)).wait_recv()
     reach(2)
     each(2, 32, lambda s: fetch(s).wait())
-    each(2, 12, settle)
     for i in range(2):
         yfar(i).wait_recv()
         yrelay(i).start()
@@ -455,14 +456,14 @@
     launch(2)
     for i in range(2):
         wforward(i, n4(col, 2)).wait_recv()
-    each(12, 32, settle)
-    for q in range(4):
-        pair = [brow_ref[q, :, pl.ds(pl.multiple_of((4 * s + col) * 128, 128), 128)] for s in range(2)]
-        pout_ref[q] = jnp.stack([x.astype(F32) for x in pair], 1).astype(BF)
     home.wait()
 
     def gray(k):
         return k + jnp.where(k == 2, 1, 0) - jnp.where(k == 3, 1, 0)
+
+    def product(e, k, z):
+        swapped(e, k, z).wait_recv()
+        update(e, z)
 
     def pass_on(k, carry):
         e = gray(k)
@@ -472,29 +473,35 @@
             def _():
                 onward(e, i, -2 * step[i]).start()
             swap(e, 1 + i, -2 * step[i]).start()
-        swapped(e, 0, 0).wait_recv()
-        update(e, 0)
+
+        def three(j, c):
+            @pl.when((j == 0) | (k > 0))
+            def _():
+                product(jnp.where(j == 0, e, gray(lax.max(k - 1, 0))), j, jnp.where(j == 0, 0, 4 * j - 6))
+            return c
+        lax.fori_loop(0, 3, three, 0)
         return carry
     lax.fori_loop(0, 4, pass_on, 0)
 
+    for q in range(4):
+        pair = [brow_ref[q, :, pl.ds(pl.multiple_of((4 * s + col) * 128, 128), 128)] for s in range(2)]
+        pout_ref[q] = jnp.stack([x.astype(F32) for x in pair], 1).astype(BF)
+
     def last(k, carry):
-        e = gray(k)
-        onward(e, 0, 4).wait_recv()
-        swap(e, 3, 4).start()
-        def sides(j, c):
-            swapped(e, 1 + j, 4 * j - 2).wait_recv()
-            update(e, 4 * j - 2)
+        @pl.when(k < 4)
+        def _():
+            e = gray(k)
+            onward(e, 0, 4).wait_recv()
+            swap(e, 3, 4).start()
+
+        def two(j, c):
+            @pl.when((j == 0) | (k == 0))
+            def _():
+                product(jnp.where(k == 0, 2, gray(lax.max(k - 1, 0))), jnp.where(k == 0, 1 + j, 3), jnp.where(k == 0, 4 * j - 2, 4))
             return c
-        lax.fori_loop(0, 2, sides, 0)
+        lax.fori_loop(0, 2, two, 0)
         return carry
-    lax.fori_loop(0, 4, last, 0)
-
-    def far(k, carry):
-        e = gray(k)
-        swapped(e, 3, 4).wait_recv()
-        update(e, 4)
-        return carry
-    lax.fori_loop(0, 4, far, 0)
+    lax.fori_loop(0, 5, last, 0)
     early(0).wait()
     early(1).wait()
     each(2, 32, lambda s: put(s).wait())

time: 229 us -> 228 us (level)
  transfers between devices with their start and end apart: 1 -> 1, of which waited for: 1 -> 1; matrix products, arithmetic and copies ran while one was open for 1% -> 1% of each run, Pallas kernels for 32% -> 33%
where the time goes in v7:
time: 228 us; the launch traced here: 227 us
  Pallas kernels  180 us (79%)
  local copies, waits for them, and re-layouts  16.6 us (7%)
  waiting for transfers between devices  15.6 us (7%)
  starting transfers between devices  13.3 us (6%)
    pallas_call x1, Pallas kernels, panel_exchange(): pl.pallas_call(panel_kernel, out_shape=(jax.ShapeDtypeStruct((4, 1, 128,...  73.2 us
    pallas_call x1, Pallas kernels, chol(): pl.pallas_call(chol_kernel, out_shape=[jax.ShapeDtypeStruct((1024, 1024),...  72.5 us
    pallas_call x1, Pallas kernels, lead_gather(): pl.pallas_call(lead_kernel, out_shape=(jax.ShapeDtypeStruct((8, 8, 128, 1...  28.6 us
    all_to_all x1, waiting for transfers between devices, local(): lax.all_to_all(outgoing, ('sub', 'row', 'col'), split_axis=0, concat_axis...  15.6 us
    unnamed x14, local copies, waits for them, and re-layouts  13.8 us
    all_to_all x1, starting transfers between devices, local(): lax.all_to_all(outgoing, ('sub', 'row', 'col'), split_axis=0, concat_axis...  13.3 us
  transfers between devices with their start and end apart: 1, of which 1 were waited for; matrix products, arithmetic and copies ran while one was open for 1% of the time, Pallas kernels for 33%

profile of v7, /device:TPU:26, one launch (start us, length us, event | category | flops | bytes accessed | tf_op | source)
XLA Modules:
  0.0 227.2 jit_solution(6693898378945579587)
XLA Ops:
  0.6 1.4 index.1
  2.0 28.6 %lead.1 = (f32[8,8,128,128]{3,2,1,0:T(8,128)}, s32[4,4,8,1,128]{4,3,2,1,0:T(1,128)}, bf16[128,2,128,128]{3,2,1,0:T(8,128)(2,1)}) custom-call(s32[2,128]{1,0:T(2,128)} %get-tuple-element.12.idx_ref, f32[4,1,128,32,1,128]{5,4,3,2,1,0:T(1,128)} %front_ref.5, s32[1,128]{1,0:T(1,128)} %get-tuple-element.13.code_ref, bf16[128,128,128]{2,1,0:T(8,128)(2,1)} %child_ref.1), custom_call_target="tpu_custom_call" | custom-call | tf_op jit(solution)/shard_map/lead/pallas_call | solution.py:750
  30.5 0.0 copy-start.5
  30.5 13.3 %all-to-all-start = ((bf16[128,2,128,128]{3,2,1,0:T(8,128)(2,1)}), bf16[128,2,128,128]{3,2,1,0:T(8,128)(2,1)}, u32[]{:S(2)}, u32[]{:S(2)}) async-start(bf16[128,2,128,128]{3,2,1,0:T(8,128)(2,1)} %get-tuple-element.15), calls=%async_computation | async-start | bytes 16777216 | tf_op jit(solution)/shard_map/all_to_all | solution.py:782
  43.9 0.0 copy-done.5
  43.9 0.6 select_reduce_fusion
  44.6 0.1 copy.15
  44.7 0.1 reduce_min.12
  44.8 0.1 copy.14
  44.9 0.1 reduce_max.12
  45.0 0.1 copy.16
  45.1 0.7 reshape.172.land_ref
  45.8 0.7 reshape_reshape.7.row_ref
  46.6 0.7 reshape_reshape.8.col_ref
  47.3 0.0 copy-start
  47.3 2.2 copy-done
  49.5 72.5 %chol.1 = (bf16[1024,1024]{1,0:T(8,128)(2,1)S(1)}, bf16[1024,1024]{1,0:T(8,128)(2,1)S(1)}, bf16[1024,1024]{1,0:T(8,128)(2,1)S(1)}) custom-call(f32[8,8,128,128]{3,2,1,0:T(8,128)S(1)} %copy-done), custom_call_target="tpu_custom_call" | custom-call | tf_op jit(solution)/shard_map/chol/pallas_call | solution.py:112
  122.0 0.0 copy-start.1
  122.0 1.3 copy-done.1
  123.3 0.0 copy-start.2
  123.3 1.3 copy-done.2
  124.6 0.0 copy-start.3
  124.6 1.3 copy-done.3
  126.0 1.8 plan.1.list_ref.order_ref
  127.8 15.6 %all-to-all-done = bf16[128,2,128,128]{3,2,1,0:T(8,128)(2,1)} async-done(((bf16[128,2,128,128]{3,2,1,0:T(8,128)(2,1)}), bf16[128,2,128,128]{3,2,1,0:T(8,128)(2,1)}, u32[]{:S(2)}, u32[]{:S(2)}) %all-to-all-start) | async-done | bytes 8388640 | tf_op jit(solution)/shard_map/all_to_all | solution.py:782
  143.4 2.9 %head.1.panel_ref = f32[2,4,128,128]{3,2,1,0:T(8,128)} custom-call(s32[256]{0:T(256)} %reshape.172.land_ref, s32[5,256]{1,0:T(8,128)} %plan.1.list_ref.order_ref, f32[4,1,128,32,1,128]{5,4,3,2,1,0:T(1,128)} %front_ref.5, bf16[256,128,128]{2,1,0:T(8,128)(2,1)} %bitcast.5.arr_ref), custom_call_target="tpu_custom_call" | custom-call | tf_op jit(solution)/shard_map/head/pallas_call | solution.py:222
  146.3 73.2 %panel.1 = (f32[4,1,128,32,1,128]{5,4,3,2,1,0:T(1,128)}, bf16[4,128,2,128]{3,2,1,0:T(2,128)(2,1)}) custom-call(s32[5,256]{1,0:T(8,128)} %plan.1.list_ref.order_ref, f32[2,4,128,128]{3,2,1,0:T(8,128)} %head.1.panel_ref, bf16[1024,1024]{1,0:T(8,128)(2,1)} %copy-done.2, bf16[1024,1024]{1,0:T(8,128)(2,1)} %copy-done.3, bf16[1024,1024]{1,0:T(8,128)(2,1)} %copy-done.1, ...), custom_call_target="tpu_custom_call" | custom-call | tf_op jit(solution)/shard_map/panel/pallas_call | solution.py:532
  219.5 0.0 copy-start.4
  219.5 7.0 %copy.23 = f32[4,1,128,32,1,128]{5,4,3,2,1,0:T(1,128)} copy(f32[4,1,128,32,1,128]{5,4,3,2,1,0:T(1,128)} %get-tuple-element.34) | data formatting | bytes 16777216
  226.5 0.0 copy-done.4
  226.5 0.7 copy.24
  (3 shorter events, 0.0 us)
Async XLA Ops:
  30.5 13.4 %copy-start.5 = (s32[4,4,8,1,128]{4,3,2,1,0:T(1,128)S(1)}, s32[4,4,8,1,128]{4,3,2,1,0:T(1,128)}, u32[]{:S(2)}) copy-start(s32[4,4,8,1,128]{4,3,2,1,0:T(1,128)} %get-tuple-element.14) | copy-start | bytes 196612
  30.5 112.8 %all-to-all-start = ((bf16[128,2,128,128]{3,2,1,0:T(8,128)(2,1)}), bf16[128,2,128,128]{3,2,1,0:T(8,128)(2,1)}, u32[]{:S(2)}, u32[]{:S(2)}) async-start(bf16[128,2,128,128]{3,2,1,0:T(8,128)(2,1)} %get-tuple-element.15), calls=%async_computation | async-start | bytes 16777216 | tf_op jit(solution)/shard_map/all_to_all | solution.py:782
  47.3 2.2 copy-start
  122.0 1.3 copy-start.1
  123.3 1.3 copy-start.2
  124.6 1.3 copy-start.3
  219.5 7.0 %copy-start.4 = (bf16[4,128,2,128]{3,2,1,0:T(2,128)(2,1)S(1)}, bf16[4,128,2,128]{3,2,1,0:T(2,128)(2,1)}, u32[]{:S(2)}) copy-start(bf16[4,128,2,128]{3,2,1,0:T(2,128)(2,1)} %get-tuple-element.21) | copy-start | bytes 786436

commit v8 on v7

--- a/solution.py
+++ b/solution.py
@@ -276,104 +276,109 @@
             return c
         lax.fori_loop(low, high, go, 0)
 
-    def take(d):
-        return remote(panel_ref.at[:, n4(col, d)], arow.at[col], ps.at[d - 1], pr.at[d - 1], col=n4(col, d))
-    def taken(d):
-        return remote(panel_ref.at[:, n4(col, d)], arow.at[n4(col, -d)], ps.at[d - 1], pr.at[d - 1], col=n4(col, d))
-    for d in (1, 3, 2):
-        take(d).start()
+    def take(h, d):
+        return remote(panel_ref.at[h, n4(col, d)], arow.at[col, h], ps.at[h, d - 1], pr.at[h, d - 1], col=n4(col, d))
+    def taken(h, d):
+        return remote(panel_ref.at[h, n4(col, d)], arow.at[n4(col, -d), h], ps.at[h, d - 1], pr.at[h, d - 1], col=n4(col, d))
+    for h in range(2):
+        for d in (1, 3, 2):
+            take(h, d).start()
     each(0, 8, lambda c: arrived(c).start())
     each(2, 32, lambda s: fetch(s).start())
     loads[3].wait()
-    for d in (1, 3, 2):
-        taken(d).wait_recv()
-    for s in range(2):
-        for t in range(4):
-            a = arow[t, s]
-            h = a.astype(BF)
-            at = (4 * s + t) * 128
-            ah[:, at:at + 128] = h
-            al[:, at:at + 128] = (a - h.astype(F32)).astype(BF)
-    for copy in loads[:3]:
-        copy.wait()
     top = (group < 8) & (col == 0)
 
     def mm(x, y):
         return lax.dot_general(x, y, (((1,), (1,)), ((), ())), preferred_element_type=F32)
-    for b in range(4):
-        w = 256 * (b + 1)
-        rows = pl.ds(256 * b, 256)
-        y = mm(ah[:, 0:w], hi[rows, 0:w]) + (mm(ah[:, 0:w], lo[rows, 0:w]) + mm(al[:, 0:w], hi[rows, 0:w]))
-        y = jnp.where(top, low[:, 256 * b:w], y.astype(BF))
-        xb[row, :, 256 * b:w] = y
-        brow_ref[col, :, 256 * b:w] = y
+
+    def solve(h):
+        for d in (1, 3, 2):
+            taken(h, d).wait_recv()
+        for t in range(4):
+            v = arow[t, h]
+            u = v.astype(BF)
+            at = (4 * h + t) * 128
+            ah[:, at:at + 128] = u
+            al[:, at:at + 128] = (v - u.astype(F32)).astype(BF)
+        if h == 0:
+            for copy in loads[:3]:
+                copy.wait()
+        for b in (2 * h, 2 * h + 1):
+            w = 256 * (b + 1)
+            rows = pl.ds(256 * b, 256)
+            y = mm(ah[:, 0:w], hi[rows, 0:w]) + (mm(ah[:, 0:w], lo[rows, 0:w]) + mm(al[:, 0:w], hi[rows, 0:w]))
+            y = jnp.where(top, low[:, 256 * b:w], y.astype(BF))
+            at = 256 * (b - 2 * h)
+            xb[h, row, :, at:at + 256] = y
+            brow_ref[h, col, :, at:at + 256] = y
 
     half = [pl.ds(0, 64), pl.ds(64, 64)]
     step = [1, -1]
-    def xsend(i):
-        return remote(xb.at[row], xb.at[row], xs.at[i], xr.at[i], row=n4(row, step[i]))
-    def xrecv(i):
-        at = xb.at[n4(row, -step[i])]
-        return remote(at, at, xs.at[i], xr.at[i], row=n4(row, step[i]))
-    def xforward(i, r):
-        at = xb.at[r, half[i]]
-        return remote(at, at, xs.at[2 + i], xr.at[2 + i], row=n4(row, step[i]))
-    def wsend(i):
-        return remote(brow_ref.at[col], brow_ref.at[col], ws.at[i], wr.at[i], col=n4(col, step[i]))
-    def wrecv(i):
-        at = brow_ref.at[n4(col, -step[i])]
-        return remote(at, at, ws.at[i], wr.at[i], col=n4(col, step[i]))
-    def wforward(i, c):
-        at = brow_ref.at[c, half[i]]
-        return remote(at, at, ws.at[2 + i], wr.at[2 + i], col=n4(col, step[i]))
-
-    def ynear(i):
-        return remote(xb.at[n4(col, step[i])], bcol_ref.at[col, sub], ys.at[i], yr.at[i], col=n4(col, step[i]))
-    def ynear_in(i):
-        return remote(xb.at[0], bcol_ref.at[n4(col, -step[i]), sub], ys.at[i], yr.at[i], col=n4(col, step[i]))
-    def yfar(i):
-        return remote(xb.at[n4(col, 2), half[i]], rl.at[i], rs.at[i], rr.at[i], col=n4(col, step[i]))
-    def yrelay(i):
-        return remote(rl.at[i], bcol_ref.at[n4(col, -step[i]), sub, half[i]], ys.at[2 + i], yr.at[2 + i], col=n4(col, step[i]))
-    def yfar_in(i):
-        return remote(rl.at[i], bcol_ref.at[n4(col, 2), sub, half[i]], ys.at[2 + i], yr.at[2 + i], col=n4(col, step[i]))
-    home = pltpu.make_async_copy(xb.at[col], bcol_ref.at[col, sub], lsem.at[4])
-
-    def ysend(c):
+    def xsend(h, i):
+        return remote(xb.at[h, row], xb.at[h, row], xs.at[h, i], xr.at[h, i], row=n4(row, step[i]))
+    def xrecv(h, i):
+        at = xb.at[h, n4(row, -step[i])]
+        return remote(at, at, xs.at[h, i], xr.at[h, i], row=n4(row, step[i]))
+    def xforward(h, i, r):
+        at = xb.at[h, r, half[i]]
+        return remote(at, at, xs.at[h, 2 + i], xr.at[h, 2 + i], row=n4(row, step[i]))
+    def wsend(h, i):
+        return remote(brow_ref.at[h, col], brow_ref.at[h, col], ws.at[h, i], wr.at[h, i], col=n4(col, step[i]))
+    def wrecv(h, i):
+        at = brow_ref.at[h, n4(col, -step[i])]
+        return remote(at, at, ws.at[h, i], wr.at[h, i], col=n4(col, step[i]))
+    def wforward(h, i, c):
+        at = brow_ref.at[h, c, half[i]]
+        return remote(at, at, ws.at[h, 2 + i], wr.at[h, 2 + i], col=n4(col, step[i]))
+
+    def ynear(h, i):
+        return remote(xb.at[h, n4(col, step[i])], bcol_ref.at[h, col, sub], ys.at[h, i], yr.at[h, i], col=n4(col, step[i]))
+    def ynear_in(h, i):
+        return remote(xb.at[h, 0], bcol_ref.at[h, n4(col, -step[i]), sub], ys.at[h, i], yr.at[h, i], col=n4(col, step[i]))
+    def yfar(h, i):
+        return remote(xb.at[h, n4(col, 2), half[i]], rl.at[h, i], rs.at[h, i], rr.at[h, i], col=n4(col, step[i]))
+    def yrelay(h, i):
+        return remote(rl.at[h, i], bcol_ref.at[h, n4(col, -step[i]), sub, half[i]], ys.at[h, 2 + i], yr.at[h, 2 + i], col=n4(col, step[i]))
+    def yfar_in(h, i):
+        return remote(rl.at[h, i], bcol_ref.at[h, n4(col, 2), sub, half[i]], ys.at[h, 2 + i], yr.at[h, 2 + i], col=n4(col, step[i]))
+    def home(h):
+        return pltpu.make_async_copy(xb.at[h, col], bcol_ref.at[h, col, sub], lsem.at[4 + h])
+
+    def ysend(h, c):
         d = n4(c, -col)
         @pl.when(d == 0)
         def _():
-            home.start()
+            home(h).start()
         for i in range(2):
             @pl.when(d == (1, 3)[i])
             def _():
-                ynear(i).start()
+                ynear(h, i).start()
         @pl.when(d == 2)
         def _():
-            yfar(0).start()
-            yfar(1).start()
-
-    def own(e, i):
-        at = bcol_ref.at[n4(col, e), sub]
-        return remote(at if e else xb.at[col], at, zs.at[i, e], zr.at[i, e], sub=n8(sub, 2 * step[i]))
-    def arrive(e, i):
-        at = bcol_ref.at[n4(col, e), n8(sub, -2 * step[i])]
-        return remote(at, at, zs.at[i, e], zr.at[i, e], sub=n8(sub, 2 * step[i]))
+            yfar(h, 0).start()
+            yfar(h, 1).start()
+
+    def own(h, e, i):
+        at = bcol_ref.at[h, n4(col, e), sub]
+        return remote(at if e else xb.at[h, col], at, zs.at[h, i, e], zr.at[h, i, e], sub=n8(sub, 2 * step[i]))
+    def arrive(h, e, i):
+        at = bcol_ref.at[h, n4(col, e), n8(sub, -2 * step[i])]
+        return remote(at, at, zs.at[h, i, e], zr.at[h, i, e], sub=n8(sub, 2 * step[i]))
     side = [0, 0, 1, 1]
-    def onward(e, i, z):
-        at = bcol_ref.at[n4(col, e), n8(sub, z)]
-        return remote(at, at, fs.at[e], fr.at[e], sub=n8(sub, 2 * step[i]))
-    def swap(e, k, z):
-        at = bcol_ref.at[n4(col, e), n8(sub, z)]
-        return remote(at if k or e else xb.at[col], at, ms.at[k, e], mr.at[k, e], sub=mate)
-    def swapped(e, k, z):
-        at = bcol_ref.at[n4(col, e), n8(mate, z)]
-        return remote(at, at, ms.at[k, e], mr.at[k, e], sub=mate)
-
-    def launch(e):
-        own(e, 0).start()
-        own(e, 1).start()
-        swap(e, 0, 0).start()
+    def onward(h, e, i, z):
+        at = bcol_ref.at[h, n4(col, e), n8(sub, z)]
+        return remote(at, at, fs.at[h, e], fr.at[h, e], sub=n8(sub, 2 * step[i]))
+    def swap(h, e, k, z):
+        at = bcol_ref.at[h, n4(col, e), n8(sub, z)]
+        return remote(at if k or e else xb.at[h, col], at, ms.at[h, k, e], mr.at[h, k, e], sub=mate)
+    def swapped(h, e, k, z):
+        at = bcol_ref.at[h, n4(col, e), n8(mate, z)]
+        return remote(at, at, ms.at[h, k, e], mr.at[h, k, e], sub=mate)
+
+    def launch(h, e):
+        own(h, e, 0).start()
+        own(h, e, 1).start()
+        swap(h, e, 0, 0).start()
     apart = n4(col, -row)
 
     def gather(c):
@@ -400,79 +405,91 @@
         def _():
             settle(s)
             settle(s + 1)
-            y = mm(brow_ref[...].reshape(512, 1024), bcol_ref[q, pl.ds(z, 2)].reshape(256, 1024))
+            y = (mm(brow_ref[0].reshape(512, 512), bcol_ref[0, q, pl.ds(z, 2)].reshape(256, 512))
+                 + mm(brow_ref[1].reshape(512, 512), bcol_ref[1, q, pl.ds(z, 2)].reshape(256, 512)))
             for u in range(2):
                 t = y[:, u * 128:(u + 1) * 128].reshape(4, 128, 128)
                 acc_ref[s + u, 0] = acc_ref[s + u, 0] - keep * t[0]
                 acc_ref[s + u, 1:4] = acc_ref[s + u, 1:4] - t[1:4]
                 put(s + u).start()
 
-    def near():
-        ynear_in(1).wait_recv()
-        launch(1)
-        ynear_in(0).wait_recv()
-        launch(3)
-
-    def reach(d):
-        ysend(n4(row, d))
+    def near(h):
+        ynear_in(h, 1).wait_recv()
+        launch(h, 1)
+        ynear_in(h, 0).wait_recv()
+        launch(h, 3)
+
+    def reach(h, d):
+        ysend(h, n4(row, d))
         @pl.when(apart == d)
         def _():
-            launch(0)
-
-    for i in range(2):
-        xsend(i).start()
-    for i in range(2):
-        wsend(i).start()
-    reach(0)
+            launch(h, 0)
+
+    for h in range(2):
+        solve(h)
+        for i in range(2):
+            xsend(h, i).start()
+        for i in range(2):
+            wsend(h, i).start()
+        reach(h, 0)
     early(0).start()
     early(1).start()
     each(0, 8, lambda c: arrived(c).wait())
-    for c in range(5):
+    for c in range(3):
         gather(c)
-    for i in range(2):
-        xrecv(i).wait_recv()
-        xforward(i, n4(row, -step[i])).start()
-        reach(3 if i == 0 else 1)
-    for i in range(2):
-        wrecv(i).wait_recv()
-        wforward(i, n4(col, -step[i])).start()
+    for h in range(2):
+        for i in range(2):
+            xrecv(h, i).wait_recv()
+            xforward(h, i, n4(row, -step[i])).start()
+            reach(h, 3 if i == 0 else 1)
+        for i in range(2):
+            wrecv(h, i).wait_recv()
+            wforward(h, i, n4(col, -step[i])).start()
     @pl.when(apart == 0)
     def _():
-        near()
-    for c in range(5, 8):
+        near(0)
+        near(1)
+    for c in range(3, 8):
         gather(c)
-    for i in range(2):
-        xforward(i, n4(row, 2)).wait_recv()
-    reach(2)
+    for h in range(2):
+        for i in range(2):
+            xforward(h, i, n4(row, 2)).wait_recv()
+        reach(h, 2)
     each(2, 32, lambda s: fetch(s).wait())
-    for i in range(2):
-        yfar(i).wait_recv()
-        yrelay(i).start()
+    for h in range(2):
+        for i in range(2):
+            yfar(h, i).wait_recv()
+            yrelay(h, i).start()
     @pl.when(apart != 0)
     def _():
-        near()
-    yfar_in(0).wait_recv()
-    yfar_in(1).wait_recv()
-    launch(2)
-    for i in range(2):
-        wforward(i, n4(col, 2)).wait_recv()
-    home.wait()
+        near(0)
+        near(1)
+    for h in range(2):
+        yfar_in(h, 0).wait_recv()
+        yfar_in(h, 1).wait_recv()
+        launch(h, 2)
+    for h in range(2):
+        for i in range(2):
+            wforward(h, i, n4(col, 2)).wait_recv()
+        home(h).wait()
 
     def gray(k):
         return k + jnp.where(k == 2, 1, 0) - jnp.where(k == 3, 1, 0)
 
     def product(e, k, z):
-        swapped(e, k, z).wait_recv()
+        for h in range(2):
+            swapped(h, e, k, z).wait_recv()
         update(e, z)
 
     def pass_on(k, carry):
         e = gray(k)
-        for i in range(2):
-            arrive(e, i).wait_recv()
-            @pl.when((e < 2) if i == 0 else (e >= 2))
-            def _():
-                onward(e, i, -2 * step[i]).start()
-            swap(e, 1 + i, -2 * step[i]).start()
+        for h in range(2):
+            for i in range(2):
+                arrive(h, e, i).wait_recv()
+                @pl.when((e < 2) if i == 0 else (e >= 2))
+                def _():
+                    onward(h, e, i, -2 * step[i]).start()
+                swap(h, e, 1 + i, -2 * step[i]).start()
 
         def three(j, c):
             @pl.when((j == 0) | (k > 0))
@@ -484,15 +501,16 @@
     lax.fori_loop(0, 4, pass_on, 0)
 
     for q in range(4):
-        pair = [brow_ref[q, :, pl.ds(pl.multiple_of((4 * s + col) * 128, 128), 128)] for s in range(2)]
+        pair = [brow_ref[s, q, :, pl.ds(pl.multiple_of(col * 128, 128), 128)] for s in range(2)]
         pout_ref[q] = jnp.stack([x.astype(F32) for x in pair], 1).astype(BF)
 
     def last(k, carry):
         @pl.when(k < 4)
         def _():
             e = gray(k)
-            onward(e, 0, 4).wait_recv()
-            swap(e, 3, 4).start()
+            for h in range(2):
+                onward(h, e, 0, 4).wait_recv()
+                swap(h, e, 3, 4).start()
 
         def two(j, c):
             @pl.when((j == 0) | (k == 0))
@@ -506,24 +524,25 @@
     early(1).wait()
     each(2, 32, lambda s: put(s).wait())
 
-    for d in (1, 2, 3):
-        take(d).wait_send()
-    for i in range(2):
-        xsend(i).wait_send()
-        wsend(i).wait_send()
-        xforward(i, n4(row, -step[i])).wait_send()
-        wforward(i, n4(col, -step[i])).wait_send()
-        ynear(i).wait_send()
-        yfar(i).wait_send()
-        yrelay(i).wait_send()
-    for e in range(4):
-        own(e, 0).wait_send()
-        own(e, 1).wait_send()
-        onward(e, side[e], -2 * step[side[e]]).wait_send()
-        swap(e, 0, 0).wait_send()
-        swap(e, 1, -2).wait_send()
-        swap(e, 2, 2).wait_send()
-        swap(e, 3, 4).wait_send()
+    for h in range(2):
+        for d in (1, 2, 3):
+            take(h, d).wait_send()
+        for i in range(2):
+            xsend(h, i).wait_send()
+            wsend(h, i).wait_send()
+            xforward(h, i, n4(row, -step[i])).wait_send()
+            wforward(h, i, n4(col, -step[i])).wait_send()
+            ynear(h, i).wait_send()
+            yfar(h, i).wait_send()
+            yrelay(h, i).wait_send()
+        for e in range(4):
+            own(h, e, 0).wait_send()
+            own(h, e, 1).wait_send()
+            onward(h, e, side[e], -2 * step[side[e]]).wait_send()
+            swap(h, e, 0, 0).wait_send()
+            swap(h, e, 1, -2).wait_send()
+            swap(h, e, 2, 2).wait_send()
+            swap(h, e, 3, 4).wait_send()
 
 
 def panel_exchange(order, panel, hi, lo, low, front, arrived):
@@ -534,12 +553,11 @@
         out_shape=(jax.ShapeDtypeStruct((4, 1, 128, 32, 1, 128), F32), jax.ShapeDtypeStruct((4, 128, 2, 128), BF)),
         in_specs=[pl.BlockSpec(memory_space=pltpu.SMEM), pl.BlockSpec(memory_space=V)] + [pl.BlockSpec(memory_space=H)] * 5,
         out_specs=(pl.BlockSpec(memory_space=H), pl.BlockSpec(memory_space=V)),
-        scratch_shapes=[V((4, 128, 1024), BF), V((4, 8, 128, 1024), BF), V((32, 4, 128, 128), F32), V((256, 128, 128), BF),
+        scratch_shapes=[V((2, 4, 128, 512), BF), V((2, 4, 8, 128, 512), BF), V((32, 4, 128, 128), F32), V((256, 128, 128), BF),
                         V((256, 128, 128), F32), V((4, 2, 128, 128), F32), V((128, 1024), BF), V((128, 1024), BF),
                         V((1024, 1024), BF), V((1024, 1024), BF),
-                        V((128, 1024), BF), V((4, 128, 1024), BF), V((2, 64, 1024), BF), D((32,)), D((8,)), D((32,)),
-                        D((5,)), D((3,)), D((3,)), D((4,)), D((4,)), D((4,)), D((4,)), D((4,)), D((4,)), D((2,)), D((2,)),
-                        D((2, 4)), D((2, 4)), D((4,)), D((4,)), D((4, 4)), D((4, 4))],
+                        V((128, 1024), BF), V((2, 4, 128, 512), BF), V((2, 2, 64, 512), BF), D((32,)), D((8,)), D((32,)), D((6,))]
+        + [D((2, 3))] * 2 + [D((2, 4))] * 6 + [D((2, 2))] * 2 + [D((2, 2, 4))] * 2 + [D((2, 4))] * 2 + [D((2, 4, 4))] * 2,
         compiler_params=pltpu.CompilerParams(vmem_limit_bytes=60 << 20, collective_id=2, has_side_effects=True),
         name="panel",
     )(order, panel, hi, lo, low, front, arrived)

time: 228 us -> 226 us (level)
  the two profiles are of different devices: /device:TPU:26 before, /device:TPU:6 now
where the time goes in v8:
time: 226 us
  Pallas kernels  174 us (77%)
  waiting for transfers between devices  17.9 us (8%)
  local copies, waits for them, and re-layouts  16.6 us (7%)
  starting transfers between devices  15.3 us (7%)
    pallas_call x1, Pallas kernels, chol(): pl.pallas_call(chol_kernel, out_shape=[jax.ShapeDtypeStruct((1024, 1024),...  72.5 us
    pallas_call x1, Pallas kernels, panel_exchange(): pl.pallas_call(panel_kernel, out_shape=(jax.ShapeDtypeStruct((4, 1, 128,...  69 us
    pallas_call x1, Pallas kernels, lead_gather(): pl.pallas_call(lead_kernel, out_shape=(jax.ShapeDtypeStruct((8, 8, 128, 1...  26.8 us
    all_to_all x1, waiting for transfers between devices, local(): lax.all_to_all(outgoing, ('sub', 'row', 'col'), split_axis=0, concat_axis...  17.9 us
    all_to_all x1, starting transfers between devices, local(): lax.all_to_all(outgoing, ('sub', 'row', 'col'), split_axis=0, concat_axis...  15.3 us
    unnamed x14, local copies, waits for them, and re-layouts  13.8 us
  transfers between devices with their start and end apart: 1, of which 1 were waited for; matrix products, arithmetic and copies ran while one was open for 2% of the time, Pallas kernels for 33%

profile of v8, /device:TPU:6, one launch (start us, length us, event | category | flops | bytes accessed | tf_op | source)
XLA Modules:
  0.0 225.6 jit_solution(16353532812101009207)
XLA Ops:
  0.6 1.4 index.1
  2.0 26.8 %lead.1 = (f32[8,8,128,128]{3,2,1,0:T(8,128)}, s32[4,4,8,1,128]{4,3,2,1,0:T(1,128)}, bf16[128,2,128,128]{3,2,1,0:T(8,128)(2,1)}) custom-call(s32[2,128]{1,0:T(2,128)} %get-tuple-element.12.idx_ref, f32[4,1,128,32,1,128]{5,4,3,2,1,0:T(1,128)} %front_ref.5, s32[1,128]{1,0:T(1,128)} %get-tuple-element.13.code_ref, bf16[128,128,128]{2,1,0:T(8,128)(2,1)} %child_ref.1), custom_call_target="tpu_custom_call" | custom-call | tf_op jit(solution)/shard_map/lead/pallas_call | solution.py:768
  28.8 0.0 copy-start.5
  28.8 15.3 %all-to-all-start = ((bf16[128,2,128,128]{3,2,1,0:T(8,128)(2,1)}), bf16[128,2,128,128]{3,2,1,0:T(8,128)(2,1)}, u32[]{:S(2)}, u32[]{:S(2)}) async-start(bf16[128,2,128,128]{3,2,1,0:T(8,128)(2,1)} %get-tuple-element.15), calls=%async_computation | async-start | bytes 16777216 | tf_op jit(solution)/shard_map/all_to_all | solution.py:800
  44.1 0.0 copy-done.5
  44.1 0.6 select_reduce_fusion
  44.8 0.1 copy.15
  44.9 0.1 reduce_min.12
  45.0 0.1 copy.14
  45.1 0.1 reduce_max.12
  45.2 0.1 copy.16
  45.4 0.7 reshape.172.land_ref
  46.1 0.7 reshape_reshape.7.row_ref
  46.8 0.7 reshape_reshape.8.col_ref
  47.5 0.0 copy-start
  47.5 2.2 copy-done
  49.7 72.5 %chol.1 = (bf16[1024,1024]{1,0:T(8,128)(2,1)S(1)}, bf16[1024,1024]{1,0:T(8,128)(2,1)S(1)}, bf16[1024,1024]{1,0:T(8,128)(2,1)S(1)}) custom-call(f32[8,8,128,128]{3,2,1,0:T(8,128)S(1)} %copy-done), custom_call_target="tpu_custom_call" | custom-call | tf_op jit(solution)/shard_map/chol/pallas_call | solution.py:112
  122.2 0.0 copy-start.1
  122.2 1.3 copy-done.1
  123.5 0.0 copy-start.2
  123.5 1.3 copy-done.2
  124.8 0.0 copy-start.3
  124.8 1.3 copy-done.3
  126.2 1.8 plan.1.list_ref.order_ref
  128.0 17.9 %all-to-all-done = bf16[128,2,128,128]{3,2,1,0:T(8,128)(2,1)} async-done(((bf16[128,2,128,128]{3,2,1,0:T(8,128)(2,1)}), bf16[128,2,128,128]{3,2,1,0:T(8,128)(2,1)}, u32[]{:S(2)}, u32[]{:S(2)}) %all-to-all-start) | async-done | bytes 8388640 | tf_op jit(solution)/shard_map/all_to_all | solution.py:800
  145.9 2.9 %head.1.panel_ref = f32[2,4,128,128]{3,2,1,0:T(8,128)} custom-call(s32[256]{0:T(256)} %reshape.172.land_ref, s32[5,256]{1,0:T(8,128)} %plan.1.list_ref.order_ref, f32[4,1,128,32,1,128]{5,4,3,2,1,0:T(1,128)} %front_ref.5, bf16[256,128,128]{2,1,0:T(8,128)(2,1)} %bitcast.5.arr_ref), custom_call_target="tpu_custom_call" | custom-call | tf_op jit(solution)/shard_map/head/pallas_call | solution.py:222
  148.9 69.0 %panel.1 = (f32[4,1,128,32,1,128]{5,4,3,2,1,0:T(1,128)}, bf16[4,128,2,128]{3,2,1,0:T(2,128)(2,1)}) custom-call(s32[5,256]{1,0:T(8,128)} %plan.1.list_ref.order_ref, f32[2,4,128,128]{3,2,1,0:T(8,128)} %head.1.panel_ref, bf16[1024,1024]{1,0:T(8,128)(2,1)} %copy-done.2, bf16[1024,1024]{1,0:T(8,128)(2,1)} %copy-done.3, bf16[1024,1024]{1,0:T(8,128)(2,1)} %copy-done.1, ...), custom_call_target="tpu_custom_call" | custom-call | tf_op jit(solution)/shard_map/panel/pallas_call | solution.py:551
  217.9 0.0 copy-start.4
  217.9 7.0 %copy.23 = f32[4,1,128,32,1,128]{5,4,3,2,1,0:T(1,128)} copy(f32[4,1,128,32,1,128]{5,4,3,2,1,0:T(1,128)} %get-tuple-element.34) | data formatting | bytes 16777216
  224.9 0.0 copy-done.4
  224.9 0.7 copy.24
  (3 shorter events, 0.0 us)
Async XLA Ops:
  28.8 15.4 %copy-start.5 = (s32[4,4,8,1,128]{4,3,2,1,0:T(1,128)S(1)}, s32[4,4,8,1,128]{4,3,2,1,0:T(1,128)}, u32[]{:S(2)}) copy-start(s32[4,4,8,1,128]{4,3,2,1,0:T(1,128)} %get-tuple-element.14) | copy-start | bytes 196612
  28.8 117.1 %all-to-all-start = ((bf16[128,2,128,128]{3,2,1,0:T(8,128)(2,1)}), bf16[128,2,128,128]{3,2,1,0:T(8,128)(2,1)}, u32[]{:S(2)}, u32[]{:S(2)}) async-start(bf16[128,2,128,128]{3,2,1,0:T(8,128)(2,1)} %get-tuple-element.15), calls=%async_computation | async-start | bytes 16777216 | tf_op jit(solution)/shard_map/all_to_all | solution.py:800
  47.5 2.2 copy-start
  122.2 1.3 copy-start.1
  123.5 1.3 copy-start.2
  124.8 1.3 copy-start.3
  217.9 7.0 %copy-start.4 = (bf16[4,128,2,128]{3,2,1,0:T(2,128)(2,1)S(1)}, bf16[4,128,2,128]{3,2,1,0:T(2,128)(2,1)}, u32[]{:S(2)}) copy-start(bf16[4,128,2,128]{3,2,1,0:T(2,128)(2,1)} %get-tuple-element.21) | copy-start | bytes 786436

commit v9 on v8

--- a/solution.py
+++ b/solution.py
@@ -563,7 +563,7 @@
     )(order, panel, hi, lo, low, front, arrived)
 
 
-def lead_kernel(idx_ref, front_ref, code_ref, child_ref, lead_ref, codes_ref, sent_ref, own_ref, tile_ref, pack_ref, tsem, psem, lsem, zs, zr, zls, zlr, xs, xr, ys, yr, as_, ar, bs, br, cas, car, cbs, cbr):
+def lead_kernel(idx_ref, front_ref, code_ref, child_ref, lead_ref, codes_ref, sent_ref, own_ref, tile_ref, pack_ref, tsem, psem, lsem, zs, zr, zls, zlr, xs, xr, ys, yr, as_, ar, bs, br, cas, car, cbs, cbr, afs, afr, bfs, bfr):
     sub, row, col = lax.axis_index("sub"), lax.axis_index("row"), lax.axis_index("col")
     par = lax.rem(sub, 2)
     mate = sub + 1 - 2 * par
@@ -677,7 +677,7 @@
         @pl.when(lax.rem(col + 4 - d, 4) <= row)
         def _():
             by(d, lax.rem(col + 4 - d, 4)).wait_recv()
-    for d in (1, 3, 2):
+    for d in (1, 3):
         @pl.when(par == 1)
         def _():
             ay(d, col).start()
@@ -685,6 +685,12 @@
             @pl.when(c <= row)
             def _():
                 bx(d, row, c).start()
+    def ay2(i, c):
+        at = lead_ref.at[pl.ds(4 + 2 * i, 2), c]
+        return remote(at, at, afs.at[i], afr.at[i], col=lax.rem(col + (1, 3)[i], 4))
+    def bx2(r, c):
+        at = lead_ref.at[4 * par + r, 4 * par + c]
+        return remote(at, at, bfs.at[c], bfr.at[c], row=lax.rem(row + (1, 3)[c // 2], 4))
 
     def swap_a(c):
         at = lead_ref.at[pl.ds(4, 4), c]
@@ -707,16 +713,30 @@
         cx(d, lax.rem(row + 4 - d, 4)).wait_recv()
     for d in range(1, 4):
         cy(d, col).start()
-    for d in (1, 3, 2):
+    for i in range(2):
+        d = (1, 3)[i]
         r = lax.rem(row + 4 - d, 4)
         @pl.when(par == 1)
         def _():
             ay(d, lax.rem(col + 4 - d, 4)).wait_recv()
+            ay2(i, lax.rem(col + 4 - d, 4)).start()
         for c in range(4):
             @pl.when(c <= r)
             def _():
                 bx(d, r, c).wait_recv()
+                if c // 2 == i:
+                    bx2(r, c).start()
         hand(r, lax.rem(col + 4 - d, 4))
+    across, beyond = lax.rem(row + 2, 4), lax.rem(col + 2, 4)
+    @pl.when(par == 1)
+    def _():
+        for i in range(2):
+            ay2(i, beyond).wait_recv()
+    for c in range(4):
+        @pl.when(c <= across)
+        def _():
+            bx2(across, c).wait_recv()
+    hand(across, beyond)
     @pl.when(par == 0)
     def _():
         for c in range(4):
@@ -744,14 +764,24 @@
         @pl.when(par == 1)
         def _():
             ax(d, row).wait_send()
+        @pl.when(col <= row)
+        def _():
+            by(d, col).wait_send()
+    for i in range(2):
+        d = (1, 3)[i]
+        r = lax.rem(row + 4 - d, 4)
+        @pl.when(par == 1)
+        def _():
             ay(d, col).wait_send()
-        @pl.when(col <= row)
-        def _():
-            by(d, col).wait_send()
+            ay2(i, lax.rem(col + 4 - d, 4)).wait_send()
         for c in range(4):
             @pl.when(c <= row)
             def _():
                 bx(d, row, c).wait_send()
+        for c in (2 * i, 2 * i + 1):
+            @pl.when(c <= r)
+            def _():
+                bx2(r, c).wait_send()
     @pl.when(par == 1)
     def _():
         for c in range(4):
@@ -773,7 +803,7 @@
                   pl.BlockSpec(memory_space=pltpu.HBM)],
         out_specs=(pl.BlockSpec(memory_space=V), pl.BlockSpec(memory_space=V), pl.BlockSpec(memory_space=pltpu.HBM)),
         scratch_shapes=[V((2, 128, 128), F32), V((128, 128, 128), BF), V((128, 2, 128, 128), BF), D((4,)), D((8,)), D((5,)), D((7,)), D((7,)), D((3, 2)), D((2,)), D((3,)), D((3,)), D((3,)), D((3,)),
-                        D((2, 3)), D((2, 3)), D((3, 5)), D((3, 5)), D((4,)), D((4,)), D((4, 4)), D((4, 4))],
+                        D((2, 3)), D((2, 3)), D((3, 5)), D((3, 5)), D((4,)), D((4,)), D((4, 4)), D((4, 4)), D((2,)), D((2,)), D((4,)), D((4,))],
         compiler_params=pltpu.CompilerParams(vmem_limit_bytes=60 << 20, collective_id=1, has_side_effects=True),
         name="lead",
     )(idx, front, code, child)

time: 226 us -> 224 us (level)
  no operation moved by 1% of the time
where the time goes in v9:
time: 224 us
  Pallas kernels  173 us (77%)
  waiting for transfers between devices  17.9 us (8%)
  local copies, waits for them, and re-layouts  16.6 us (7%)
  starting transfers between devices  14.9 us (7%)
    pallas_call x1, Pallas kernels, chol(): pl.pallas_call(chol_kernel, out_shape=[jax.ShapeDtypeStruct((1024, 1024),...  72.5 us
    pallas_call x1, Pallas kernels, panel_exchange(): pl.pallas_call(panel_kernel, out_shape=(jax.ShapeDtypeStruct((4, 1, 128,...  69 us
    pallas_call x1, Pallas kernels, lead_gather(): pl.pallas_call(lead_kernel, out_shape=(jax.ShapeDtypeStruct((8, 8, 128, 1...  25 us
    all_to_all x1, waiting for transfers between devices, local(): lax.all_to_all(outgoing, ('sub', 'row', 'col'), split_axis=0, concat_axis...  17.9 us
    all_to_all x1, starting transfers between devices, local(): lax.all_to_all(outgoing, ('sub', 'row', 'col'), split_axis=0, concat_axis...  14.9 us
    unnamed x14, local copies, waits for them, and re-layouts  13.8 us
  transfers between devices with their start and end apart: 1, of which 1 were waited for; matrix products, arithmetic and copies ran while one was open for 2% of the time, Pallas kernels for 33%

profile of v9, /device:TPU:6, one launch (start us, length us, event | category | flops | bytes accessed | tf_op | source)
XLA Modules:
  0.0 223.5 jit_solution(15353101754529412926)
XLA Ops:
  0.6 1.4 index.1
  2.0 25.0 %lead.1 = (f32[8,8,128,128]{3,2,1,0:T(8,128)}, s32[4,4,8,1,128]{4,3,2,1,0:T(1,128)}, bf16[128,2,128,128]{3,2,1,0:T(8,128)(2,1)}) custom-call(s32[2,128]{1,0:T(2,128)} %get-tuple-element.12.idx_ref, f32[4,1,128,32,1,128]{5,4,3,2,1,0:T(1,128)} %front_ref.5, s32[1,128]{1,0:T(1,128)} %get-tuple-element.13.code_ref, bf16[128,128,128]{2,1,0:T(8,128)(2,1)} %child_ref.1), custom_call_target="tpu_custom_call" | custom-call | tf_op jit(solution)/shard_map/lead/pallas_call | solution.py:798
  27.0 0.0 copy-start.5
  27.0 14.9 %all-to-all-start = ((bf16[128,2,128,128]{3,2,1,0:T(8,128)(2,1)}), bf16[128,2,128,128]{3,2,1,0:T(8,128)(2,1)}, u32[]{:S(2)}, u32[]{:S(2)}) async-start(bf16[128,2,128,128]{3,2,1,0:T(8,128)(2,1)} %get-tuple-element.15), calls=%async_computation | async-start | bytes 16777216 | tf_op jit(solution)/shard_map/all_to_all | solution.py:830
  42.0 0.0 copy-done.5
  42.0 0.6 select_reduce_fusion
  42.7 0.1 copy.15
  42.8 0.1 reduce_min.12
  42.9 0.1 copy.14
  43.0 0.1 reduce_max.12
  43.1 0.1 copy.16
  43.2 0.7 reshape.172.land_ref
  43.9 0.7 reshape_reshape.7.row_ref
  44.7 0.7 reshape_reshape.8.col_ref
  45.4 0.0 copy-start
  45.4 2.2 copy-done
  47.6 72.5 %chol.1 = (bf16[1024,1024]{1,0:T(8,128)(2,1)S(1)}, bf16[1024,1024]{1,0:T(8,128)(2,1)S(1)}, bf16[1024,1024]{1,0:T(8,128)(2,1)S(1)}) custom-call(f32[8,8,128,128]{3,2,1,0:T(8,128)S(1)} %copy-done), custom_call_target="tpu_custom_call" | custom-call | tf_op jit(solution)/shard_map/chol/pallas_call | solution.py:112
  120.1 0.0 copy-start.1
  120.1 1.3 copy-done.1
  121.4 0.0 copy-start.2
  121.4 1.3 copy-done.2
  122.7 0.0 copy-start.3
  122.7 1.3 copy-done.3
  124.1 1.8 plan.1.list_ref.order_ref
  125.9 17.9 %all-to-all-done = bf16[128,2,128,128]{3,2,1,0:T(8,128)(2,1)} async-done(((bf16[128,2,128,128]{3,2,1,0:T(8,128)(2,1)}), bf16[128,2,128,128]{3,2,1,0:T(8,128)(2,1)}, u32[]{:S(2)}, u32[]{:S(2)}) %all-to-all-start) | async-done | bytes 8388640 | tf_op jit(solution)/shard_map/all_to_all | solution.py:830
  143.8 2.9 %head.1.panel_ref = f32[2,4,128,128]{3,2,1,0:T(8,128)} custom-call(s32[256]{0:T(256)} %reshape.172.land_ref, s32[5,256]{1,0:T(8,128)} %plan.1.list_ref.order_ref, f32[4,1,128,32,1,128]{5,4,3,2,1,0:T(1,128)} %front_ref.5, bf16[256,128,128]{2,1,0:T(8,128)(2,1)} %bitcast.5.arr_ref), custom_call_target="tpu_custom_call" | custom-call | tf_op jit(solution)/shard_map/head/pallas_call | solution.py:222
  146.7 69.0 %panel.1 = (f32[4,1,128,32,1,128]{5,4,3,2,1,0:T(1,128)}, bf16[4,128,2,128]{3,2,1,0:T(2,128)(2,1)}) custom-call(s32[5,256]{1,0:T(8,128)} %plan.1.list_ref.order_ref, f32[2,4,128,128]{3,2,1,0:T(8,128)} %head.1.panel_ref, bf16[1024,1024]{1,0:T(8,128)(2,1)} %copy-done.2, bf16[1024,1024]{1,0:T(8,128)(2,1)} %copy-done.3, bf16[1024,1024]{1,0:T(8,128)(2,1)} %copy-done.1, ...), custom_call_target="tpu_custom_call" | custom-call | tf_op jit(solution)/shard_map/panel/pallas_call | solution.py:551
  215.8 0.0 copy-start.4
  215.8 7.0 %copy.23 = f32[4,1,128,32,1,128]{5,4,3,2,1,0:T(1,128)} copy(f32[4,1,128,32,1,128]{5,4,3,2,1,0:T(1,128)} %get-tuple-element.34) | data formatting | bytes 16777216
  222.8 0.0 copy-done.4
  222.8 0.7 copy.24
  (3 shorter events, 0.0 us)
Async XLA Ops:
  27.0 15.0 %copy-start.5 = (s32[4,4,8,1,128]{4,3,2,1,0:T(1,128)S(1)}, s32[4,4,8,1,128]{4,3,2,1,0:T(1,128)}, u32[]{:S(2)}) copy-start(s32[4,4,8,1,128]{4,3,2,1,0:T(1,128)} %get-tuple-element.14) | copy-start | bytes 196612
  27.0 116.7 %all-to-all-start = ((bf16[128,2,128,128]{3,2,1,0:T(8,128)(2,1)}), bf16[128,2,128,128]{3,2,1,0:T(8,128)(2,1)}, u32[]{:S(2)}, u32[]{:S(2)}) async-start(bf16[128,2,128,128]{3,2,1,0:T(8,128)(2,1)} %get-tuple-element.15), calls=%async_computation | async-start | bytes 16777216 | tf_op jit(solution)/shard_map/all_to_all | solution.py:830
  45.4 2.2 copy-start
  120.1 1.3 copy-start.1
  121.4 1.3 copy-start.2
  122.7 1.3 copy-start.3
  215.8 7.0 %copy-start.4 = (bf16[4,128,2,128]{3,2,1,0:T(2,128)(2,1)S(1)}, bf16[4,128,2,128]{3,2,1,0:T(2,128)(2,1)}, u32[]{:S(2)}) copy-start(bf16[4,128,2,128]{3,2,1,0:T(2,128)(2,1)} %get-tuple-element.21) | copy-start | bytes 786436

commit v10 on v9

--- a/solution.py
+++ b/solution.py
@@ -434,32 +434,33 @@
         reach(h, 0)
     early(0).start()
     early(1).start()
-    each(0, 8, lambda c: arrived(c).wait())
-    for c in range(3):
-        gather(c)
     for h in range(2):
         for i in range(2):
             xrecv(h, i).wait_recv()
             xforward(h, i, n4(row, -step[i])).start()
             reach(h, 3 if i == 0 else 1)
+        if h == 0:
+            each(0, 8, lambda c: arrived(c).wait())
+            gather(0)
+    for h in range(2):
         for i in range(2):
             wrecv(h, i).wait_recv()
             wforward(h, i, n4(col, -step[i])).start()
+    gather(1)
     @pl.when(apart == 0)
     def _():
         near(0)
         near(1)
-    for c in range(3, 8):
-        gather(c)
     for h in range(2):
         for i in range(2):
             xforward(h, i, n4(row, 2)).wait_recv()
         reach(h, 2)
-    each(2, 32, lambda s: fetch(s).wait())
+        gather(2 + h)
     for h in range(2):
         for i in range(2):
             yfar(h, i).wait_recv()
             yrelay(h, i).start()
+    gather(4)
     @pl.when(apart != 0)
     def _():
         near(0)
@@ -468,6 +469,9 @@
         yfar_in(h, 0).wait_recv()
         yfar_in(h, 1).wait_recv()
         launch(h, 2)
+    for c in range(5, 8):
+        gather(c)
+    each(2, 32, lambda s: fetch(s).wait())
     for h in range(2):
         for i in range(2):
             wforward(h, i, n4(col, 2)).wait_recv()
@@ -707,7 +711,7 @@
             def _():
                 swap_b(par, r, u).start()
     hand(row, col)
-    for g in range(4, 8):
+    for g in range(4, 6):
         pack(g)
     for d in range(1, 4):
         cx(d, lax.rem(row + 4 - d, 4)).wait_recv()
@@ -737,6 +741,8 @@
         def _():
             bx2(across, c).wait_recv()
     hand(across, beyond)
+    for g in range(6, 8):
+        pack(g)
     @pl.when(par == 0)
     def _():
         for c in range(4):

time: 224 us -> 223 us (level)
  no operation moved by 1% of the time
where the time goes in v10:
time: 223 us; the launch traced here: 222 us
  Pallas kernels  171 us (77%)
  waiting for transfers between devices  17.9 us (8%)
  local copies, waits for them, and re-layouts  16.6 us (7%)
  starting transfers between devices  14.9 us (7%)
    pallas_call x1, Pallas kernels, chol(): pl.pallas_call(chol_kernel, out_shape=[jax.ShapeDtypeStruct((1024, 1024),...  72.5 us
    pallas_call x1, Pallas kernels, panel_exchange(): pl.pallas_call(panel_kernel, out_shape=(jax.ShapeDtypeStruct((4, 1, 128,...  67.6 us
    pallas_call x1, Pallas kernels, lead_gather(): pl.pallas_call(lead_kernel, out_shape=(jax.ShapeDtypeStruct((8, 8, 128, 1...  25 us
    all_to_all x1, waiting for transfers between devices, local(): lax.all_to_all(outgoing, ('sub', 'row', 'col'), split_axis=0, concat_axis...  17.9 us
    all_to_all x1, starting transfers between devices, local(): lax.all_to_all(outgoing, ('sub', 'row', 'col'), split_axis=0, concat_axis...  14.9 us
    unnamed x14, local copies, waits for them, and re-layouts  13.8 us
  transfers between devices with their start and end apart: 1, of which 1 were waited for; matrix products, arithmetic and copies ran while one was open for 2% of the time, Pallas kernels for 33%

profile of v10, /device:TPU:6, one launch (start us, length us, event | category | flops | bytes accessed | tf_op | source)
XLA Modules:
  0.0 222.0 jit_solution(2861454749590398465)
XLA Ops:
  0.6 1.4 index.1
  2.0 25.0 %lead.1 = (f32[8,8,128,128]{3,2,1,0:T(8,128)}, s32[4,4,8,1,128]{4,3,2,1,0:T(1,128)}, bf16[128,2,128,128]{3,2,1,0:T(8,128)(2,1)}) custom-call(s32[2,128]{1,0:T(2,128)} %get-tuple-element.12.idx_ref, f32[4,1,128,32,1,128]{5,4,3,2,1,0:T(1,128)} %front_ref.5, s32[1,128]{1,0:T(1,128)} %get-tuple-element.13.code_ref, bf16[128,128,128]{2,1,0:T(8,128)(2,1)} %child_ref.1), custom_call_target="tpu_custom_call" | custom-call | tf_op jit(solution)/shard_map/lead/pallas_call | solution.py:804
  27.0 0.0 copy-start.5
  27.0 14.9 %all-to-all-start = ((bf16[128,2,128,128]{3,2,1,0:T(8,128)(2,1)}), bf16[128,2,128,128]{3,2,1,0:T(8,128)(2,1)}, u32[]{:S(2)}, u32[]{:S(2)}) async-start(bf16[128,2,128,128]{3,2,1,0:T(8,128)(2,1)} %get-tuple-element.15), calls=%async_computation | async-start | bytes 16777216 | tf_op jit(solution)/shard_map/all_to_all | solution.py:836
  42.0 0.0 copy-done.5
  42.0 0.6 select_reduce_fusion
  42.7 0.1 copy.15
  42.8 0.1 reduce_min.12
  42.9 0.1 copy.14
  43.0 0.1 reduce_max.12
  43.1 0.1 copy.16
  43.2 0.7 reshape.172.land_ref
  43.9 0.7 reshape_reshape.7.row_ref
  44.7 0.7 reshape_reshape.8.col_ref
  45.4 0.0 copy-start
  45.4 2.2 copy-done
  47.6 72.5 %chol.1 = (bf16[1024,1024]{1,0:T(8,128)(2,1)S(1)}, bf16[1024,1024]{1,0:T(8,128)(2,1)S(1)}, bf16[1024,1024]{1,0:T(8,128)(2,1)S(1)}) custom-call(f32[8,8,128,128]{3,2,1,0:T(8,128)S(1)} %copy-done), custom_call_target="tpu_custom_call" | custom-call | tf_op jit(solution)/shard_map/chol/pallas_call | solution.py:112
  120.1 0.0 copy-start.1
  120.1 1.3 copy-done.1
  121.4 0.0 copy-start.2
  121.4 1.3 copy-done.2
  122.7 0.0 copy-start.3
  122.7 1.3 copy-done.3
  124.1 1.8 plan.1.list_ref.order_ref
  125.9 17.9 %all-to-all-done = bf16[128,2,128,128]{3,2,1,0:T(8,128)(2,1)} async-done(((bf16[128,2,128,128]{3,2,1,0:T(8,128)(2,1)}), bf16[128,2,128,128]{3,2,1,0:T(8,128)(2,1)}, u32[]{:S(2)}, u32[]{:S(2)}) %all-to-all-start) | async-done | bytes 8388640 | tf_op jit(solution)/shard_map/all_to_all | solution.py:836
  143.8 2.9 %head.1.panel_ref = f32[2,4,128,128]{3,2,1,0:T(8,128)} custom-call(s32[256]{0:T(256)} %reshape.172.land_ref, s32[5,256]{1,0:T(8,128)} %plan.1.list_ref.order_ref, f32[4,1,128,32,1,128]{5,4,3,2,1,0:T(1,128)} %front_ref.5, bf16[256,128,128]{2,1,0:T(8,128)(2,1)} %bitcast.5.arr_ref), custom_call_target="tpu_custom_call" | custom-call | tf_op jit(solution)/shard_map/head/pallas_call | solution.py:222
  146.7 67.6 %panel.1 = (f32[4,1,128,32,1,128]{5,4,3,2,1,0:T(1,128)}, bf16[4,128,2,128]{3,2,1,0:T(2,128)(2,1)}) custom-call(s32[5,256]{1,0:T(8,128)} %plan.1.list_ref.order_ref, f32[2,4,128,128]{3,2,1,0:T(8,128)} %head.1.panel_ref, bf16[1024,1024]{1,0:T(8,128)(2,1)} %copy-done.2, bf16[1024,1024]{1,0:T(8,128)(2,1)} %copy-done.3, bf16[1024,1024]{1,0:T(8,128)(2,1)} %copy-done.1, ...), custom_call_target="tpu_custom_call" | custom-call | tf_op jit(solution)/shard_map/panel/pallas_call | solution.py:555
  214.3 0.0 copy-start.4
  214.3 7.0 %copy.23 = f32[4,1,128,32,1,128]{5,4,3,2,1,0:T(1,128)} copy(f32[4,1,128,32,1,128]{5,4,3,2,1,0:T(1,128)} %get-tuple-element.34) | data formatting | bytes 16777216
  221.3 0.0 copy-done.4
  221.3 0.7 copy.24
  (3 shorter events, 0.0 us)
Async XLA Ops:
  27.0 15.0 %copy-start.5 = (s32[4,4,8,1,128]{4,3,2,1,0:T(1,128)S(1)}, s32[4,4,8,1,128]{4,3,2,1,0:T(1,128)}, u32[]{:S(2)}) copy-start(s32[4,4,8,1,128]{4,3,2,1,0:T(1,128)} %get-tuple-element.14) | copy-start | bytes 196612
  27.0 116.7 %all-to-all-start = ((bf16[128,2,128,128]{3,2,1,0:T(8,128)(2,1)}), bf16[128,2,128,128]{3,2,1,0:T(8,128)(2,1)}, u32[]{:S(2)}, u32[]{:S(2)}) async-start(bf16[128,2,128,128]{3,2,1,0:T(8,128)(2,1)} %get-tuple-element.15), calls=%async_computation | async-start | bytes 16777216 | tf_op jit(solution)/shard_map/all_to_all | solution.py:836
  45.4 2.2 copy-start
  120.1 1.3 copy-start.1
  121.4 1.3 copy-start.2
  122.7 1.3 copy-start.3
  214.3 7.0 %copy-start.4 = (bf16[4,128,2,128]{3,2,1,0:T(2,128)(2,1)S(1)}, bf16[4,128,2,128]{3,2,1,0:T(2,128)(2,1)}, u32[]{:S(2)}) copy-start(bf16[4,128,2,128]{3,2,1,0:T(2,128)(2,1)} %get-tuple-element.21) | copy-start | bytes 786436
